TPU v7x, 32 devices: a whole 2x2x4 slice. The times are simulated.
32 devices in a mesh: dp: 2 (over y), gx: 4 (over x, core), gy: 4 (over z).
Axes of the slice: x: 2, y: 2, z: 4, core: 2. Of those that a mesh axis runs over, the one named last changes fastest.
Arguments:
- cell_values: float32 [2, 20, 32, 16, 512], P('dp', None, 'gx', 'gy'), may hold values from -6 to 6
- cotangent: float32 [2, 20, 32, 16, 512], P('dp', None, 'gx', 'gy'), may hold values from -6 to 6
- spectral_weight: float32 [2, 20, 20, 128, 256], P(None, None, None, ('gx', 'gy')), may hold values from -9 to 9
- channel_weight: float32 [20, 20], replicated, may hold values from -1.25 to 1.25
- channel_bias: float32 [20], replicated, may hold values from -4 to 4
Outputs:
- cell_grads: float32 [2, 20, 32, 16, 512], P('dp', None, 'gx', 'gy')
- spectral_grads: float32 [2, 20, 20, 128, 256], P(None, None, None, ('gx', 'gy'))
All inputs are finite; a program needn't handle non-finite values.
Results may differ from a plain program's by a relative error of at most 0.00016.
Values sent between devices are 32-bit elements; how exact they have to be, the bound alone decides.
No kernel may reach another device: no remote copies, remote signals or barrier semaphores. Data moves between devices by JAX's collectives and lax.ppermute only.
A program may use at most 192 MiB of HBM per device.

v0:
```python
import math

import jax
import jax.numpy as jnp
import numpy as np
from jax import lax
from jax.experimental import pallas as pl
from jax.experimental.pallas import tpu as pltpu
from jax.sharding import PartitionSpec as P

NZ = 32
NT = 16
KX = 16
KY = 16
KZ = 16
KT = 8


highest = lax.Precision.HIGHEST


def gelu_slope(values):
    return (
        0.5 * (1.0 + lax.erf(values * 0.7071067811865476))
        + values * jnp.exp(-0.5 * values * values) * 0.3989422804014327
    )


def signed_freq(number, kept_count):
    return jnp.where(number < kept_count // 2, number, number - kept_count)


def line_table(length, kept_count):
    positions = jnp.arange(length, dtype=jnp.int32)
    frequency = signed_freq(jnp.arange(kept_count, dtype=jnp.int32), kept_count)
    phases = positions[:, None] * frequency[None, :] % length
    angles = phases.astype(jnp.float32) * (-2.0 * math.pi / length)
    return jnp.stack([jnp.cos(angles), jnp.sin(angles)]) / math.sqrt(length)


def block_table(length, kept_count):
    table = line_table(length, kept_count)
    upper = jnp.stack([table[0], table[1]], axis=1)
    lower = jnp.stack([-table[1], table[0]], axis=1)
    return jnp.stack([upper, lower]).reshape(2 * length, 2 * kept_count)


def plane_table(mode_index):
    row_index = jnp.arange(NZ * NT, dtype=jnp.int32)
    depth = row_index // NT
    time_step = row_index % NT
    depth_freq = signed_freq(mode_index // KT, KZ)
    time_freq = signed_freq(mode_index % KT, KT)
    fraction = (depth[:, None] * depth_freq[None, :] % NZ).astype(jnp.float32) / NZ
    fraction = fraction + (time_step[:, None] * time_freq[None, :] % NT).astype(jnp.float32) / NT
    angles = fraction * (-2.0 * math.pi)
    table = jnp.stack([jnp.cos(angles), jnp.sin(angles)]) / math.sqrt(NZ * NT)
    return jnp.moveaxis(table, 0, -1).reshape(NZ * NT, -1)


def line_forward(data, block):
    return jnp.einsum("mpr,pk->mkr", data, block, precision=highest)


def line_adjoint(data, block):
    return jnp.einsum("mkr,pk->mpr", data, block, precision=highest)


def plane_front(real_field, planar, form):
    coeffs = jnp.einsum("cxyn,nk->" + form, real_field, planar, precision=highest)
    return coeffs.reshape(KZ * KT, 2, -1)


def plane_back(stacked, planar, form, first_cells, second_cells, channels):
    rows = stacked.reshape(-1, first_cells, second_cells, channels)
    return jnp.einsum(form + ",nk->cxyn", rows, planar, precision=highest)


def swap_inner(data, first, second, channels):
    leading = data.shape[0]
    moved = jnp.transpose(data.reshape(leading, 2, first, second, channels), (0, 1, 3, 2, 4))
    return moved.reshape(leading, 2, -1)


def mode_mix(weight, spectrum):

    def single(left_arg, right_arg):
        return jnp.einsum("imn,iomn->omn", left_arg, right_arg, precision=highest)

    real_part = single(spectrum[0], weight[0]) - single(spectrum[1], weight[1])
    imag_part = single(spectrum[1], weight[0]) + single(spectrum[0], weight[1])
    return jnp.stack([real_part, imag_part])


def mode_unmix(weight, spectrum):

    def single(left_arg, right_arg):
        return jnp.einsum("omn,iomn->imn", left_arg, right_arg, precision=highest)

    real_part = single(spectrum[0], weight[0]) + single(spectrum[1], weight[1])
    imag_part = single(spectrum[1], weight[0]) - single(spectrum[0], weight[1])
    return jnp.stack([real_part, imag_part])


def mode_outer(grad_spectrum, spectrum):

    def single(left_arg, right_arg):
        return jnp.einsum("omn,imn->iomn", left_arg, right_arg, precision=highest)

    real_part = single(grad_spectrum[0], spectrum[0]) + single(grad_spectrum[1], spectrum[1])
    imag_part = single(grad_spectrum[1], spectrum[0]) - single(grad_spectrum[0], spectrum[1])
    return jnp.stack([real_part, imag_part])


def on_device(cell_values, cotangent, spectral_weight, channel_weight, channel_bias):
    sample_cells = cell_values[0]
    upstream = cotangent[0]
    count_x = lax.axis_size("gx")
    count_y = lax.axis_size("gy")
    channels, cells_x, cells_y, depth_time = sample_cells.shape
    length_x = count_x * cells_x
    length_y = count_y * cells_y
    local_modes = KZ * KT // (count_x * count_y)
    block_x = block_table(length_x, KX)
    block_y = block_table(length_y, KY)
    column = jnp.arange(KZ * KT, dtype=jnp.int32)

    def to_spectrum(last):
        shaped = jnp.transpose(last.reshape(local_modes, 2, KX, KY, channels), (1, 4, 0, 3, 2))
        return shaped.reshape(2, channels, local_modes, KY * KX)

    def from_spectrum(spectrum):
        shaped = spectrum.reshape(2, channels, local_modes, KY, KX)
        return jnp.transpose(shaped, (2, 0, 4, 3, 1)).reshape(local_modes, 2 * KX, KY * channels)

    planar = plane_table(column)

    def forward(real_field):
        gathered = lax.all_to_all(
            plane_front(real_field, planar, "kyxc"),
            ("gx", "gy"),
            split_axis=0,
            concat_axis=2,
            tiled=True,
        )
        arranged = gathered.reshape(local_modes, 2, count_x, count_y, cells_y, cells_x * channels)
        arranged = jnp.transpose(arranged, (0, 1, 3, 4, 2, 5)).reshape(
            local_modes, 2 * length_y, length_x * channels
        )
        along_y = line_forward(arranged, block_y)
        along_y = swap_inner(along_y, KY, length_x, channels).reshape(
            local_modes, 2 * length_x, KY * channels
        )
        along_x = line_forward(along_y, block_x)
        return to_spectrum(along_x)

    def inverse(spectrum):
        back_x = line_adjoint(from_spectrum(spectrum), block_x)
        back_x = swap_inner(back_x, length_x, KY, channels).reshape(
            local_modes, 2 * KY, length_x * channels
        )
        back_y = line_adjoint(back_x, block_y)
        ordered = back_y.reshape(local_modes, 2, count_y, cells_y, count_x, cells_x * channels)
        ordered = jnp.transpose(ordered, (0, 1, 4, 2, 3, 5)).reshape(local_modes, 2, -1)
        spread = lax.all_to_all(ordered, ("gx", "gy"), split_axis=2, concat_axis=0, tiled=True)
        return plane_back(spread, planar, "kyxc", cells_y, cells_x, channels)

    spectra = forward(sample_cells)
    mixed = mode_mix(spectral_weight, spectra)
    pre_act = jnp.einsum("oi,ixyn->oxyn", channel_weight, sample_cells, precision=highest)
    pre_act = pre_act + channel_bias[:, None, None, None] + inverse(mixed)
    grad_pre = upstream * gelu_slope(pre_act)
    grad_spectra = forward(grad_pre)
    back_modes = mode_unmix(spectral_weight, grad_spectra)
    cell_grad = jnp.einsum("oi,oxyn->ixyn", channel_weight, grad_pre, precision=highest) + inverse(
        back_modes
    )
    spectral_grads = lax.psum(mode_outer(grad_spectra, spectra), "dp")
    return (cell_grad[None], spectral_grads)


LANES = 128
VMEM_LIMIT = 56 * 1024 * 1024


def params():
    return pltpu.CompilerParams(vmem_limit_bytes=VMEM_LIMIT)


def halves(values):
    upper = values.astype(jnp.bfloat16)
    return upper, (values - upper.astype(jnp.float32)).astype(jnp.bfloat16)


def host_halves(table):
    upper = table.astype(jnp.bfloat16)
    lower = (table - upper.astype(np.float64)).astype(jnp.bfloat16)
    return upper, lower


def host_freq(number, kept_count):
    return np.where(number < kept_count // 2, number, number - kept_count)


def host_plane(owners, local_modes):
    mode = np.arange(owners * local_modes)
    cell = np.arange(NZ * NT)
    turns = np.outer(host_freq(mode // KT, KZ), cell // NT) / NZ
    turns = turns + np.outer(host_freq(mode % KT, KT), cell % NT) / NT
    angles = 2.0 * np.pi * turns
    table = np.stack([np.cos(angles), -np.sin(angles)]) / np.sqrt(NZ * NT)
    table = table.reshape(2, owners, local_modes, NZ * NT)
    return np.swapaxes(table, 0, 1).reshape(owners * 2 * local_modes, NZ * NT)


def host_cross(count_x, count_y, cells_x, cells_y):
    length_x = count_x * cells_x
    length_y = count_y * cells_y
    row = np.arange(length_x * length_y)
    cell = row % (cells_x * cells_y)
    owner = row // (cells_x * cells_y)
    place_x = owner // count_y * cells_x + cell // cells_y
    place_y = owner % count_y * cells_y + cell % cells_y
    mode = np.arange(KY * KX)
    turns = np.outer(place_x, host_freq(mode % KX, KX)) / length_x
    turns = turns + np.outer(place_y, host_freq(mode // KX, KY)) / length_y
    angles = 2.0 * np.pi * turns
    return np.concatenate([np.cos(angles), np.sin(angles)], axis=1) / np.sqrt(length_x * length_y)


def product(left, right, left_dim, right_dim):
    dims = (((left_dim,), (right_dim,)), ((), ()))

    def single(one, other):
        return lax.dot_general(one, other, dims, preferred_element_type=jnp.float32)

    return single(left[0], right[0]) + (single(left[0], right[1]) + single(left[1], right[0]))


def swap_groups(parts):
    width = LANES // 4
    lane = lax.broadcasted_iota(jnp.int32, parts[0].shape, 1)
    low_half = lane < 2 * width
    low_quarter = lane % (2 * width) < width

    def trade(one, other, mask, shift):
        return (
            jnp.where(mask, one, pltpu.roll(other, shift, 1)),
            jnp.where(mask, pltpu.roll(one, LANES - shift, 1), other),
        )

    first, third = trade(parts[0], parts[2], low_half, 2 * width)
    second, fourth = trade(parts[1], parts[3], low_half, 2 * width)
    first, second = trade(first, second, low_quarter, width)
    third, fourth = trade(third, fourth, low_quarter, width)
    return first, second, third, fourth


def pack_rows(field_ref, rows_ref):
    channels, cells_x, cells_y, _ = field_ref.shape
    for channel in range(channels):
        for place in range(cells_x):
            row = (channel * cells_x + place) * cells_y
            rows_ref[row : row + cells_y, :] = field_ref[channel, place]


def front_kernel(field_ref, high_ref, low_ref, out_ref, rows_ref):
    pack_rows(field_ref, rows_ref)
    out_ref[...] = product((high_ref[...], low_ref[...]), halves(rows_ref[...]), 1, 1)


def mode_kernel(conjugate, got_ref, weight_ref, high_ref, low_ref, out_ref, spectra_ref, field_ref, mixed_ref):
    _, channels, local_modes, modes = spectra_ref.shape
    rows = channels * local_modes
    cells = high_ref.shape[0]
    owners = got_ref.shape[0] // (2 * local_modes)
    block = 2 * local_modes
    table = (high_ref[...], low_ref[...])
    for quad in range(owners // 4):
        for group in range(channels // 4):
            parts = [
                got_ref[(4 * quad + j) * block : (4 * quad + j + 1) * block, group * LANES : (group + 1) * LANES]
                for j in range(4)
            ]
            for m, part in enumerate(swap_groups(parts)):
                row = (4 * group + m) * local_modes
                for side in range(2):
                    field_ref[side * rows + row : side * rows + row + local_modes, quad * LANES : (quad + 1) * LANES] = part[
                        side * local_modes : (side + 1) * local_modes
                    ]
    waves = product(halves(field_ref[...]), table, 1, 0)
    real = waves[:rows, :modes] + waves[rows:, modes:]
    imag = waves[rows:, :modes] - waves[:rows, modes:]
    spectra_ref[0] = real.reshape(channels, local_modes, modes)
    spectra_ref[1] = imag.reshape(channels, local_modes, modes)
    for start in range(0, modes, LANES):
        span = slice(start, start + LANES)
        ins = [(spectra_ref[0, c, :, span], spectra_ref[1, c, :, span]) for c in range(channels)]

        def one(result, carry, span=span, ins=ins):
            total_real = jnp.zeros((local_modes, LANES), jnp.float32)
            total_imag = jnp.zeros((local_modes, LANES), jnp.float32)
            for c, (in_real, in_imag) in enumerate(ins):
                if conjugate:
                    w_real = weight_ref[0, result, c, :, span]
                    w_imag = weight_ref[1, result, c, :, span]
                    total_real = total_real + (in_real * w_real + in_imag * w_imag)
                    total_imag = total_imag + (in_imag * w_real - in_real * w_imag)
                else:
                    w_real = weight_ref[0, c, result, :, span]
                    w_imag = weight_ref[1, c, result, :, span]
                    total_real = total_real + (in_real * w_real - in_imag * w_imag)
                    total_imag = total_imag + (in_imag * w_real + in_real * w_imag)
            row = pl.multiple_of(result * local_modes, local_modes)
            other = pl.multiple_of(rows + result * local_modes, local_modes)
            mixed_ref[pl.ds(row, local_modes), start : start + LANES] = total_real
            mixed_ref[pl.ds(other, local_modes), start : start + LANES] = total_imag
            mixed_ref[pl.ds(row, local_modes), modes + start : modes + start + LANES] = -total_imag
            mixed_ref[pl.ds(other, local_modes), modes + start : modes + start + LANES] = total_real
            return carry

        lax.fori_loop(0, channels, one, 0)
    field_ref[...] = product(halves(mixed_ref[...]), table, 1, 1)
    for quad in range(owners // 4):
        for group in range(channels // 4):
            for side in range(2):
                first = side * rows + 4 * group * local_modes
                parts = [
                    field_ref[first + m * local_modes : first + (m + 1) * local_modes, quad * LANES : (quad + 1) * LANES]
                    for m in range(4)
                ]
                for j, part in enumerate(swap_groups(parts)):
                    row = (4 * quad + j) * block + side * local_modes
                    out_ref[row : row + local_modes, group * LANES : (group + 1) * LANES] = part


def channel_sums(transposed, rows_ref, weight_ref, bias_ref, out_ref, channels):
    height = rows_ref.shape[0] // channels
    for start in range(0, rows_ref.shape[1], LANES):
        span = slice(start, start + LANES)

        def one(step, carry, span=span):
            ins = [rows_ref[pl.ds(pl.multiple_of(i * height + step * 8, 8), 8), span] for i in range(channels)]
            for o in range(channels):
                total = None
                for i in range(channels):
                    factor = weight_ref[i, o] if transposed else weight_ref[o, i]
                    term = ins[i] * factor
                    total = term if total is None else total + term
                if bias_ref is not None:
                    total = total + bias_ref[o]
                out_ref[pl.ds(pl.multiple_of(o * height + step * 8, 8), 8), span] = total
            return carry

        lax.fori_loop(0, height // 8, one, 0)


def local_kernel(field_ref, upstream_ref, weight_ref, bias_ref, out_ref, packed_ref, rows_ref):
    pack_rows(field_ref, rows_ref)
    pack_rows(upstream_ref, packed_ref)
    channel_sums(False, rows_ref, weight_ref, bias_ref, out_ref, field_ref.shape[0])


def middle_kernel(got_ref, local_ref, upstream_ref, high_ref, low_ref, out_ref, grad_ref):
    table = (high_ref[...], low_ref[...])
    pre_act = product(halves(got_ref[...]), table, 0, 0) + local_ref[...]
    grad_ref[...] = upstream_ref[...] * gelu_slope(pre_act)
    out_ref[...] = product(table, halves(grad_ref[...]), 1, 1)


def grads_kernel(rows_ref, weight_ref, out_ref):
    channel_sums(True, rows_ref, weight_ref, None, out_ref, weight_ref.shape[0])


def last_kernel(got_ref, local_ref, high_ref, low_ref, out_ref, rows_ref):
    channels, cells_x, cells_y, _ = out_ref.shape
    rows_ref[...] = product(halves(got_ref[...]), (high_ref[...], low_ref[...]), 0, 0) + local_ref[...]
    for channel in range(channels):
        for place in range(cells_x):
            row = (channel * cells_x + place) * cells_y
            out_ref[channel, place] = rows_ref[row : row + cells_y, :]


def outer_kernel(spectra_ref, grads_ref, out_ref):
    _, _, channels, local_modes, modes = spectra_ref.shape
    source = pl.program_id(0)
    for start in range(0, modes, LANES):
        span = slice(start, start + LANES)
        ins = [(spectra_ref[s, 0, source, :, span], spectra_ref[s, 1, source, :, span]) for s in range(2)]
        for o in range(channels):
            total_real = None
            total_imag = None
            for s, (in_real, in_imag) in enumerate(ins):
                g_real = grads_ref[s, 0, o, :, span]
                g_imag = grads_ref[s, 1, o, :, span]
                real = g_real * in_real + g_imag * in_imag
                imag = g_imag * in_real - g_real * in_imag
                total_real = real if total_real is None else total_real + real
                total_imag = imag if total_imag is None else total_imag + imag
            out_ref[0, 0, o, :, span] = total_real
            out_ref[1, 0, o, :, span] = total_imag


def in_order(own):
    other = lax.ppermute(own, "dp", [(0, 1), (1, 0)])
    first = lax.axis_index("dp") == 0
    return jnp.stack([jnp.where(first, own, other), jnp.where(first, other, own)])


def on_tiles(cell_values, cotangent, spectral_weight, channel_weight, channel_bias):
    sample_cells = cell_values[0]
    upstream = cotangent[0]
    count_x = lax.axis_size("gx")
    count_y = lax.axis_size("gy")
    owners = count_x * count_y
    channels, cells_x, cells_y, depth_time = sample_cells.shape
    local_modes = spectral_weight.shape[3]
    modes = spectral_weight.shape[4]
    rows = channels * cells_x * cells_y
    plane = [jnp.asarray(t) for t in host_halves(host_plane(owners, local_modes))]
    cross = [jnp.asarray(t) for t in host_halves(host_cross(count_x, count_y, cells_x, cells_y))]
    f32 = jnp.float32
    whole = pl.BlockSpec(memory_space=pltpu.VMEM)
    scalars = pl.BlockSpec(memory_space=pltpu.SMEM)
    sent = jax.ShapeDtypeStruct((owners * 2 * local_modes, rows), f32)
    cells = jax.ShapeDtypeStruct((rows, depth_time), f32)
    spectrum = jax.ShapeDtypeStruct((2, channels, local_modes, modes), f32)

    def trade(values):
        return lax.all_to_all(values, ("gx", "gy"), split_axis=0, concat_axis=0, tiled=True)

    def across(values, conjugate):
        def body(*refs):
            mode_kernel(conjugate, *refs)

        return pl.pallas_call(
            body,
            out_shape=(sent, spectrum),
            in_specs=[whole] * 4,
            out_specs=(whole, whole),
            scratch_shapes=[
                pltpu.VMEM((2 * channels * local_modes, owners * cells_x * cells_y), f32),
                pltpu.VMEM((2 * channels * local_modes, 2 * modes), f32),
            ],
            compiler_params=params(),
            name="unmix_modes" if conjugate else "mix_modes",
        )(values, spectral_weight, *cross)

    front = pl.pallas_call(
        front_kernel,
        out_shape=sent,
        in_specs=[whole] * 3,
        out_specs=whole,
        scratch_shapes=[pltpu.VMEM((rows, depth_time), f32)],
        compiler_params=params(),
        name="front",
    )(sample_cells, *plane)
    got = trade(front)
    local, packed = pl.pallas_call(
        local_kernel,
        out_shape=(cells, cells),
        in_specs=[whole, whole, scalars, scalars],
        out_specs=(whole, whole),
        scratch_shapes=[pltpu.VMEM((rows, depth_time), f32)],
        compiler_params=params(),
        name="local_pre",
    )(sample_cells, upstream, channel_weight, channel_bias)
    mixed, spectra = across(got, False)
    both_spectra = in_order(spectra)
    got = trade(mixed)
    front, grad_pre = pl.pallas_call(
        middle_kernel,
        out_shape=(sent, cells),
        in_specs=[whole] * 5,
        out_specs=(whole, whole),
        compiler_params=params(),
        name="middle",
    )(got, local, packed, *plane)
    got = trade(front)
    back, grad_spectra = across(got, True)
    both_grads = in_order(grad_spectra)
    got = trade(back)
    local_grad = pl.pallas_call(
        grads_kernel,
        out_shape=cells,
        in_specs=[whole, scalars],
        out_specs=whole,
        compiler_params=params(),
        name="local_grad",
    )(grad_pre, channel_weight)
    full = pl.BlockSpec((2, 2, channels, local_modes, modes), lambda i: (0, 0, 0, 0, 0))
    spectral_grads = pl.pallas_call(
        outer_kernel,
        out_shape=jax.ShapeDtypeStruct(spectral_weight.shape, f32),
        grid=(channels,),
        in_specs=[full, full],
        out_specs=pl.BlockSpec((2, 1, channels, local_modes, modes), lambda i: (0, i, 0, 0, 0)),
        compiler_params=params(),
        name="outer",
    )(both_spectra, both_grads)
    cell_grad = pl.pallas_call(
        last_kernel,
        out_shape=jax.ShapeDtypeStruct(sample_cells.shape, f32),
        in_specs=[whole] * 4,
        out_specs=whole,
        scratch_shapes=[pltpu.VMEM((rows, depth_time), f32)],
        compiler_params=params(),
        name="last",
    )(got, local_grad, *plane)
    return (cell_grad[None], spectral_grads)


def solution(mesh):
    placed = (
        P("dp", None, "gx", "gy", None),
        P("dp", None, "gx", "gy", None),
        P(None, None, None, ("gx", "gy"), None),
        P(),
        P(),
    )

    def on_any(*args):
        _, channels, cells_x, cells_y, _ = args[0].shape
        owners = lax.axis_size("gx") * lax.axis_size("gy")
        fits = args[2].shape[3] == 8 and cells_x * cells_y == LANES // 4
        fits = fits and channels % 4 == 0 and owners % 4 == 0 and lax.axis_size("dp") == 2
        return on_tiles(*args) if fits else on_device(*args)

    return jax.shard_map(
        on_any,
        mesh=mesh,
        in_specs=placed,
        out_specs=(P("dp", None, "gx", "gy", None), P(None, None, None, ("gx", "gy"), None)),
        check_vma=False,
    )
```

profile of v0, /device:TPU:0, one launch (start us, length us, event | category | flops | bytes accessed | tf_op | source)
XLA Modules:
  0.0 133.2 jit_solution(4187578080994356398)
XLA Ops:
  0.6 3.1 %front.1 = f32[256,640]{1,0:T(8,128)} custom-call(f32[20,8,4,512]{3,2,1,0:T(4,128)} %bitcast.19, bf16[256,512]{1,0:T(8,128)(2,1)} %constant.16.clone.high_ref, bf16[256,512]{1,0:T(8,128)(2,1)} %constant.17.clone.low_ref), custom_call_target="tpu_custom_call" | custom-call | tf_op jit(solution)/shard_map/front/pallas_call | solution.py:449
  3.7 26.0 %all_to_all.44 = f32[16,16,640]{2,1,0:T(8,128)} all-to-all(f32[16,16,640]{2,1,0:T(8,128)} %bitcast.23), channel_id=1, replica_groups=mesh['dp'=2,'gx'=4,'gy'=4] {'gx','gy'}, dimensions={0} | all-to-all | bytes 1310720 | tf_op jit(solution)/shard_map/all_to_all | solution.py:430
  29.7 8.8 %mix_modes.1 = (f32[256,640]{1,0:T(8,128)}, f32[2,20,8,256]{3,2,1,0:T(8,128)}) custom-call(f32[256,640]{1,0:T(8,128)} %bitcast.22, f32[2,20,20,8,256]{4,3,2,1,0:T(8,128)} %refs_1_.3, bf16[512,512]{1,0:T(8,128)(2,1)} %constant.18.clone.refs_2_, bf16[512,512]{1,0:T(8,128)(2,1)} %constant.19.clone.refs_3_), custom_call_target="tpu_custom_call" | custom-call | tf_op jit(solution)/shard_map/mix_modes/pallas_call | solution.py:436
  38.5 3.6 %all-to-all-start.1 = ((f32[16,16,640]{2,1,0:T(8,128)}), f32[16,16,640]{2,1,0:T(8,128)S(1)}, u32[]{:S(2)}, u32[]{:S(2)}) async-start(f32[16,16,640]{2,1,0:T(8,128)} %bitcast.29), calls=%async_computation.1 | async-start | bytes 1310720 | tf_op jit(solution)/shard_map/all_to_all | solution.py:430
  42.1 6.7 %local_pre.1 = (f32[640,512]{1,0:T(8,128)}, f32[640,512]{1,0:T(8,128)}) custom-call(f32[20,8,4,512]{3,2,1,0:T(4,128)} %bitcast.20, f32[20,8,4,512]{3,2,1,0:T(4,128)} %bitcast.26, f32[20,20]{1,0:T(8,128)} %weight_ref.3, f32[20]{0:T(128)} %bias_ref.1), custom_call_target="tpu_custom_call" | custom-call | tf_op jit(solution)/shard_map/local_pre/pallas_call | solution.py:459
  48.9 11.7 %all-to-all-done.1 = f32[16,16,640]{2,1,0:T(8,128)S(1)} async-done(((f32[16,16,640]{2,1,0:T(8,128)}), f32[16,16,640]{2,1,0:T(8,128)S(1)}, u32[]{:S(2)}, u32[]{:S(2)}) %all-to-all-start.1) | async-done | bytes 655392 | tf_op jit(solution)/shard_map/all_to_all | solution.py:430
  60.6 0.9 copy-done.1
  61.5 4.7 %middle.1 = (f32[256,640]{1,0:T(8,128)}, f32[640,512]{1,0:T(8,128)}) custom-call(f32[256,640]{1,0:T(8,128)} %bitcast.25, f32[640,512]{1,0:T(8,128)} %get-tuple-element.11.local_ref, f32[640,512]{1,0:T(8,128)} %get-tuple-element.12.upstream_ref, bf16[256,512]{1,0:T(8,128)(2,1)} %constant.16.clone.high_ref, bf16[256,512]{1,0:T(8,128)(2,1)} %constant.17.clone.low_ref), custom_call_target="tpu_custom_call" | custom-call | tf_op jit(solution)/shard_map/middle/pallas_call | solution.py:471
  66.1 22.8 %all_to_all.45 = f32[16,16,640]{2,1,0:T(8,128)} all-to-all(f32[16,16,640]{2,1,0:T(8,128)} %bitcast.30), channel_id=1, replica_groups=mesh['dp'=2,'gx'=4,'gy'=4] {'gx','gy'}, dimensions={0} | all-to-all | bytes 1310720 | tf_op jit(solution)/shard_map/all_to_all | solution.py:430
  88.9 8.6 %unmix_modes.1 = (f32[256,640]{1,0:T(8,128)}, f32[2,20,8,256]{3,2,1,0:T(8,128)}) custom-call(f32[256,640]{1,0:T(8,128)} %bitcast.21, f32[2,20,20,8,256]{4,3,2,1,0:T(8,128)} %refs_1_.3, bf16[512,512]{1,0:T(8,128)(2,1)} %constant.18.clone.refs_2_, bf16[512,512]{1,0:T(8,128)(2,1)} %constant.19.clone.refs_3_), custom_call_target="tpu_custom_call" | custom-call | tf_op jit(solution)/shard_map/unmix_modes/pallas_call | solution.py:436
  97.5 3.7 %all-to-all-start.3 = ((f32[16,16,640]{2,1,0:T(8,128)}), f32[16,16,640]{2,1,0:T(8,128)S(1)}, u32[]{:S(2)}, u32[]{:S(2)}) async-start(f32[16,16,640]{2,1,0:T(8,128)} %bitcast.28), calls=%async_computation.3 | async-start | bytes 1310720 | tf_op jit(solution)/shard_map/all_to_all | solution.py:430
  101.2 0.0 copy-done.2
  101.2 1.6 %collective-permute-start = (f32[2,20,8,256]{3,2,1,0:T(8,128)S(1)}, f32[2,20,8,256]{3,2,1,0:T(8,128)S(1)}, u32[]{:S(2)}, u32[]{:S(2)}) collective-permute-start(f32[2,20,8,256]{3,2,1,0:T(8,128)S(1)} %copy-done.2), channel_id=1, source_target_pairs={{0,16},{16,0},{1,17},{17,1},{2,18},{18,2},{3,19},{19,3},{4,20},{20... | collective-permute-start | bytes 983048 | tf_op jit(solution)/shard_map/ppermute | solution.py:405
  102.8 0.5 collective-permute-start.1
  103.3 8.5 %collective-permute-done = f32[2,20,8,256]{3,2,1,0:T(8,128)S(1)} collective-permute-done((f32[2,20,8,256]{3,2,1,0:T(8,128)S(1)}, f32[2,20,8,256]{3,2,1,0:T(8,128)S(1)}, u32[]{:S(2)}, u32[]{:S(2)}) %collective-permute-start) | collective-permute-done | bytes 327712 | tf_op jit(solution)/shard_map/ppermute | solution.py:405
  111.8 0.1 select_bitcast_fusion.3
  111.9 5.4 %local_grad.1.local_ref = f32[640,512]{1,0:T(8,128)} custom-call(f32[640,512]{1,0:T(8,128)} %get-tuple-element.15.rows_ref, f32[20,20]{1,0:T(8,128)} %weight_ref.3), custom_call_target="tpu_custom_call" | custom-call | tf_op jit(solution)/shard_map/local_grad/pallas_call | solution.py:483
  117.3 0.9 collective-permute-done.1
  118.3 0.1 select_bitcast_fusion.1
  118.3 1.2 pad_maximum_fusion
  119.5 9.4 %outer.1 = f32[2,20,20,8,256]{4,3,2,1,0:T(8,128)} custom-call(f32[2,2,20,8,256]{4,3,2,1,0:T(8,128)} %get-tuple-element.22.spectra_ref, f32[2,2,20,8,256]{4,3,2,1,0:T(8,128)} %get-tuple-element.23.grads_ref), custom_call_target="tpu_custom_call" | custom-call | tf_op jit(solution)/shard_map/outer/pallas_call | solution.py:492
  128.9 0.0 all-to-all-done.3
  128.9 0.8 copy-done
  129.8 3.5 %last.1 = f32[20,8,4,512]{3,2,1,0:T(4,128)} custom-call(f32[256,640]{1,0:T(8,128)} %bitcast.24, f32[640,512]{1,0:T(8,128)} %local_grad.1.local_ref, bf16[256,512]{1,0:T(8,128)(2,1)} %constant.16.clone.high_ref, bf16[256,512]{1,0:T(8,128)(2,1)} %constant.17.clone.low_ref), custom_call_target="tpu_custom_call" | custom-call | tf_op jit(solution)/shard_map/last/pallas_call | solution.py:501
  (5 shorter events, 0.0 us)
Async XLA Ops:
  38.5 22.0 %all-to-all-start.1 = ((f32[16,16,640]{2,1,0:T(8,128)}), f32[16,16,640]{2,1,0:T(8,128)S(1)}, u32[]{:S(2)}, u32[]{:S(2)}) async-start(f32[16,16,640]{2,1,0:T(8,128)} %bitcast.29), calls=%async_computation.1 | async-start | bytes 1310720 | tf_op jit(solution)/shard_map/all_to_all | solution.py:430
  60.6 0.9 copy-start.1
  97.5 3.7 %copy-start.2 = (f32[2,20,8,256]{3,2,1,0:T(8,128)S(1)}, f32[2,20,8,256]{3,2,1,0:T(8,128)}, u32[]{:S(2)}) copy-start(f32[2,20,8,256]{3,2,1,0:T(8,128)} %get-tuple-element.16) | copy-start | bytes 983044
  97.5 5.3 %copy-start.3 = (f32[2,20,8,256]{3,2,1,0:T(8,128)S(1)}, f32[2,20,8,256]{3,2,1,0:T(8,128)}, u32[]{:S(2)}) copy-start(f32[2,20,8,256]{3,2,1,0:T(8,128)} %get-tuple-element.17) | copy-start | bytes 983044
  97.5 31.4 %all-to-all-start.3 = ((f32[16,16,640]{2,1,0:T(8,128)}), f32[16,16,640]{2,1,0:T(8,128)S(1)}, u32[]{:S(2)}, u32[]{:S(2)}) async-start(f32[16,16,640]{2,1,0:T(8,128)} %bitcast.28), calls=%async_computation.3 | async-start | bytes 1310720 | tf_op jit(solution)/shard_map/all_to_all | solution.py:430
  101.2 10.6 %collective-permute-start = (f32[2,20,8,256]{3,2,1,0:T(8,128)S(1)}, f32[2,20,8,256]{3,2,1,0:T(8,128)S(1)}, u32[]{:S(2)}, u32[]{:S(2)}) collective-permute-start(f32[2,20,8,256]{3,2,1,0:T(8,128)S(1)} %copy-done.2), channel_id=1, source_target_pairs={{0,16},{16,0},{1,17},{17,1},{2,18},{18,2},{3,19},{19,3},{4,20},{20... | collective-permute-start | bytes 983048 | tf_op jit(solution)/shard_map/ppermute | solution.py:405
  102.8 15.4 %collective-permute-start.1 = (f32[2,20,8,256]{3,2,1,0:T(8,128)S(1)}, f32[2,20,8,256]{3,2,1,0:T(8,128)S(1)}, u32[]{:S(2)}, u32[]{:S(2)}) collective-permute-start(f32[2,20,8,256]{3,2,1,0:T(8,128)S(1)} %copy-done.3), channel_id=1, source_target_pairs={{0,16},{16,0},{1,17},{17,1},{2,18},{18,2},{3,19},{19,3},{4,20},{20... | collective-permute-start | bytes 983048 | tf_op jit(solution)/shard_map/ppermute | solution.py:405
  128.9 0.8 copy-start
where the time goes:
time: 134 us; the launch traced here: 133 us
  Pallas kernels  50.2 us (37%)
  blocking collectives  48.8 us (36%)
  waiting for transfers between devices  21.1 us (16%)
  starting transfers between devices  9.41 us (7%)
  local copies, waits for them, and re-layouts  1.72 us (1%)
    all_to_all x2, blocking collectives, trade(): lax.all_to_all(values, ('gx', 'gy'), split_axis=0, concat_axis=0, tiled=T...  48.8 us
    pallas_call x2, Pallas kernels, across(): pl.pallas_call(body, out_shape=(sent, spectrum), in_specs=[whole] * 4, ou...  17.4 us
    all_to_all x2, waiting for transfers between devices, trade(): lax.all_to_all(values, ('gx', 'gy'), split_axis=0, concat_axis=0, tiled=T...  11.7 us
    ppermute x2, waiting for transfers between devices, in_order(): other = lax.ppermute(own, 'dp', [(0, 1), (1, 0)])  9.42 us
    pallas_call x1, Pallas kernels, on_tiles(): pl.pallas_call(outer_kernel, out_shape=jax.ShapeDtypeStruct(spectral_weig...  9.42 us
    all_to_all x2, starting transfers between devices, trade(): lax.all_to_all(values, ('gx', 'gy'), split_axis=0, concat_axis=0, tiled=T...  7.32 us
    pallas_call x1, Pallas kernels, on_tiles(): pl.pallas_call(local_kernel, out_shape=(cells, cells), in_specs=[whole, w...  6.72 us
    pallas_call x1, Pallas kernels, on_tiles(): pl.pallas_call(grads_kernel, out_shape=cells, in_specs=[whole, scalars],...  5.43 us
  transfers between devices with their start and end apart: 4, of which 3 were waited for; matrix products, arithmetic and copies ran while one was open for 1% of the time, Pallas kernels for 16%

commit v1 on v0

--- a/solution.py
+++ b/solution.py
@@ -180,7 +180,7 @@
 
 
 LANES = 128
-VMEM_LIMIT = 56 * 1024 * 1024
+VMEM_LIMIT = 24 * 1024 * 1024
 
 
 def params():
@@ -264,13 +264,57 @@
             rows_ref[row : row + cells_y, :] = field_ref[channel, place]
 
 
-def front_kernel(field_ref, high_ref, low_ref, out_ref, rows_ref):
-    pack_rows(field_ref, rows_ref)
-    out_ref[...] = product((high_ref[...], low_ref[...]), halves(rows_ref[...]), 1, 1)
-
-
-def mode_kernel(conjugate, got_ref, weight_ref, high_ref, low_ref, out_ref, spectra_ref, field_ref, mixed_ref):
+def start(source, target, semaphore):
+    copy = pltpu.make_async_copy(source, target, semaphore)
+    copy.start()
+    return copy
+
+
+def front_kernel(field_hbm, high_hbm, low_hbm, out_ref, field_ref, high_ref, low_ref, rows_ref, table_sems, field_sems):
+    channels, cells_x, cells_y, _ = field_ref.shape
+    tables = [start(high_hbm, high_ref, table_sems.at[0]), start(low_hbm, low_ref, table_sems.at[1])]
+    pieces = []
+    for first in range(0, channels, 8):
+        span = pl.ds(first, min(8, channels - first))
+        pieces.append((span, start(field_hbm.at[span], field_ref.at[span], field_sems.at[len(pieces)])))
+    for copy in tables:
+        copy.wait()
+    table = (high_ref[...], low_ref[...])
+    for span, copy in pieces:
+        copy.wait()
+        first = span.start * cells_x * cells_y
+        last = first + span.size * cells_x * cells_y
+        for channel in range(span.start, span.start + span.size):
+            for place in range(cells_x):
+                row = (channel * cells_x + place) * cells_y
+                rows_ref[row : row + cells_y, :] = field_ref[channel, place]
+        out_ref[:, first:last] = product(table, halves(rows_ref[first:last, :]), 1, 1)
+
+
+def mode_kernel(
+    conjugate,
+    got_ref,
+    weight_hbm,
+    high_ref,
+    low_ref,
+    out_hbm,
+    spectra_hbm,
+    weight_ref,
+    out_ref,
+    spectra_ref,
+    field_ref,
+    mixed_ref,
+    weight_sems,
+    spectra_sem,
+    out_sems,
+):
     _, channels, local_modes, modes = spectra_ref.shape
+    chunk = channels // weight_sems.shape[0]
+    weight_copies = []
+    for k in range(weight_sems.shape[0]):
+        span = pl.ds(k * chunk, chunk)
+        place = (slice(None), span) if conjugate else (slice(None), slice(None), span)
+        weight_copies.append(start(weight_hbm.at[place], weight_ref.at[place], weight_sems.at[k]))
     rows = channels * local_modes
     cells = high_ref.shape[0]
     owners = got_ref.shape[0] // (2 * local_modes)
@@ -293,11 +337,17 @@
     imag = waves[rows:, :modes] - waves[:rows, modes:]
     spectra_ref[0] = real.reshape(channels, local_modes, modes)
     spectra_ref[1] = imag.reshape(channels, local_modes, modes)
-    for start in range(0, modes, LANES):
-        span = slice(start, start + LANES)
+    spectra_copy = start(spectra_ref, spectra_hbm, spectra_sem)
+    for part in range(len(weight_copies) * modes // LANES):
+        first_lane = part % (modes // LANES) * LANES
+        first_result = part // (modes // LANES) * chunk
+        span = slice(first_lane, first_lane + LANES)
         ins = [(spectra_ref[0, c, :, span], spectra_ref[1, c, :, span]) for c in range(channels)]
-
-        def one(result, carry, span=span, ins=ins):
+        if first_lane == 0:
+            weight_copies[part // (modes // LANES)].wait()
+
+        def one(step, carry, span=span, ins=ins, first_lane=first_lane, first_result=first_result):
+            result = first_result + step
             total_real = jnp.zeros((local_modes, LANES), jnp.float32)
             total_imag = jnp.zeros((local_modes, LANES), jnp.float32)
             for c, (in_real, in_imag) in enumerate(ins):
@@ -313,14 +363,15 @@
                     total_imag = total_imag + (in_imag * w_real + in_real * w_imag)
             row = pl.multiple_of(result * local_modes, local_modes)
             other = pl.multiple_of(rows + result * local_modes, local_modes)
-            mixed_ref[pl.ds(row, local_modes), start : start + LANES] = total_real
-            mixed_ref[pl.ds(other, local_modes), start : start + LANES] = total_imag
-            mixed_ref[pl.ds(row, local_modes), modes + start : modes + start + LANES] = -total_imag
-            mixed_ref[pl.ds(other, local_modes), modes + start : modes + start + LANES] = total_real
+            mixed_ref[pl.ds(row, local_modes), first_lane : first_lane + LANES] = total_real
+            mixed_ref[pl.ds(other, local_modes), first_lane : first_lane + LANES] = total_imag
+            mixed_ref[pl.ds(row, local_modes), modes + first_lane : modes + first_lane + LANES] = -total_imag
+            mixed_ref[pl.ds(other, local_modes), modes + first_lane : modes + first_lane + LANES] = total_real
             return carry
 
-        lax.fori_loop(0, channels, one, 0)
+        lax.fori_loop(0, chunk, one, 0)
     field_ref[...] = product(halves(mixed_ref[...]), table, 1, 1)
+    out_copies = []
     for quad in range(owners // 4):
         for group in range(channels // 4):
             for side in range(2):
@@ -332,12 +383,17 @@
                 for j, part in enumerate(swap_groups(parts)):
                     row = (4 * quad + j) * block + side * local_modes
                     out_ref[row : row + local_modes, group * LANES : (group + 1) * LANES] = part
+        span = pl.ds(4 * quad * block, 4 * block)
+        out_copies.append(start(out_ref.at[span], out_hbm.at[span], out_sems.at[quad]))
+    spectra_copy.wait()
+    for copy in out_copies:
+        copy.wait()
 
 
 def channel_sums(transposed, rows_ref, weight_ref, bias_ref, out_ref, channels):
     height = rows_ref.shape[0] // channels
-    for start in range(0, rows_ref.shape[1], LANES):
-        span = slice(start, start + LANES)
+    for lane in range(0, rows_ref.shape[1], LANES):
+        span = slice(lane, lane + LANES)
 
         def one(step, carry, span=span):
             ins = [rows_ref[pl.ds(pl.multiple_of(i * height + step * 8, 8), 8), span] for i in range(channels)]
@@ -361,50 +417,83 @@
     channel_sums(False, rows_ref, weight_ref, bias_ref, out_ref, field_ref.shape[0])
 
 
-def middle_kernel(got_ref, local_ref, upstream_ref, high_ref, low_ref, out_ref, grad_ref):
+def middle_kernel(got_ref, local_hbm, upstream_hbm, high_ref, low_ref, out_ref, grad_hbm, local_ref, upstream_ref, grad_ref, sems):
+    copies = [start(local_hbm, local_ref, sems.at[0]), start(upstream_hbm, upstream_ref, sems.at[1])]
     table = (high_ref[...], low_ref[...])
-    pre_act = product(halves(got_ref[...]), table, 0, 0) + local_ref[...]
-    grad_ref[...] = upstream_ref[...] * gelu_slope(pre_act)
+    grad_ref[...] = product(halves(got_ref[...]), table, 0, 0)
+    for copy in copies:
+        copy.wait()
+    grad_ref[...] = upstream_ref[...] * gelu_slope(grad_ref[...] + local_ref[...])
+    copy = start(grad_ref, grad_hbm, sems.at[2])
     out_ref[...] = product(table, halves(grad_ref[...]), 1, 1)
+    copy.wait()
 
 
 def grads_kernel(rows_ref, weight_ref, out_ref):
     channel_sums(True, rows_ref, weight_ref, None, out_ref, weight_ref.shape[0])
 
 
-def last_kernel(got_ref, local_ref, high_ref, low_ref, out_ref, rows_ref):
+def last_kernel(got_ref, local_hbm, high_ref, low_ref, out_hbm, local_ref, out_ref, local_sem, out_sems):
     channels, cells_x, cells_y, _ = out_ref.shape
-    rows_ref[...] = product(halves(got_ref[...]), (high_ref[...], low_ref[...]), 0, 0) + local_ref[...]
-    for channel in range(channels):
-        for place in range(cells_x):
-            row = (channel * cells_x + place) * cells_y
-            out_ref[channel, place] = rows_ref[row : row + cells_y, :]
-
-
-def outer_kernel(spectra_ref, grads_ref, out_ref):
-    _, _, channels, local_modes, modes = spectra_ref.shape
-    source = pl.program_id(0)
-    for start in range(0, modes, LANES):
-        span = slice(start, start + LANES)
-        ins = [(spectra_ref[s, 0, source, :, span], spectra_ref[s, 1, source, :, span]) for s in range(2)]
-        for o in range(channels):
-            total_real = None
-            total_imag = None
-            for s, (in_real, in_imag) in enumerate(ins):
-                g_real = grads_ref[s, 0, o, :, span]
-                g_imag = grads_ref[s, 1, o, :, span]
-                real = g_real * in_real + g_imag * in_imag
-                imag = g_imag * in_real - g_real * in_imag
-                total_real = real if total_real is None else total_real + real
-                total_imag = imag if total_imag is None else total_imag + imag
-            out_ref[0, 0, o, :, span] = total_real
-            out_ref[1, 0, o, :, span] = total_imag
+    local_copy = start(local_hbm, local_ref, local_sem)
+    table = (high_ref[...], low_ref[...])
+    copies = []
+    for first in range(0, channels, 4):
+        begin = first * cells_x * cells_y
+        end = (first + 4) * cells_x * cells_y
+        values = product(halves(got_ref[:, begin:end]), table, 0, 0)
+        if first == 0:
+            local_copy.wait()
+        local_ref[begin:end, :] = local_ref[begin:end, :] + values
+        for channel in range(first, first + 4):
+            for place in range(cells_x):
+                row = (channel * cells_x + place) * cells_y
+                out_ref[channel, place] = local_ref[row : row + cells_y, :]
+        span = pl.ds(first, 4)
+        copies.append(start(out_ref.at[span], out_hbm.at[span], out_sems.at[len(copies)]))
+    for copy in copies:
+        copy.wait()
+
+
+def outer_kernel(first_spectra, second_spectra, first_grads, second_grads, out_ref):
+    _, channels, local_modes, modes = first_spectra.shape
+    sources = out_ref.shape[1]
+    pairs = ((first_spectra, first_grads), (second_spectra, second_grads))
+
+    def one(step, carry):
+        source = pl.program_id(0) * sources + step
+        for lane in range(0, modes, LANES):
+            span = slice(lane, lane + LANES)
+            ins = [(spectra[0, source, :, span], spectra[1, source, :, span]) for spectra, _ in pairs]
+            for o in range(channels):
+                total_real = None
+                total_imag = None
+                for (_, grads), (in_real, in_imag) in zip(pairs, ins):
+                    g_real = grads[0, o, :, span]
+                    g_imag = grads[1, o, :, span]
+                    real = g_real * in_real + g_imag * in_imag
+                    imag = g_imag * in_real - g_real * in_imag
+                    total_real = real if total_real is None else total_real + real
+                    total_imag = imag if total_imag is None else total_imag + imag
+                out_ref[0, step, o, :, span] = total_real
+                out_ref[1, step, o, :, span] = total_imag
+        return carry
+
+    lax.fori_loop(0, sources, one, 0)
 
 
 def in_order(own):
     other = lax.ppermute(own, "dp", [(0, 1), (1, 0)])
     first = lax.axis_index("dp") == 0
-    return jnp.stack([jnp.where(first, own, other), jnp.where(first, other, own)])
+    return jnp.where(first, own, other), jnp.where(first, other, own)
+
+
+def far(*values):
+    return [pltpu.with_memory_space_constraint(v, pltpu.HBM) for v in values]
+
+
+def near(*values):
+    return [pltpu.with_memory_space_constraint(v, pltpu.VMEM) for v in values]
 
 
 def on_tiles(cell_values, cotangent, spectral_weight, channel_weight, channel_bias):
@@ -420,11 +509,19 @@
     plane = [jnp.asarray(t) for t in host_halves(host_plane(owners, local_modes))]
     cross = [jnp.asarray(t) for t in host_halves(host_cross(count_x, count_y, cells_x, cells_y))]
     f32 = jnp.float32
+    bf16 = jnp.bfloat16
     whole = pl.BlockSpec(memory_space=pltpu.VMEM)
     scalars = pl.BlockSpec(memory_space=pltpu.SMEM)
-    sent = jax.ShapeDtypeStruct((owners * 2 * local_modes, rows), f32)
-    cells = jax.ShapeDtypeStruct((rows, depth_time), f32)
-    spectrum = jax.ShapeDtypeStruct((2, channels, local_modes, modes), f32)
+    stays = pl.BlockSpec(memory_space=pltpu.HBM)
+    copies = pltpu.SemaphoreType.DMA
+    vmem = pltpu.VMEM
+    sent = (owners * 2 * local_modes, rows)
+    cells = (rows, depth_time)
+    spectrum = (2, channels, local_modes, modes)
+    group = next(g for g in (4, 2, 1) if channels % g == 0)
+
+    def held(shape):
+        return pltpu.HBM(shape, f32)
 
     def trade(values):
         return lax.all_to_all(values, ("gx", "gy"), split_axis=0, concat_axis=0, tiled=True)
@@ -435,78 +532,91 @@
 
         return pl.pallas_call(
             body,
-            out_shape=(sent, spectrum),
-            in_specs=[whole] * 4,
-            out_specs=(whole, whole),
+            out_shape=(held(sent), held(spectrum)),
+            in_specs=[whole, stays, whole, whole],
+            out_specs=(stays, stays),
             scratch_shapes=[
-                pltpu.VMEM((2 * channels * local_modes, owners * cells_x * cells_y), f32),
-                pltpu.VMEM((2 * channels * local_modes, 2 * modes), f32),
+                vmem(spectral_weight.shape, f32),
+                vmem(sent, f32),
+                vmem(spectrum, f32),
+                vmem((2 * channels * local_modes, owners * cells_x * cells_y), f32),
+                vmem((2 * channels * local_modes, 2 * modes), f32),
+                copies((4,)),
+                copies,
+                copies((owners // 4,)),
             ],
             compiler_params=params(),
             name="unmix_modes" if conjugate else "mix_modes",
-        )(values, spectral_weight, *cross)
+        )(*near(values), *far(spectral_weight), *near(*cross))
 
     front = pl.pallas_call(
         front_kernel,
-        out_shape=sent,
-        in_specs=[whole] * 3,
+        out_shape=vmem(sent, f32),
+        in_specs=[stays] * 3,
         out_specs=whole,
-        scratch_shapes=[pltpu.VMEM((rows, depth_time), f32)],
+        scratch_shapes=[
+            vmem(sample_cells.shape, f32),
+            vmem(plane[0].shape, bf16),
+            vmem(plane[1].shape, bf16),
+            vmem(cells, f32),
+            copies((2,)),
+            copies((-(-channels // 8),)),
+        ],
         compiler_params=params(),
         name="front",
-    )(sample_cells, *plane)
+    )(*far(sample_cells, *plane))
     got = trade(front)
     local, packed = pl.pallas_call(
         local_kernel,
-        out_shape=(cells, cells),
+        out_shape=(held(cells), held(cells)),
         in_specs=[whole, whole, scalars, scalars],
         out_specs=(whole, whole),
-        scratch_shapes=[pltpu.VMEM((rows, depth_time), f32)],
+        scratch_shapes=[vmem(cells, f32)],
         compiler_params=params(),
         name="local_pre",
-    )(sample_cells, upstream, channel_weight, channel_bias)
+    )(*far(sample_cells, upstream), channel_weight, channel_bias)
     mixed, spectra = across(got, False)
     both_spectra = in_order(spectra)
-    got = trade(mixed)
+    got, both_spectra = lax.optimization_barrier((trade(mixed), both_spectra))
     front, grad_pre = pl.pallas_call(
         middle_kernel,
-        out_shape=(sent, cells),
-        in_specs=[whole] * 5,
-        out_specs=(whole, whole),
+        out_shape=(vmem(sent, f32), held(cells)),
+        in_specs=[whole, stays, stays, whole, whole],
+        out_specs=(whole, stays),
+        scratch_shapes=[vmem(cells, f32), vmem(cells, f32), vmem(cells, f32), copies((3,))],
         compiler_params=params(),
         name="middle",
-    )(got, local, packed, *plane)
+    )(*near(got), *far(local, packed), *near(*plane))
     got = trade(front)
     back, grad_spectra = across(got, True)
     both_grads = in_order(grad_spectra)
     got = trade(back)
     local_grad = pl.pallas_call(
         grads_kernel,
-        out_shape=cells,
+        out_shape=held(cells),
         in_specs=[whole, scalars],
         out_specs=whole,
         compiler_params=params(),
         name="local_grad",
-    )(grad_pre, channel_weight)
-    full = pl.BlockSpec((2, 2, channels, local_modes, modes), lambda i: (0, 0, 0, 0, 0))
+    )(*far(grad_pre), channel_weight)
     spectral_grads = pl.pallas_call(
         outer_kernel,
-        out_shape=jax.ShapeDtypeStruct(spectral_weight.shape, f32),
-        grid=(channels,),
-        in_specs=[full, full],
-        out_specs=pl.BlockSpec((2, 1, channels, local_modes, modes), lambda i: (0, i, 0, 0, 0)),
+        out_shape=held(spectral_weight.shape),
+        grid=(channels // group,),
+        in_specs=[whole] * 4,
+        out_specs=pl.BlockSpec((2, group, channels, local_modes, modes), lambda i: (0, i, 0, 0, 0)),
         compiler_params=params(),
         name="outer",
-    )(both_spectra, both_grads)
+    )(*far(*both_spectra), *near(*both_grads))
     cell_grad = pl.pallas_call(
         last_kernel,
-        out_shape=jax.ShapeDtypeStruct(sample_cells.shape, f32),
-        in_specs=[whole] * 4,
-        out_specs=whole,
-        scratch_shapes=[pltpu.VMEM((rows, depth_time), f32)],
+        out_shape=held(sample_cells.shape),
+        in_specs=[whole, stays, whole, whole],
+        out_specs=stays,
+        scratch_shapes=[vmem(cells, f32), vmem(sample_cells.shape, f32), copies, copies((channels // 4,))],
         compiler_params=params(),
         name="last",
-    )(got, local_grad, *plane)
+    )(*near(got), *far(local_grad), *near(*plane))
     return (cell_grad[None], spectral_grads)
 
 

time: 134 us -> 117 us (0.87)
  Pallas kernels: 50.2 us -> 40.9 us
  waiting for transfers between devices: 21.1 us -> 15.3 us
  local copies, waits for them, and re-layouts: 1.72 us -> 0.05 us
  blocking collectives: 48.8 us -> 47.4 us
    pallas_call x8, Pallas kernels: 50.2 us -> 40.9 us  [the longest x2 13.6 us: across(): pl.pallas_call(body, out_shape=(held(sent), held(spectrum)), in_specs=[wh...]
    ppermute x2, waiting for transfers between devices: 9.42 us -> 4.63 us  [in_order(): other = lax.ppermute(own, 'dp', [(0, 1), (1, 0)])]
    unnamed x8 -> x16, local copies, waits for them, and re-layouts: 1.72 us -> 0.05 us
    all_to_all x2, blocking collectives: 48.8 us -> 47.4 us  [trade(): lax.all_to_all(values, ('gx', 'gy'), split_axis=0, concat_axis=0, tiled=T...]
  transfers between devices with their start and end apart: 4 -> 4, of which waited for: 3 -> 4; matrix products, arithmetic and copies ran while one was open for 1% -> 1% of each run, Pallas kernels for 16% -> 15%
where the time goes in v1:
time: 117 us; the launch traced here: 116 us
  blocking collectives  47.4 us (41%)
  Pallas kernels  40.9 us (35%)
  waiting for transfers between devices  15.3 us (13%)
  starting transfers between devices  10.7 us (9%)
    all_to_all x2, blocking collectives, trade(): lax.all_to_all(values, ('gx', 'gy'), split_axis=0, concat_axis=0, tiled=T...  47.4 us
    pallas_call x2, Pallas kernels, across(): pl.pallas_call(body, out_shape=(held(sent), held(spectrum)), in_specs=[wh...  13.6 us
    all_to_all x2, waiting for transfers between devices, trade(): lax.all_to_all(values, ('gx', 'gy'), split_axis=0, concat_axis=0, tiled=T...  10.7 us
    all_to_all x2, starting transfers between devices, trade(): lax.all_to_all(values, ('gx', 'gy'), split_axis=0, concat_axis=0, tiled=T...  7.47 us
    pallas_call x1, Pallas kernels, on_tiles(): pl.pallas_call(local_kernel, out_shape=(held(cells), held(cells)), in_spe...  6.72 us
    pallas_call x1, Pallas kernels, on_tiles(): pl.pallas_call(grads_kernel, out_shape=held(cells), in_specs=[whole, scal...  5.44 us
    pallas_call x1, Pallas kernels, on_tiles(): pl.pallas_call(outer_kernel, out_shape=held(spectral_weight.shape), grid=...  5.23 us
    ppermute x2, waiting for transfers between devices, in_order(): other = lax.ppermute(own, 'dp', [(0, 1), (1, 0)])  4.63 us
  transfers between devices with their start and end apart: 4, of which 4 were waited for; matrix products, arithmetic and copies ran while one was open for 1% of the time, Pallas kernels for 15%

profile of v1, /device:TPU:0, one launch (start us, length us, event | category | flops | bytes accessed | tf_op | source)
XLA Modules:
  0.0 116.1 jit_solution(18031876034870849279)
XLA Ops:
  0.6 0.0 copy-start.2
  0.6 0.0 copy-start.3
  0.7 3.1 %front.1 = f32[256,640]{1,0:T(8,128)S(1)} custom-call(f32[20,8,4,512]{3,2,1,0:T(4,128)} %bitcast.17, bf16[256,512]{1,0:T(8,128)(2,1)} %constant.16.clone.high_hbm.high_ref, bf16[256,512]{1,0:T(8,128)(2,1)} %constant.17.clone.low_hbm.low_ref), custom_call_target="tpu_custom_call" | custom-call | tf_op jit(solution)/shard_map/front/pallas_call | solution.py:552
  3.8 25.7 %all_to_all.45 = f32[16,16,640]{2,1,0:T(8,128)S(1)} all-to-all(f32[16,16,640]{2,1,0:T(8,128)S(1)} %bitcast.13), channel_id=1, replica_groups=mesh['dp'=2,'gx'=4,'gy'=4] {'gx','gy'}, dimensions={0} | all-to-all | bytes 1310720 | tf_op jit(solution)/shard_map/all_to_all | solution.py:527
  29.5 6.8 %mix_modes.1 = (f32[256,640]{1,0:T(8,128)}, f32[2,20,8,256]{3,2,1,0:T(8,128)}) custom-call(f32[256,640]{1,0:T(8,128)S(1)} %bitcast.12, f32[2,20,20,8,256]{4,3,2,1,0:T(8,128)} %refs_1_.3, bf16[512,512]{1,0:T(8,128)(2,1)S(1)} %copy-done.3, bf16[512,512]{1,0:T(8,128)(2,1)S(1)} %copy-done.2), custom_call_target="tpu_custom_call" | custom-call | tf_op jit(solution)/shard_map/mix_modes/pallas_call | solution.py:533
  36.4 0.0 copy-start.4
  36.4 0.0 copy-start.5
  36.4 3.7 %all-to-all-start.1 = ((f32[16,16,640]{2,1,0:T(8,128)}), f32[16,16,640]{2,1,0:T(8,128)S(1)}, u32[]{:S(2)}, u32[]{:S(2)}) async-start(f32[16,16,640]{2,1,0:T(8,128)} %bitcast.21), calls=%async_computation.1 | async-start | bytes 1310720 | tf_op jit(solution)/shard_map/all_to_all | solution.py:527
  40.1 1.6 %collective-permute-start = (f32[2,20,8,256]{3,2,1,0:T(8,128)S(1)}, f32[2,20,8,256]{3,2,1,0:T(8,128)S(1)}, u32[]{:S(2)}, u32[]{:S(2)}) collective-permute-start(f32[2,20,8,256]{3,2,1,0:T(8,128)S(1)} %copy-done.6), channel_id=1, source_target_pairs={{0,16},{16,0},{1,17},{17,1},{2,18},{18,2},{3,19},{19,3},{4,20},{20... | collective-permute-start | bytes 983048 | tf_op jit(solution)/shard_map/ppermute | solution.py:486
  41.7 6.7 %local_pre.1 = (f32[640,512]{1,0:T(8,128)}, f32[640,512]{1,0:T(8,128)}) custom-call(f32[20,8,4,512]{3,2,1,0:T(4,128)} %bitcast.18, f32[20,8,4,512]{3,2,1,0:T(4,128)} %bitcast.19, f32[20,20]{1,0:T(8,128)S(1)} %copy-done.4, f32[20]{0:T(128)S(1)} %copy-done.5), custom_call_target="tpu_custom_call" | custom-call | tf_op jit(solution)/shard_map/local_pre/pallas_call | solution.py:569
  48.5 1.7 %collective-permute-done = f32[2,20,8,256]{3,2,1,0:T(8,128)S(1)} collective-permute-done((f32[2,20,8,256]{3,2,1,0:T(8,128)S(1)}, f32[2,20,8,256]{3,2,1,0:T(8,128)S(1)}, u32[]{:S(2)}, u32[]{:S(2)}) %collective-permute-start) | collective-permute-done | bytes 327712 | tf_op jit(solution)/shard_map/ppermute | solution.py:486
  50.1 0.9 broadcast_select_fusion.2
  51.0 7.5 %all-to-all-done.1 = f32[16,16,640]{2,1,0:T(8,128)S(1)} async-done(((f32[16,16,640]{2,1,0:T(8,128)}), f32[16,16,640]{2,1,0:T(8,128)S(1)}, u32[]{:S(2)}, u32[]{:S(2)}) %all-to-all-start.1) | async-done | bytes 655392 | tf_op jit(solution)/shard_map/all_to_all | solution.py:527
  58.6 3.9 %middle.1 = (f32[256,640]{1,0:T(8,128)S(1)}, f32[640,512]{1,0:T(8,128)}) custom-call(f32[256,640]{1,0:T(8,128)S(1)} %bitcast.14, f32[640,512]{1,0:T(8,128)} %get-tuple-element.16.local_hbm, f32[640,512]{1,0:T(8,128)} %get-tuple-element.17.upstream_hbm, bf16[256,512]{1,0:T(8,128)(2,1)S(1)} %copy-done.1, bf16[256,512]{1,0:T(8,128)(2,1)S(1)} %copy-done), custom_call_target="tpu_custom_call" | custom-call | tf_op jit(solution)/shard_map/middle/pallas_call | solution.py:581
  62.5 21.7 %all_to_all.46 = f32[16,16,640]{2,1,0:T(8,128)S(1)} all-to-all(f32[16,16,640]{2,1,0:T(8,128)S(1)} %bitcast.16), channel_id=1, replica_groups=mesh['dp'=2,'gx'=4,'gy'=4] {'gx','gy'}, dimensions={0} | all-to-all | bytes 1310720 | tf_op jit(solution)/shard_map/all_to_all | solution.py:527
  84.2 6.8 %unmix_modes.1 = (f32[256,640]{1,0:T(8,128)}, f32[2,20,8,256]{3,2,1,0:T(8,128)}) custom-call(f32[256,640]{1,0:T(8,128)S(1)} %bitcast.11, f32[2,20,20,8,256]{4,3,2,1,0:T(8,128)} %refs_1_.3, bf16[512,512]{1,0:T(8,128)(2,1)S(1)} %copy-done.3, bf16[512,512]{1,0:T(8,128)(2,1)S(1)} %copy-done.2), custom_call_target="tpu_custom_call" | custom-call | tf_op jit(solution)/shard_map/unmix_modes/pallas_call | solution.py:533
  91.0 3.7 %all-to-all-start.3 = ((f32[16,16,640]{2,1,0:T(8,128)}), f32[16,16,640]{2,1,0:T(8,128)S(1)}, u32[]{:S(2)}, u32[]{:S(2)}) async-start(f32[16,16,640]{2,1,0:T(8,128)} %bitcast.22), calls=%async_computation.3 | async-start | bytes 1310720 | tf_op jit(solution)/shard_map/all_to_all | solution.py:527
  94.8 1.6 %collective-permute-start.1 = (f32[2,20,8,256]{3,2,1,0:T(8,128)S(1)}, f32[2,20,8,256]{3,2,1,0:T(8,128)S(1)}, u32[]{:S(2)}, u32[]{:S(2)}) collective-permute-start(f32[2,20,8,256]{3,2,1,0:T(8,128)S(1)} %copy-done.7), channel_id=1, source_target_pairs={{0,16},{16,0},{1,17},{17,1},{2,18},{18,2},{3,19},{19,3},{4,20},{20... | collective-permute-start | bytes 983048 | tf_op jit(solution)/shard_map/ppermute | solution.py:486
  96.3 5.4 %local_grad.1.local_hbm = f32[640,512]{1,0:T(8,128)} custom-call(f32[640,512]{1,0:T(8,128)} %get-tuple-element.20.rows_ref, f32[20,20]{1,0:T(8,128)S(1)} %copy-done.4), custom_call_target="tpu_custom_call" | custom-call | tf_op jit(solution)/shard_map/local_grad/pallas_call | solution.py:594
  101.8 3.0 %collective-permute-done.1 = f32[2,20,8,256]{3,2,1,0:T(8,128)S(1)} collective-permute-done((f32[2,20,8,256]{3,2,1,0:T(8,128)S(1)}, f32[2,20,8,256]{3,2,1,0:T(8,128)S(1)}, u32[]{:S(2)}, u32[]{:S(2)}) %collective-permute-start.1) | collective-permute-done | bytes 327712 | tf_op jit(solution)/shard_map/ppermute | solution.py:486
  104.7 0.1 broadcast_select_fusion
  104.8 5.2 %outer.1 = f32[2,20,20,8,256]{4,3,2,1,0:T(8,128)} custom-call(f32[2,20,8,256]{3,2,1,0:T(8,128)} %get-tuple-element.21.first_spectra, f32[2,20,8,256]{3,2,1,0:T(8,128)} %get-tuple-element.22.second_spectra, f32[2,20,8,256]{3,2,1,0:T(8,128)S(1)} %get-tuple-element.25.first_grads, f32[2,20,8,256]{3,2,1,0:T(8,128)S(1)} %get-tuple-element.24.second_grads), custom_call_target="tpu_custom_call" | custom-call | tf_op jit(solution)/shard_map/outer/pallas_call | solution.py:602
  110.0 3.2 %all-to-all-done.3 = f32[16,16,640]{2,1,0:T(8,128)S(1)} async-done(((f32[16,16,640]{2,1,0:T(8,128)}), f32[16,16,640]{2,1,0:T(8,128)S(1)}, u32[]{:S(2)}, u32[]{:S(2)}) %all-to-all-start.3) | async-done | bytes 655392 | tf_op jit(solution)/shard_map/all_to_all | solution.py:527
  113.2 2.9 %last.1 = f32[20,8,4,512]{3,2,1,0:T(4,128)} custom-call(f32[256,640]{1,0:T(8,128)S(1)} %bitcast.15, f32[640,512]{1,0:T(8,128)} %local_grad.1.local_hbm, bf16[256,512]{1,0:T(8,128)(2,1)S(1)} %copy-done.1, bf16[256,512]{1,0:T(8,128)(2,1)S(1)} %copy-done), custom_call_target="tpu_custom_call" | custom-call | tf_op jit(solution)/shard_map/last/pallas_call | solution.py:611
  (12 shorter events, 0.0 us)
Async XLA Ops:
  0.6 28.9 %copy-start.2 = (bf16[512,512]{1,0:T(8,128)(2,1)S(1)}, bf16[512,512]{1,0:T(8,128)(2,1)}, u32[]{:S(2)}) copy-start(bf16[512,512]{1,0:T(8,128)(2,1)} %constant.19.clone.refs_3_) | copy-start | bytes 1572868
  0.6 28.9 %copy-start.3 = (bf16[512,512]{1,0:T(8,128)(2,1)S(1)}, bf16[512,512]{1,0:T(8,128)(2,1)}, u32[]{:S(2)}) copy-start(bf16[512,512]{1,0:T(8,128)(2,1)} %constant.18.clone.refs_2_) | copy-start | bytes 1572868
  36.4 3.8 %copy-start.6 = (f32[2,20,8,256]{3,2,1,0:T(8,128)S(1)}, f32[2,20,8,256]{3,2,1,0:T(8,128)}, u32[]{:S(2)}) copy-start(f32[2,20,8,256]{3,2,1,0:T(8,128)} %get-tuple-element.14) | copy-start | bytes 983044
  36.4 5.4 %copy-start.4 = (f32[20,20]{1,0:T(8,128)S(1)}, f32[20,20]{1,0:T(8,128)}, u32[]{:S(2)}) copy-start(f32[20,20]{1,0:T(8,128)} %weight_ref.3) | copy-start | bytes 4804
  36.4 5.4 %copy-start.5 = (f32[20]{0:T(128)S(1)}, f32[20]{0:T(128)}, u32[]{:S(2)}) copy-start(f32[20]{0:T(128)} %bias_ref.1) | copy-start | bytes 244
  36.4 22.2 %all-to-all-start.1 = ((f32[16,16,640]{2,1,0:T(8,128)}), f32[16,16,640]{2,1,0:T(8,128)S(1)}, u32[]{:S(2)}, u32[]{:S(2)}) async-start(f32[16,16,640]{2,1,0:T(8,128)} %bitcast.21), calls=%async_computation.1 | async-start | bytes 1310720 | tf_op jit(solution)/shard_map/all_to_all | solution.py:527
  40.1 10.0 %collective-permute-start = (f32[2,20,8,256]{3,2,1,0:T(8,128)S(1)}, f32[2,20,8,256]{3,2,1,0:T(8,128)S(1)}, u32[]{:S(2)}, u32[]{:S(2)}) collective-permute-start(f32[2,20,8,256]{3,2,1,0:T(8,128)S(1)} %copy-done.6), channel_id=1, source_target_pairs={{0,16},{16,0},{1,17},{17,1},{2,18},{18,2},{3,19},{19,3},{4,20},{20... | collective-permute-start | bytes 983048 | tf_op jit(solution)/shard_map/ppermute | solution.py:486
  48.5 10.1 %copy-start = (bf16[256,512]{1,0:T(8,128)(2,1)S(1)}, bf16[256,512]{1,0:T(8,128)(2,1)}, u32[]{:S(2)}) copy-start(bf16[256,512]{1,0:T(8,128)(2,1)} %constant.17.clone.low_hbm.low_ref) | copy-start | bytes 786436
  48.5 10.1 %copy-start.1 = (bf16[256,512]{1,0:T(8,128)(2,1)S(1)}, bf16[256,512]{1,0:T(8,128)(2,1)}, u32[]{:S(2)}) copy-start(bf16[256,512]{1,0:T(8,128)(2,1)} %constant.16.clone.high_hbm.high_ref) | copy-start | bytes 786436
  91.0 3.8 %copy-start.7 = (f32[2,20,8,256]{3,2,1,0:T(8,128)S(1)}, f32[2,20,8,256]{3,2,1,0:T(8,128)}, u32[]{:S(2)}) copy-start(f32[2,20,8,256]{3,2,1,0:T(8,128)} %get-tuple-element.23) | copy-start | bytes 983044
  91.0 22.2 %all-to-all-start.3 = ((f32[16,16,640]{2,1,0:T(8,128)}), f32[16,16,640]{2,1,0:T(8,128)S(1)}, u32[]{:S(2)}, u32[]{:S(2)}) async-start(f32[16,16,640]{2,1,0:T(8,128)} %bitcast.22), calls=%async_computation.3 | async-start | bytes 1310720 | tf_op jit(solution)/shard_map/all_to_all | solution.py:527
  94.8 10.0 %collective-permute-start.1 = (f32[2,20,8,256]{3,2,1,0:T(8,128)S(1)}, f32[2,20,8,256]{3,2,1,0:T(8,128)S(1)}, u32[]{:S(2)}, u32[]{:S(2)}) collective-permute-start(f32[2,20,8,256]{3,2,1,0:T(8,128)S(1)} %copy-done.7), channel_id=1, source_target_pairs={{0,16},{16,0},{1,17},{17,1},{2,18},{18,2},{3,19},{19,3},{4,20},{20... | collective-permute-start | bytes 983048 | tf_op jit(solution)/shard_map/ppermute | solution.py:486

commit v2 on v1

--- a/solution.py
+++ b/solution.py
@@ -270,25 +270,28 @@
     return copy
 
 
+def spans_of(channels, step):
+    return [(first, min(first + step, channels)) for first in range(0, channels, step)]
+
+
 def front_kernel(field_hbm, high_hbm, low_hbm, out_ref, field_ref, high_ref, low_ref, rows_ref, table_sems, field_sems):
     channels, cells_x, cells_y, _ = field_ref.shape
-    tables = [start(high_hbm, high_ref, table_sems.at[0]), start(low_hbm, low_ref, table_sems.at[1])]
+    cells = cells_x * cells_y
     pieces = []
-    for first in range(0, channels, 8):
-        span = pl.ds(first, min(8, channels - first))
-        pieces.append((span, start(field_hbm.at[span], field_ref.at[span], field_sems.at[len(pieces)])))
+    for first, last in spans_of(channels, 4):
+        span = pl.ds(first, last - first)
+        pieces.append(start(field_hbm.at[span], field_ref.at[span], field_sems.at[len(pieces)]))
+        if first == 0:
+            tables = [start(high_hbm, high_ref, table_sems.at[0]), start(low_hbm, low_ref, table_sems.at[1])]
+    for piece, (first, last) in enumerate(spans_of(channels, 4)):
+        pieces[piece].wait()
+        for channel in range(first, last):
+            for place in range(cells_x):
+                row = channel * cells + place * cells_y
+                rows_ref[row : row + cells_y, :] = field_ref[channel, place]
     for copy in tables:
         copy.wait()
-    table = (high_ref[...], low_ref[...])
-    for span, copy in pieces:
-        copy.wait()
-        first = span.start * cells_x * cells_y
-        last = first + span.size * cells_x * cells_y
-        for channel in range(span.start, span.start + span.size):
-            for place in range(cells_x):
-                row = (channel * cells_x + place) * cells_y
-                rows_ref[row : row + cells_y, :] = field_ref[channel, place]
-        out_ref[:, first:last] = product(table, halves(rows_ref[first:last, :]), 1, 1)
+    out_ref[...] = product((high_ref[...], low_ref[...]), halves(rows_ref[...]), 1, 1)
 
 
 def mode_kernel(
@@ -369,10 +372,13 @@
             mixed_ref[pl.ds(other, local_modes), modes + first_lane : modes + first_lane + LANES] = total_real
             return carry
 
-        lax.fori_loop(0, chunk, one, 0)
-    field_ref[...] = product(halves(mixed_ref[...]), table, 1, 1)
+        lax.fori_loop(0, chunk, one, 0, unroll=True)
+    mixed = halves(mixed_ref[...])
     out_copies = []
     for quad in range(owners // 4):
+        if quad % 2 == 0:
+            span = slice(quad * LANES, min(quad + 2, owners // 4) * LANES)
+            field_ref[:, span] = product(mixed, (high_ref[span, :], low_ref[span, :]), 1, 1)
         for group in range(channels // 4):
             for side in range(2):
                 first = side * rows + 4 * group * local_modes
@@ -417,41 +423,41 @@
     channel_sums(False, rows_ref, weight_ref, bias_ref, out_ref, field_ref.shape[0])
 
 
-def middle_kernel(got_ref, local_hbm, upstream_hbm, high_ref, low_ref, out_ref, grad_hbm, local_ref, upstream_ref, grad_ref, sems):
-    copies = [start(local_hbm, local_ref, sems.at[0]), start(upstream_hbm, upstream_ref, sems.at[1])]
+def middle_kernel(got_ref, local_hbm, upstream_hbm, high_ref, low_ref, out_ref, grad_ref, local_ref, upstream_ref, sems):
+    spans = [pl.ds(first, last - first) for first, last in spans_of(local_ref.shape[0], 128)]
+    copies = [
+        (start(local_hbm.at[span], local_ref.at[span], sems.at[0, k]), start(upstream_hbm.at[span], upstream_ref.at[span], sems.at[1, k]))
+        for k, span in enumerate(spans)
+    ]
     table = (high_ref[...], low_ref[...])
     grad_ref[...] = product(halves(got_ref[...]), table, 0, 0)
-    for copy in copies:
-        copy.wait()
-    grad_ref[...] = upstream_ref[...] * gelu_slope(grad_ref[...] + local_ref[...])
-    copy = start(grad_ref, grad_hbm, sems.at[2])
+    for k, span in enumerate(spans):
+        rows = slice(span.start, span.start + span.size)
+        for copy in copies[k]:
+            copy.wait()
+        grad_ref[rows, :] = upstream_ref[rows, :] * gelu_slope(grad_ref[rows, :] + local_ref[rows, :])
     out_ref[...] = product(table, halves(grad_ref[...]), 1, 1)
-    copy.wait()
 
 
 def grads_kernel(rows_ref, weight_ref, out_ref):
     channel_sums(True, rows_ref, weight_ref, None, out_ref, weight_ref.shape[0])
 
 
-def last_kernel(got_ref, local_hbm, high_ref, low_ref, out_hbm, local_ref, out_ref, local_sem, out_sems):
+def last_kernel(got_ref, local_ref, high_ref, low_ref, out_hbm, rows_ref, out_ref, sems):
     channels, cells_x, cells_y, _ = out_ref.shape
-    local_copy = start(local_hbm, local_ref, local_sem)
-    table = (high_ref[...], low_ref[...])
-    copies = []
-    for first in range(0, channels, 4):
-        begin = first * cells_x * cells_y
-        end = (first + 4) * cells_x * cells_y
-        values = product(halves(got_ref[:, begin:end]), table, 0, 0)
-        if first == 0:
-            local_copy.wait()
-        local_ref[begin:end, :] = local_ref[begin:end, :] + values
-        for channel in range(first, first + 4):
+    cells = cells_x * cells_y
+    rows_ref[...] = product(halves(got_ref[...]), (high_ref[...], low_ref[...]), 0, 0)
+    leaving = []
+    for first, last in spans_of(channels, 4):
+        rows = slice(first * cells, last * cells)
+        rows_ref[rows, :] = rows_ref[rows, :] + local_ref[rows, :]
+        for channel in range(first, last):
             for place in range(cells_x):
-                row = (channel * cells_x + place) * cells_y
-                out_ref[channel, place] = local_ref[row : row + cells_y, :]
-        span = pl.ds(first, 4)
-        copies.append(start(out_ref.at[span], out_hbm.at[span], out_sems.at[len(copies)]))
-    for copy in copies:
+                row = channel * cells + place * cells_y
+                out_ref[channel, place] = rows_ref[row : row + cells_y, :]
+        span = pl.ds(first, last - first)
+        leaving.append(start(out_ref.at[span], out_hbm.at[span], sems.at[len(leaving)]))
+    for copy in leaving:
         copy.wait()
 
 
@@ -560,7 +566,7 @@
             vmem(plane[1].shape, bf16),
             vmem(cells, f32),
             copies((2,)),
-            copies((-(-channels // 8),)),
+            copies((-(-channels // 4),)),
         ],
         compiler_params=params(),
         name="front",
@@ -580,10 +586,10 @@
     got, both_spectra = lax.optimization_barrier((trade(mixed), both_spectra))
     front, grad_pre = pl.pallas_call(
         middle_kernel,
-        out_shape=(vmem(sent, f32), held(cells)),
+        out_shape=(vmem(sent, f32), vmem(cells, f32)),
         in_specs=[whole, stays, stays, whole, whole],
-        out_specs=(whole, stays),
-        scratch_shapes=[vmem(cells, f32), vmem(cells, f32), vmem(cells, f32), copies((3,))],
+        out_specs=(whole, whole),
+        scratch_shapes=[vmem(cells, f32), vmem(cells, f32), copies((2, -(-rows // 128)))],
         compiler_params=params(),
         name="middle",
     )(*near(got), *far(local, packed), *near(*plane))
@@ -611,12 +617,12 @@
     cell_grad = pl.pallas_call(
         last_kernel,
         out_shape=held(sample_cells.shape),
-        in_specs=[whole, stays, whole, whole],
+        in_specs=[whole] * 4,
         out_specs=stays,
-        scratch_shapes=[vmem(cells, f32), vmem(sample_cells.shape, f32), copies, copies((channels // 4,))],
+        scratch_shapes=[vmem(cells, f32), vmem(sample_cells.shape, f32), copies((-(-channels // 4),))],
         compiler_params=params(),
         name="last",
-    )(*near(got), *far(local_grad), *near(*plane))
+    )(*near(got, local_grad, *plane))
     return (cell_grad[None], spectral_grads)
 
 

time: 117 us -> 111 us (0.949)
  Pallas kernels: 40.9 us -> 35.7 us
    pallas_call x2, Pallas kernels: 13.6 us -> 11 us  [across(): pl.pallas_call(body, out_shape=(held(sent), held(spectrum)), in_specs=[wh...]
    pallas_call x1, Pallas kernels: 2.88 us -> 1.69 us  [on_tiles(): pl.pallas_call(last_kernel, out_shape=held(sample_cells.shape), in_specs=...]
  transfers between devices with their start and end apart: 4 -> 4, of which waited for: 4 -> 4; matrix products, arithmetic and copies ran while one was open for 1% -> 1% of each run, Pallas kernels for 15% -> 16%
where the time goes in v2:
time: 111 us
  blocking collectives  47.4 us (43%)
  Pallas kernels  35.7 us (32%)
  waiting for transfers between devices  15.2 us (14%)
  starting transfers between devices  10.6 us (10%)
    all_to_all x2, blocking collectives, trade(): lax.all_to_all(values, ('gx', 'gy'), split_axis=0, concat_axis=0, tiled=T...  47.4 us
    pallas_call x2, Pallas kernels, across(): pl.pallas_call(body, out_shape=(held(sent), held(spectrum)), in_specs=[wh...  11 us
    all_to_all x2, waiting for transfers between devices, trade(): lax.all_to_all(values, ('gx', 'gy'), split_axis=0, concat_axis=0, tiled=T...  10.6 us
    all_to_all x2, starting transfers between devices, trade(): lax.all_to_all(values, ('gx', 'gy'), split_axis=0, concat_axis=0, tiled=T...  7.47 us
    pallas_call x1, Pallas kernels, on_tiles(): pl.pallas_call(local_kernel, out_shape=(held(cells), held(cells)), in_spe...  6.72 us
    pallas_call x1, Pallas kernels, on_tiles(): pl.pallas_call(grads_kernel, out_shape=held(cells), in_specs=[whole, scal...  5.43 us
    pallas_call x1, Pallas kernels, on_tiles(): pl.pallas_call(outer_kernel, out_shape=held(spectral_weight.shape), grid=...  5.32 us
    ppermute x2, waiting for transfers between devices, in_order(): other = lax.ppermute(own, 'dp', [(0, 1), (1, 0)])  4.65 us
  transfers between devices with their start and end apart: 4, of which 4 were waited for; matrix products, arithmetic and copies ran while one was open for 1% of the time, Pallas kernels for 16%

profile of v2, /device:TPU:0, one launch (start us, length us, event | category | flops | bytes accessed | tf_op | source)
XLA Modules:
  0.0 110.7 jit_solution(16618561338323445645)
XLA Ops:
  0.6 0.0 copy-start.3
  0.6 0.0 copy-start.4
  0.7 2.4 %front.1 = f32[256,640]{1,0:T(8,128)S(1)} custom-call(f32[20,8,4,512]{3,2,1,0:T(4,128)} %bitcast.17, bf16[256,512]{1,0:T(8,128)(2,1)} %constant.16.clone.high_hbm.high_ref, bf16[256,512]{1,0:T(8,128)(2,1)} %constant.17.clone.low_hbm.low_ref), custom_call_target="tpu_custom_call" | custom-call | tf_op jit(solution)/shard_map/front/pallas_call | solution.py:558
  3.1 25.7 %all_to_all.45 = f32[16,16,640]{2,1,0:T(8,128)S(1)} all-to-all(f32[16,16,640]{2,1,0:T(8,128)S(1)} %bitcast.13), channel_id=1, replica_groups=mesh['dp'=2,'gx'=4,'gy'=4] {'gx','gy'}, dimensions={0} | all-to-all | bytes 1310720 | tf_op jit(solution)/shard_map/all_to_all | solution.py:533
  28.8 5.5 %mix_modes.1 = (f32[256,640]{1,0:T(8,128)}, f32[2,20,8,256]{3,2,1,0:T(8,128)}) custom-call(f32[256,640]{1,0:T(8,128)S(1)} %bitcast.12, f32[2,20,20,8,256]{4,3,2,1,0:T(8,128)} %refs_1_.3, bf16[512,512]{1,0:T(8,128)(2,1)S(1)} %copy-done.4, bf16[512,512]{1,0:T(8,128)(2,1)S(1)} %copy-done.3), custom_call_target="tpu_custom_call" | custom-call | tf_op jit(solution)/shard_map/mix_modes/pallas_call | solution.py:539
  34.3 0.0 copy-start.8
  34.3 3.7 %all-to-all-start.1 = ((f32[16,16,640]{2,1,0:T(8,128)}), f32[16,16,640]{2,1,0:T(8,128)S(1)}, u32[]{:S(2)}, u32[]{:S(2)}) async-start(f32[16,16,640]{2,1,0:T(8,128)} %bitcast.21), calls=%async_computation.1 | async-start | bytes 1310720 | tf_op jit(solution)/shard_map/all_to_all | solution.py:533
  38.1 1.6 %collective-permute-start = (f32[2,20,8,256]{3,2,1,0:T(8,128)S(1)}, f32[2,20,8,256]{3,2,1,0:T(8,128)S(1)}, u32[]{:S(2)}, u32[]{:S(2)}) collective-permute-start(f32[2,20,8,256]{3,2,1,0:T(8,128)S(1)} %copy-done.8), channel_id=1, source_target_pairs={{0,16},{16,0},{1,17},{17,1},{2,18},{18,2},{3,19},{19,3},{4,20},{20... | collective-permute-start | bytes 983048 | tf_op jit(solution)/shard_map/ppermute | solution.py:492
  39.7 6.7 %local_pre.1 = (f32[640,512]{1,0:T(8,128)}, f32[640,512]{1,0:T(8,128)}) custom-call(f32[20,8,4,512]{3,2,1,0:T(4,128)} %bitcast.18, f32[20,8,4,512]{3,2,1,0:T(4,128)} %bitcast.19, f32[20,20]{1,0:T(8,128)S(1)} %copy-done.6, f32[20]{0:T(128)S(1)} %copy-done.7), custom_call_target="tpu_custom_call" | custom-call | tf_op jit(solution)/shard_map/local_pre/pallas_call | solution.py:575
  46.4 1.7 %collective-permute-done = f32[2,20,8,256]{3,2,1,0:T(8,128)S(1)} collective-permute-done((f32[2,20,8,256]{3,2,1,0:T(8,128)S(1)}, f32[2,20,8,256]{3,2,1,0:T(8,128)S(1)}, u32[]{:S(2)}, u32[]{:S(2)}) %collective-permute-start) | collective-permute-done | bytes 327712 | tf_op jit(solution)/shard_map/ppermute | solution.py:492
  48.1 0.9 broadcast_select_fusion.2
  49.0 7.5 %all-to-all-done.1 = f32[16,16,640]{2,1,0:T(8,128)S(1)} async-done(((f32[16,16,640]{2,1,0:T(8,128)}), f32[16,16,640]{2,1,0:T(8,128)S(1)}, u32[]{:S(2)}, u32[]{:S(2)}) %all-to-all-start.1) | async-done | bytes 655392 | tf_op jit(solution)/shard_map/all_to_all | solution.py:533
  56.5 3.1 %middle.1 = (f32[256,640]{1,0:T(8,128)S(1)}, f32[640,512]{1,0:T(8,128)S(1)}) custom-call(f32[256,640]{1,0:T(8,128)S(1)} %bitcast.14, f32[640,512]{1,0:T(8,128)} %get-tuple-element.16.local_hbm, f32[640,512]{1,0:T(8,128)} %get-tuple-element.17.upstream_hbm, bf16[256,512]{1,0:T(8,128)(2,1)S(1)} %copy-done.2, bf16[256,512]{1,0:T(8,128)(2,1)S(1)} %copy-done.1), custom_call_target="tpu_custom_call" | custom-call | tf_op jit(solution)/shard_map/middle/pallas_call | solution.py:587
  59.6 0.0 copy-start.5
  59.7 21.7 %all_to_all.46 = f32[16,16,640]{2,1,0:T(8,128)S(1)} all-to-all(f32[16,16,640]{2,1,0:T(8,128)S(1)} %bitcast.16), channel_id=1, replica_groups=mesh['dp'=2,'gx'=4,'gy'=4] {'gx','gy'}, dimensions={0} | all-to-all | bytes 1310720 | tf_op jit(solution)/shard_map/all_to_all | solution.py:533
  81.3 5.5 %unmix_modes.1 = (f32[256,640]{1,0:T(8,128)}, f32[2,20,8,256]{3,2,1,0:T(8,128)}) custom-call(f32[256,640]{1,0:T(8,128)S(1)} %bitcast.11, f32[2,20,20,8,256]{4,3,2,1,0:T(8,128)} %refs_1_.3, bf16[512,512]{1,0:T(8,128)(2,1)S(1)} %copy-done.4, bf16[512,512]{1,0:T(8,128)(2,1)S(1)} %copy-done.3), custom_call_target="tpu_custom_call" | custom-call | tf_op jit(solution)/shard_map/unmix_modes/pallas_call | solution.py:539
  86.9 3.7 %all-to-all-start.3 = ((f32[16,16,640]{2,1,0:T(8,128)}), f32[16,16,640]{2,1,0:T(8,128)S(1)}, u32[]{:S(2)}, u32[]{:S(2)}) async-start(f32[16,16,640]{2,1,0:T(8,128)} %bitcast.22), calls=%async_computation.3 | async-start | bytes 1310720 | tf_op jit(solution)/shard_map/all_to_all | solution.py:533
  90.6 1.6 %collective-permute-start.1 = (f32[2,20,8,256]{3,2,1,0:T(8,128)S(1)}, f32[2,20,8,256]{3,2,1,0:T(8,128)S(1)}, u32[]{:S(2)}, u32[]{:S(2)}) collective-permute-start(f32[2,20,8,256]{3,2,1,0:T(8,128)S(1)} %copy-done.9), channel_id=1, source_target_pairs={{0,16},{16,0},{1,17},{17,1},{2,18},{18,2},{3,19},{19,3},{4,20},{20... | collective-permute-start | bytes 983048 | tf_op jit(solution)/shard_map/ppermute | solution.py:492
  92.2 5.4 %local_grad.1.local_ref = f32[640,512]{1,0:T(8,128)} custom-call(f32[640,512]{1,0:T(8,128)} %copy-done.5, f32[20,20]{1,0:T(8,128)S(1)} %copy-done.6), custom_call_target="tpu_custom_call" | custom-call | tf_op jit(solution)/shard_map/local_grad/pallas_call | solution.py:600
  97.6 3.0 %collective-permute-done.1 = f32[2,20,8,256]{3,2,1,0:T(8,128)S(1)} collective-permute-done((f32[2,20,8,256]{3,2,1,0:T(8,128)S(1)}, f32[2,20,8,256]{3,2,1,0:T(8,128)S(1)}, u32[]{:S(2)}, u32[]{:S(2)}) %collective-permute-start.1) | collective-permute-done | bytes 327712 | tf_op jit(solution)/shard_map/ppermute | solution.py:492
  100.6 0.1 broadcast_select_fusion
  100.7 5.3 %outer.1 = f32[2,20,20,8,256]{4,3,2,1,0:T(8,128)} custom-call(f32[2,20,8,256]{3,2,1,0:T(8,128)} %get-tuple-element.21.first_spectra, f32[2,20,8,256]{3,2,1,0:T(8,128)} %get-tuple-element.22.second_spectra, f32[2,20,8,256]{3,2,1,0:T(8,128)S(1)} %get-tuple-element.25.first_grads, f32[2,20,8,256]{3,2,1,0:T(8,128)S(1)} %get-tuple-element.24.second_grads), custom_call_target="tpu_custom_call" | custom-call | tf_op jit(solution)/shard_map/outer/pallas_call | solution.py:608
  106.0 3.1 %all-to-all-done.3 = f32[16,16,640]{2,1,0:T(8,128)S(1)} async-done(((f32[16,16,640]{2,1,0:T(8,128)}), f32[16,16,640]{2,1,0:T(8,128)S(1)}, u32[]{:S(2)}, u32[]{:S(2)}) %all-to-all-start.3) | async-done | bytes 655392 | tf_op jit(solution)/shard_map/all_to_all | solution.py:533
  109.0 1.7 %last.1 = f32[20,8,4,512]{3,2,1,0:T(4,128)} custom-call(f32[256,640]{1,0:T(8,128)S(1)} %bitcast.15, f32[640,512]{1,0:T(8,128)S(1)} %copy-done, bf16[256,512]{1,0:T(8,128)(2,1)S(1)} %copy-done.2, bf16[256,512]{1,0:T(8,128)(2,1)S(1)} %copy-done.1), custom_call_target="tpu_custom_call" | custom-call | tf_op jit(solution)/shard_map/last/pallas_call | solution.py:617
  (16 shorter events, 0.0 us)
Async XLA Ops:
  0.6 28.1 %copy-start.3 = (bf16[512,512]{1,0:T(8,128)(2,1)S(1)}, bf16[512,512]{1,0:T(8,128)(2,1)}, u32[]{:S(2)}) copy-start(bf16[512,512]{1,0:T(8,128)(2,1)} %constant.19.clone.refs_3_) | copy-start | bytes 1572868
  0.6 28.1 %copy-start.4 = (bf16[512,512]{1,0:T(8,128)(2,1)S(1)}, bf16[512,512]{1,0:T(8,128)(2,1)}, u32[]{:S(2)}) copy-start(bf16[512,512]{1,0:T(8,128)(2,1)} %constant.18.clone.refs_2_) | copy-start | bytes 1572868
  34.3 3.8 %copy-start.8 = (f32[2,20,8,256]{3,2,1,0:T(8,128)S(1)}, f32[2,20,8,256]{3,2,1,0:T(8,128)}, u32[]{:S(2)}) copy-start(f32[2,20,8,256]{3,2,1,0:T(8,128)} %get-tuple-element.14) | copy-start | bytes 983044
  34.3 5.4 %copy-start.6 = (f32[20,20]{1,0:T(8,128)S(1)}, f32[20,20]{1,0:T(8,128)}, u32[]{:S(2)}) copy-start(f32[20,20]{1,0:T(8,128)} %weight_ref.3) | copy-start | bytes 4804
  34.3 5.4 %copy-start.7 = (f32[20]{0:T(128)S(1)}, f32[20]{0:T(128)}, u32[]{:S(2)}) copy-start(f32[20]{0:T(128)} %bias_ref.1) | copy-start | bytes 244
  34.3 22.2 %all-to-all-start.1 = ((f32[16,16,640]{2,1,0:T(8,128)}), f32[16,16,640]{2,1,0:T(8,128)S(1)}, u32[]{:S(2)}, u32[]{:S(2)}) async-start(f32[16,16,640]{2,1,0:T(8,128)} %bitcast.21), calls=%async_computation.1 | async-start | bytes 1310720 | tf_op jit(solution)/shard_map/all_to_all | solution.py:533
  38.1 10.0 %collective-permute-start = (f32[2,20,8,256]{3,2,1,0:T(8,128)S(1)}, f32[2,20,8,256]{3,2,1,0:T(8,128)S(1)}, u32[]{:S(2)}, u32[]{:S(2)}) collective-permute-start(f32[2,20,8,256]{3,2,1,0:T(8,128)S(1)} %copy-done.8), channel_id=1, source_target_pairs={{0,16},{16,0},{1,17},{17,1},{2,18},{18,2},{3,19},{19,3},{4,20},{20... | collective-permute-start | bytes 983048 | tf_op jit(solution)/shard_map/ppermute | solution.py:492
  46.4 10.1 %copy-start.1 = (bf16[256,512]{1,0:T(8,128)(2,1)S(1)}, bf16[256,512]{1,0:T(8,128)(2,1)}, u32[]{:S(2)}) copy-start(bf16[256,512]{1,0:T(8,128)(2,1)} %constant.17.clone.low_hbm.low_ref) | copy-start | bytes 786436
  46.4 10.1 %copy-start.2 = (bf16[256,512]{1,0:T(8,128)(2,1)S(1)}, bf16[256,512]{1,0:T(8,128)(2,1)}, u32[]{:S(2)}) copy-start(bf16[256,512]{1,0:T(8,128)(2,1)} %constant.16.clone.high_hbm.high_ref) | copy-start | bytes 786436
  59.6 27.2 %copy-start.5 = (f32[640,512]{1,0:T(8,128)}, f32[640,512]{1,0:T(8,128)S(1)}, u32[]{:S(2)}) copy-start(f32[640,512]{1,0:T(8,128)S(1)} %get-tuple-element.20.rows_ref) | copy-start | bytes 3932164
  86.8 3.8 %copy-start.9 = (f32[2,20,8,256]{3,2,1,0:T(8,128)S(1)}, f32[2,20,8,256]{3,2,1,0:T(8,128)}, u32[]{:S(2)}) copy-start(f32[2,20,8,256]{3,2,1,0:T(8,128)} %get-tuple-element.23) | copy-start | bytes 983044
  86.9 22.2 %all-to-all-start.3 = ((f32[16,16,640]{2,1,0:T(8,128)}), f32[16,16,640]{2,1,0:T(8,128)S(1)}, u32[]{:S(2)}, u32[]{:S(2)}) async-start(f32[16,16,640]{2,1,0:T(8,128)} %bitcast.22), calls=%async_computation.3 | async-start | bytes 1310720 | tf_op jit(solution)/shard_map/all_to_all | solution.py:533
  90.6 10.0 %collective-permute-start.1 = (f32[2,20,8,256]{3,2,1,0:T(8,128)S(1)}, f32[2,20,8,256]{3,2,1,0:T(8,128)S(1)}, u32[]{:S(2)}, u32[]{:S(2)}) collective-permute-start(f32[2,20,8,256]{3,2,1,0:T(8,128)S(1)} %copy-done.9), channel_id=1, source_target_pairs={{0,16},{16,0},{1,17},{17,1},{2,18},{18,2},{3,19},{19,3},{4,20},{20... | collective-permute-start | bytes 983048 | tf_op jit(solution)/shard_map/ppermute | solution.py:492
  100.7 8.4 %copy-start = (f32[640,512]{1,0:T(8,128)S(1)}, f32[640,512]{1,0:T(8,128)}, u32[]{:S(2)}) copy-start(f32[640,512]{1,0:T(8,128)} %local_grad.1.local_ref) | copy-start | bytes 3932164

commit v3 on v2

--- a/solution.py
+++ b/solution.py
@@ -216,16 +216,21 @@
 def host_cross(count_x, count_y, cells_x, cells_y):
     length_x = count_x * cells_x
     length_y = count_y * cells_y
-    row = np.arange(length_x * length_y)
+    row = np.arange(length_x * length_y // 2)
     cell = row % (cells_x * cells_y)
     owner = row // (cells_x * cells_y)
-    place_x = owner // count_y * cells_x + cell // cells_y
-    place_y = owner % count_y * cells_y + cell % cells_y
-    mode = np.arange(KY * KX)
-    turns = np.outer(place_x, host_freq(mode % KX, KX)) / length_x
-    turns = turns + np.outer(place_y, host_freq(mode // KX, KY)) / length_y
-    angles = 2.0 * np.pi * turns
-    return np.concatenate([np.cos(angles), np.sin(angles)], axis=1) / np.sqrt(length_x * length_y)
+    place_x = owner // (count_y // 2) * cells_x + cell // cells_y
+    place_y = owner % (count_y // 2) * cells_y + cell % cells_y
+    column = np.arange(KY // 2 * KX)
+    number_x = column % KX
+    block = column // KX
+    tables = []
+    for number_y in (np.where(block % 2 == 0, block, block + 7), np.where(block % 2 == 1, block, block + 9)):
+        turns = np.outer(place_x, host_freq(number_x, KX)) / length_x
+        turns = turns + np.outer(place_y, host_freq(number_y, KY)) / length_y
+        angles = 2.0 * np.pi * turns
+        tables.append(np.concatenate([np.cos(angles), np.sin(angles)], axis=1))
+    return np.stack(tables) / np.sqrt(length_x * length_y)
 
 
 def product(left, right, left_dim, right_dim):
@@ -292,6 +297,24 @@
     for copy in tables:
         copy.wait()
     out_ref[...] = product((high_ref[...], low_ref[...]), halves(rows_ref[...]), 1, 1)
+
+
+def blocks_even(shape):
+    return lax.broadcasted_iota(jnp.int32, shape, 1) // KX % 2 == 0
+
+
+def in_ky_order(even, odd):
+    mask = blocks_even(even.shape)
+    low = jnp.where(mask, even, odd)
+    high = jnp.where(mask, pltpu.roll(even, LANES - KX, 1), pltpu.roll(odd, KX, 1))
+    return low, high
+
+
+def by_ky_parity(low, high):
+    mask = blocks_even(low.shape)
+    even = jnp.where(mask, low, pltpu.roll(high, KX, 1))
+    odd = jnp.where(mask, pltpu.roll(high, LANES - KX, 1), low)
+    return even, odd
 
 
 def mode_kernel(
@@ -319,37 +342,47 @@
         place = (slice(None), span) if conjugate else (slice(None), slice(None), span)
         weight_copies.append(start(weight_hbm.at[place], weight_ref.at[place], weight_sems.at[k]))
     rows = channels * local_modes
-    cells = high_ref.shape[0]
-    owners = got_ref.shape[0] // (2 * local_modes)
     block = 2 * local_modes
-    table = (high_ref[...], low_ref[...])
-    for quad in range(owners // 4):
-        for group in range(channels // 4):
-            parts = [
-                got_ref[(4 * quad + j) * block : (4 * quad + j + 1) * block, group * LANES : (group + 1) * LANES]
-                for j in range(4)
+    quads = got_ref.shape[0] // (4 * block)
+    groups = channels // 4
+
+    def owner_rows(quad, j):
+        return slice((4 * quad + j) * block, (4 * quad + j + 1) * block)
+
+    for pair in range(quads // 2):
+        for group in range(groups):
+            lanes = slice(group * LANES, (group + 1) * LANES)
+            near_half, far_half = [
+                [got_ref[owner_rows(2 * pair + i, 2 * half + j), lanes] for i in range(2) for j in range(2)] for half in range(2)
             ]
-            for m, part in enumerate(swap_groups(parts)):
-                row = (4 * group + m) * local_modes
-                for side in range(2):
-                    field_ref[side * rows + row : side * rows + row + local_modes, quad * LANES : (quad + 1) * LANES] = part[
-                        side * local_modes : (side + 1) * local_modes
-                    ]
-    waves = product(halves(field_ref[...]), table, 1, 0)
-    real = waves[:rows, :modes] + waves[rows:, modes:]
-    imag = waves[rows:, :modes] - waves[:rows, modes:]
-    spectra_ref[0] = real.reshape(channels, local_modes, modes)
-    spectra_ref[1] = imag.reshape(channels, local_modes, modes)
+            sums = [one + other for one, other in zip(near_half, far_half)]
+            gaps = [one - other for one, other in zip(near_half, far_half)]
+            for parity, parts in enumerate((sums, gaps)):
+                for m, part in enumerate(swap_groups(parts)):
+                    row = (4 * group + m) * local_modes
+                    for side in range(2):
+                        field_ref[
+                            parity, side * rows + row : side * rows + row + local_modes, pair * LANES : (pair + 1) * LANES
+                        ] = part[side * local_modes : (side + 1) * local_modes]
+    real = []
+    imag = []
+    for parity in range(2):
+        waves = product(halves(field_ref[parity]), (high_ref[parity], low_ref[parity]), 1, 0)
+        real.append(waves[:rows, :LANES] + waves[rows:, LANES:])
+        imag.append(waves[rows:, :LANES] - waves[:rows, LANES:])
+    for part, pair in enumerate((real, imag)):
+        for k, values in enumerate(in_ky_order(*pair)):
+            spectra_ref[part, :, :, k * LANES : (k + 1) * LANES] = values.reshape(channels, local_modes, LANES)
     spectra_copy = start(spectra_ref, spectra_hbm, spectra_sem)
-    for part in range(len(weight_copies) * modes // LANES):
-        first_lane = part % (modes // LANES) * LANES
-        first_result = part // (modes // LANES) * chunk
+    for part in range(len(weight_copies) * 2):
+        first_lane = part % 2 * LANES
+        first_result = part // 2 * chunk
         span = slice(first_lane, first_lane + LANES)
         ins = [(spectra_ref[0, c, :, span], spectra_ref[1, c, :, span]) for c in range(channels)]
         if first_lane == 0:
-            weight_copies[part // (modes // LANES)].wait()
-
-        def one(step, carry, span=span, ins=ins, first_lane=first_lane, first_result=first_result):
+            weight_copies[part // 2].wait()
+
+        def one(step, carry, span=span, ins=ins, first_result=first_result):
             result = first_result + step
             total_real = jnp.zeros((local_modes, LANES), jnp.float32)
             total_imag = jnp.zeros((local_modes, LANES), jnp.float32)
@@ -365,32 +398,46 @@
                     total_real = total_real + (in_real * w_real - in_imag * w_imag)
                     total_imag = total_imag + (in_imag * w_real + in_real * w_imag)
             row = pl.multiple_of(result * local_modes, local_modes)
-            other = pl.multiple_of(rows + result * local_modes, local_modes)
-            mixed_ref[pl.ds(row, local_modes), first_lane : first_lane + LANES] = total_real
-            mixed_ref[pl.ds(other, local_modes), first_lane : first_lane + LANES] = total_imag
-            mixed_ref[pl.ds(row, local_modes), modes + first_lane : modes + first_lane + LANES] = -total_imag
-            mixed_ref[pl.ds(other, local_modes), modes + first_lane : modes + first_lane + LANES] = total_real
+            mixed_ref[0, pl.ds(row, local_modes), span] = total_real
+            mixed_ref[1, pl.ds(row, local_modes), span] = total_imag
             return carry
 
         lax.fori_loop(0, chunk, one, 0, unroll=True)
-    mixed = halves(mixed_ref[...])
     out_copies = []
-    for quad in range(owners // 4):
-        if quad % 2 == 0:
-            span = slice(quad * LANES, min(quad + 2, owners // 4) * LANES)
-            field_ref[:, span] = product(mixed, (high_ref[span, :], low_ref[span, :]), 1, 1)
-        for group in range(channels // 4):
-            for side in range(2):
-                first = side * rows + 4 * group * local_modes
-                parts = [
-                    field_ref[first + m * local_modes : first + (m + 1) * local_modes, quad * LANES : (quad + 1) * LANES]
-                    for m in range(4)
-                ]
-                for j, part in enumerate(swap_groups(parts)):
-                    row = (4 * quad + j) * block + side * local_modes
-                    out_ref[row : row + local_modes, group * LANES : (group + 1) * LANES] = part
-        span = pl.ds(4 * quad * block, 4 * block)
-        out_copies.append(start(out_ref.at[span], out_hbm.at[span], out_sems.at[quad]))
+    for first, last in spans_of(groups, -(-groups // 2)):
+        begin, end = 4 * first * local_modes, 4 * last * local_modes
+        reals = by_ky_parity(mixed_ref[0, begin:end, :LANES], mixed_ref[0, begin:end, LANES:])
+        imags = by_ky_parity(mixed_ref[1, begin:end, :LANES], mixed_ref[1, begin:end, LANES:])
+        for parity in range(2):
+            left = jnp.concatenate([reals[parity], imags[parity]], axis=0)
+            right = jnp.concatenate([-imags[parity], reals[parity]], axis=0)
+            both = halves(jnp.concatenate([left, right], axis=1))
+            field_ref[parity, 2 * begin : 2 * end, :] = product(both, (high_ref[parity], low_ref[parity]), 1, 1)
+        for pair in range(quads // 2):
+            for group in range(first, last):
+                lanes = slice(group * LANES, (group + 1) * LANES)
+                for side in range(2):
+                    base = 2 * begin + side * (end - begin) + 4 * (group - first) * local_modes
+                    sums, gaps = [
+                        swap_groups(
+                            [
+                                field_ref[
+                                    parity,
+                                    base + m * local_modes : base + (m + 1) * local_modes,
+                                    pair * LANES : (pair + 1) * LANES,
+                                ]
+                                for m in range(4)
+                            ]
+                        )
+                        for parity in range(2)
+                    ]
+                    for k in range(4):
+                        row = (4 * (2 * pair + k // 2) + k % 2) * block + side * local_modes
+                        other = row + 2 * block
+                        out_ref[row : row + local_modes, lanes] = sums[k] + gaps[k]
+                        out_ref[other : other + local_modes, lanes] = sums[k] - gaps[k]
+        place = (slice(None), pl.ds(first * LANES, (last - first) * LANES))
+        out_copies.append(start(out_ref.at[place], out_hbm.at[place], out_sems.at[len(out_copies)]))
     spectra_copy.wait()
     for copy in out_copies:
         copy.wait()
@@ -545,11 +592,11 @@
                 vmem(spectral_weight.shape, f32),
                 vmem(sent, f32),
                 vmem(spectrum, f32),
-                vmem((2 * channels * local_modes, owners * cells_x * cells_y), f32),
-                vmem((2 * channels * local_modes, 2 * modes), f32),
-                copies((4,)),
+                vmem((2, 2 * channels * local_modes, owners * cells_x * cells_y // 2), f32),
+                vmem((2, channels * local_modes, modes), f32),
+                copies((5,)),
                 copies,
-                copies((owners // 4,)),
+                copies((2,)),
             ],
             compiler_params=params(),
             name="unmix_modes" if conjugate else "mix_modes",
@@ -637,9 +684,9 @@
 
     def on_any(*args):
         _, channels, cells_x, cells_y, _ = args[0].shape
-        owners = lax.axis_size("gx") * lax.axis_size("gy")
-        fits = args[2].shape[3] == 8 and cells_x * cells_y == LANES // 4
-        fits = fits and channels % 4 == 0 and owners % 4 == 0 and lax.axis_size("dp") == 2
+        fits = args[2].shape[3] == 8 and args[2].shape[4] == 2 * LANES and KX * KY == 2 * LANES and cells_x * cells_y == LANES // 4
+        fits = fits and channels % 20 == 0 and lax.axis_size("dp") == 2
+        fits = fits and lax.axis_size("gx") % 2 == 0 and lax.axis_size("gy") == 4 and cells_y * 4 == KY
         return on_tiles(*args) if fits else on_device(*args)
 
     return jax.shard_map(

time: 111 us -> 110 us (level)
  Pallas kernels: 35.7 us -> 34.3 us
    pallas_call x2, Pallas kernels: 11 us -> 9.7 us  [across(): pl.pallas_call(body, out_shape=(held(sent), held(spectrum)), in_specs=[wh...]
where the time goes in v3:
time: 110 us; the launch traced here: 109 us
  blocking collectives  47.4 us (43%)
  Pallas kernels  34.3 us (31%)
  waiting for transfers between devices  15.3 us (14%)
  starting transfers between devices  10.6 us (10%)
    all_to_all x2, blocking collectives, trade(): lax.all_to_all(values, ('gx', 'gy'), split_axis=0, concat_axis=0, tiled=T...  47.4 us
    all_to_all x2, waiting for transfers between devices, trade(): lax.all_to_all(values, ('gx', 'gy'), split_axis=0, concat_axis=0, tiled=T...  10.6 us
    pallas_call x2, Pallas kernels, across(): pl.pallas_call(body, out_shape=(held(sent), held(spectrum)), in_specs=[wh...  9.7 us
    all_to_all x2, starting transfers between devices, trade(): lax.all_to_all(values, ('gx', 'gy'), split_axis=0, concat_axis=0, tiled=T...  7.47 us
    pallas_call x1, Pallas kernels, on_tiles(): pl.pallas_call(local_kernel, out_shape=(held(cells), held(cells)), in_spe...  6.72 us
    pallas_call x1, Pallas kernels, on_tiles(): pl.pallas_call(grads_kernel, out_shape=held(cells), in_specs=[whole, scal...  5.43 us
    pallas_call x1, Pallas kernels, on_tiles(): pl.pallas_call(outer_kernel, out_shape=held(spectral_weight.shape), grid=...  5.32 us
    ppermute x2, waiting for transfers between devices, in_order(): other = lax.ppermute(own, 'dp', [(0, 1), (1, 0)])  4.65 us
  transfers between devices with their start and end apart: 4, of which 4 were waited for; matrix products, arithmetic and copies ran while one was open for 1% of the time, Pallas kernels for 16%

profile of v3, /device:TPU:0, one launch (start us, length us, event | category | flops | bytes accessed | tf_op | source)
XLA Modules:
  0.0 109.4 jit_solution(4828783920965293392)
XLA Ops:
  0.6 0.0 copy-start.4
  0.6 0.0 copy-start.5
  0.7 2.4 %front.1 = f32[256,640]{1,0:T(8,128)S(1)} custom-call(f32[20,8,4,512]{3,2,1,0:T(4,128)} %bitcast.17, bf16[256,512]{1,0:T(8,128)(2,1)} %constant.16.clone.high_hbm.high_ref, bf16[256,512]{1,0:T(8,128)(2,1)} %constant.17.clone.low_hbm.low_ref), custom_call_target="tpu_custom_call" | custom-call | tf_op jit(solution)/shard_map/front/pallas_call | solution.py:605
  3.0 25.7 %all_to_all.45 = f32[16,16,640]{2,1,0:T(8,128)S(1)} all-to-all(f32[16,16,640]{2,1,0:T(8,128)S(1)} %bitcast.11), channel_id=1, replica_groups=mesh['dp'=2,'gx'=4,'gy'=4] {'gx','gy'}, dimensions={0} | all-to-all | bytes 1310720 | tf_op jit(solution)/shard_map/all_to_all | solution.py:580
  28.7 4.9 %mix_modes.1 = (f32[256,640]{1,0:T(8,128)}, f32[2,20,8,256]{3,2,1,0:T(8,128)}) custom-call(f32[256,640]{1,0:T(8,128)S(1)} %bitcast.15, f32[2,20,20,8,256]{4,3,2,1,0:T(8,128)} %refs_1_.3, bf16[2,256,256]{2,1,0:T(8,128)(2,1)S(1)} %copy-done.5, bf16[2,256,256]{2,1,0:T(8,128)(2,1)S(1)} %copy-done.4), custom_call_target="tpu_custom_call" | custom-call | tf_op jit(solution)/shard_map/mix_modes/pallas_call | solution.py:586
  33.6 0.0 copy-start.7
  33.7 3.7 %all-to-all-start.1 = ((f32[16,16,640]{2,1,0:T(8,128)}), f32[16,16,640]{2,1,0:T(8,128)S(1)}, u32[]{:S(2)}, u32[]{:S(2)}) async-start(f32[16,16,640]{2,1,0:T(8,128)} %bitcast.21), calls=%async_computation.1 | async-start | bytes 1310720 | tf_op jit(solution)/shard_map/all_to_all | solution.py:580
  37.4 1.6 %collective-permute-start = (f32[2,20,8,256]{3,2,1,0:T(8,128)S(1)}, f32[2,20,8,256]{3,2,1,0:T(8,128)S(1)}, u32[]{:S(2)}, u32[]{:S(2)}) collective-permute-start(f32[2,20,8,256]{3,2,1,0:T(8,128)S(1)} %copy-done.8), channel_id=1, source_target_pairs={{0,16},{16,0},{1,17},{17,1},{2,18},{18,2},{3,19},{19,3},{4,20},{20... | collective-permute-start | bytes 983048 | tf_op jit(solution)/shard_map/ppermute | solution.py:539
  39.0 6.7 %local_pre.1 = (f32[640,512]{1,0:T(8,128)}, f32[640,512]{1,0:T(8,128)}) custom-call(f32[20,8,4,512]{3,2,1,0:T(4,128)} %bitcast.18, f32[20,8,4,512]{3,2,1,0:T(4,128)} %bitcast.19, f32[20,20]{1,0:T(8,128)S(1)} %copy-done.6, f32[20]{0:T(128)S(1)} %copy-done.7), custom_call_target="tpu_custom_call" | custom-call | tf_op jit(solution)/shard_map/local_pre/pallas_call | solution.py:622
  45.7 1.7 %collective-permute-done = f32[2,20,8,256]{3,2,1,0:T(8,128)S(1)} collective-permute-done((f32[2,20,8,256]{3,2,1,0:T(8,128)S(1)}, f32[2,20,8,256]{3,2,1,0:T(8,128)S(1)}, u32[]{:S(2)}, u32[]{:S(2)}) %collective-permute-start) | collective-permute-done | bytes 327712 | tf_op jit(solution)/shard_map/ppermute | solution.py:539
  47.4 0.9 broadcast_select_fusion.2
  48.3 7.5 %all-to-all-done.1 = f32[16,16,640]{2,1,0:T(8,128)S(1)} async-done(((f32[16,16,640]{2,1,0:T(8,128)}), f32[16,16,640]{2,1,0:T(8,128)S(1)}, u32[]{:S(2)}, u32[]{:S(2)}) %all-to-all-start.1) | async-done | bytes 655392 | tf_op jit(solution)/shard_map/all_to_all | solution.py:580
  55.9 3.1 %middle.1 = (f32[256,640]{1,0:T(8,128)S(1)}, f32[640,512]{1,0:T(8,128)S(1)}) custom-call(f32[256,640]{1,0:T(8,128)S(1)} %bitcast.12, f32[640,512]{1,0:T(8,128)} %get-tuple-element.16.local_hbm, f32[640,512]{1,0:T(8,128)} %get-tuple-element.17.upstream_hbm, bf16[256,512]{1,0:T(8,128)(2,1)S(1)} %copy-done.2, bf16[256,512]{1,0:T(8,128)(2,1)S(1)} %copy-done.1), custom_call_target="tpu_custom_call" | custom-call | tf_op jit(solution)/shard_map/middle/pallas_call | solution.py:634
  59.0 0.0 copy-start.3
  59.0 21.7 %all_to_all.46 = f32[16,16,640]{2,1,0:T(8,128)S(1)} all-to-all(f32[16,16,640]{2,1,0:T(8,128)S(1)} %bitcast.16), channel_id=1, replica_groups=mesh['dp'=2,'gx'=4,'gy'=4] {'gx','gy'}, dimensions={0} | all-to-all | bytes 1310720 | tf_op jit(solution)/shard_map/all_to_all | solution.py:580
  80.7 4.8 %unmix_modes.1 = (f32[256,640]{1,0:T(8,128)}, f32[2,20,8,256]{3,2,1,0:T(8,128)}) custom-call(f32[256,640]{1,0:T(8,128)S(1)} %bitcast.14, f32[2,20,20,8,256]{4,3,2,1,0:T(8,128)} %refs_1_.3, bf16[2,256,256]{2,1,0:T(8,128)(2,1)S(1)} %copy-done.5, bf16[2,256,256]{2,1,0:T(8,128)(2,1)S(1)} %copy-done.4), custom_call_target="tpu_custom_call" | custom-call | tf_op jit(solution)/shard_map/unmix_modes/pallas_call | solution.py:586
  85.5 0.0 copy-start.9
  85.5 3.7 %all-to-all-start.3 = ((f32[16,16,640]{2,1,0:T(8,128)}), f32[16,16,640]{2,1,0:T(8,128)S(1)}, u32[]{:S(2)}, u32[]{:S(2)}) async-start(f32[16,16,640]{2,1,0:T(8,128)} %bitcast.22), calls=%async_computation.3 | async-start | bytes 1310720 | tf_op jit(solution)/shard_map/all_to_all | solution.py:580
  89.3 1.6 %collective-permute-start.1 = (f32[2,20,8,256]{3,2,1,0:T(8,128)S(1)}, f32[2,20,8,256]{3,2,1,0:T(8,128)S(1)}, u32[]{:S(2)}, u32[]{:S(2)}) collective-permute-start(f32[2,20,8,256]{3,2,1,0:T(8,128)S(1)} %copy-done.9), channel_id=1, source_target_pairs={{0,16},{16,0},{1,17},{17,1},{2,18},{18,2},{3,19},{19,3},{4,20},{20... | collective-permute-start | bytes 983048 | tf_op jit(solution)/shard_map/ppermute | solution.py:539
  90.9 5.4 %local_grad.1.local_ref = f32[640,512]{1,0:T(8,128)} custom-call(f32[640,512]{1,0:T(8,128)} %copy-done.3, f32[20,20]{1,0:T(8,128)S(1)} %copy-done.6), custom_call_target="tpu_custom_call" | custom-call | tf_op jit(solution)/shard_map/local_grad/pallas_call | solution.py:647
  96.3 3.0 %collective-permute-done.1 = f32[2,20,8,256]{3,2,1,0:T(8,128)S(1)} collective-permute-done((f32[2,20,8,256]{3,2,1,0:T(8,128)S(1)}, f32[2,20,8,256]{3,2,1,0:T(8,128)S(1)}, u32[]{:S(2)}, u32[]{:S(2)}) %collective-permute-start.1) | collective-permute-done | bytes 327712 | tf_op jit(solution)/shard_map/ppermute | solution.py:539
  99.3 5.3 %outer.1 = f32[2,20,20,8,256]{4,3,2,1,0:T(8,128)} custom-call(f32[2,20,8,256]{3,2,1,0:T(8,128)} %get-tuple-element.21.first_spectra, f32[2,20,8,256]{3,2,1,0:T(8,128)} %get-tuple-element.22.second_spectra, f32[2,20,8,256]{3,2,1,0:T(8,128)S(1)} %get-tuple-element.25.first_grads, f32[2,20,8,256]{3,2,1,0:T(8,128)S(1)} %get-tuple-element.24.second_grads), custom_call_target="tpu_custom_call" | custom-call | tf_op jit(solution)/shard_map/outer/pallas_call | solution.py:655
  104.6 3.1 %all-to-all-done.3 = f32[16,16,640]{2,1,0:T(8,128)S(1)} async-done(((f32[16,16,640]{2,1,0:T(8,128)}), f32[16,16,640]{2,1,0:T(8,128)S(1)}, u32[]{:S(2)}, u32[]{:S(2)}) %all-to-all-start.3) | async-done | bytes 655392 | tf_op jit(solution)/shard_map/all_to_all | solution.py:580
  107.7 1.7 %last.1 = f32[20,8,4,512]{3,2,1,0:T(4,128)} custom-call(f32[256,640]{1,0:T(8,128)S(1)} %bitcast.13, f32[640,512]{1,0:T(8,128)S(1)} %copy-done, bf16[256,512]{1,0:T(8,128)(2,1)S(1)} %copy-done.2, bf16[256,512]{1,0:T(8,128)(2,1)S(1)} %copy-done.1), custom_call_target="tpu_custom_call" | custom-call | tf_op jit(solution)/shard_map/last/pallas_call | solution.py:664
  (16 shorter events, 0.1 us)
Async XLA Ops:
  0.6 28.1 %copy-start.4 = (bf16[2,256,256]{2,1,0:T(8,128)(2,1)S(1)}, bf16[2,256,256]{2,1,0:T(8,128)(2,1)}, u32[]{:S(2)}) copy-start(bf16[2,256,256]{2,1,0:T(8,128)(2,1)} %constant.19.clone.refs_3_) | copy-start | bytes 786436
  0.6 28.1 %copy-start.5 = (bf16[2,256,256]{2,1,0:T(8,128)(2,1)S(1)}, bf16[2,256,256]{2,1,0:T(8,128)(2,1)}, u32[]{:S(2)}) copy-start(bf16[2,256,256]{2,1,0:T(8,128)(2,1)} %constant.18.clone.refs_2_) | copy-start | bytes 786436
  33.6 3.8 %copy-start.8 = (f32[2,20,8,256]{3,2,1,0:T(8,128)S(1)}, f32[2,20,8,256]{3,2,1,0:T(8,128)}, u32[]{:S(2)}) copy-start(f32[2,20,8,256]{3,2,1,0:T(8,128)} %get-tuple-element.14) | copy-start | bytes 983044
  33.6 5.4 %copy-start.6 = (f32[20,20]{1,0:T(8,128)S(1)}, f32[20,20]{1,0:T(8,128)}, u32[]{:S(2)}) copy-start(f32[20,20]{1,0:T(8,128)} %weight_ref.3) | copy-start | bytes 4804
  33.6 5.4 %copy-start.7 = (f32[20]{0:T(128)S(1)}, f32[20]{0:T(128)}, u32[]{:S(2)}) copy-start(f32[20]{0:T(128)} %bias_ref.1) | copy-start | bytes 244
  33.7 22.2 %all-to-all-start.1 = ((f32[16,16,640]{2,1,0:T(8,128)}), f32[16,16,640]{2,1,0:T(8,128)S(1)}, u32[]{:S(2)}, u32[]{:S(2)}) async-start(f32[16,16,640]{2,1,0:T(8,128)} %bitcast.21), calls=%async_computation.1 | async-start | bytes 1310720 | tf_op jit(solution)/shard_map/all_to_all | solution.py:580
  37.4 10.0 %collective-permute-start = (f32[2,20,8,256]{3,2,1,0:T(8,128)S(1)}, f32[2,20,8,256]{3,2,1,0:T(8,128)S(1)}, u32[]{:S(2)}, u32[]{:S(2)}) collective-permute-start(f32[2,20,8,256]{3,2,1,0:T(8,128)S(1)} %copy-done.8), channel_id=1, source_target_pairs={{0,16},{16,0},{1,17},{17,1},{2,18},{18,2},{3,19},{19,3},{4,20},{20... | collective-permute-start | bytes 983048 | tf_op jit(solution)/shard_map/ppermute | solution.py:539
  45.7 10.1 %copy-start.1 = (bf16[256,512]{1,0:T(8,128)(2,1)S(1)}, bf16[256,512]{1,0:T(8,128)(2,1)}, u32[]{:S(2)}) copy-start(bf16[256,512]{1,0:T(8,128)(2,1)} %constant.17.clone.low_hbm.low_ref) | copy-start | bytes 786436
  45.7 10.1 %copy-start.2 = (bf16[256,512]{1,0:T(8,128)(2,1)S(1)}, bf16[256,512]{1,0:T(8,128)(2,1)}, u32[]{:S(2)}) copy-start(bf16[256,512]{1,0:T(8,128)(2,1)} %constant.16.clone.high_hbm.high_ref) | copy-start | bytes 786436
  59.0 26.5 %copy-start.3 = (f32[640,512]{1,0:T(8,128)}, f32[640,512]{1,0:T(8,128)S(1)}, u32[]{:S(2)}) copy-start(f32[640,512]{1,0:T(8,128)S(1)} %get-tuple-element.20.rows_ref) | copy-start | bytes 3932164
  85.5 3.8 %copy-start.9 = (f32[2,20,8,256]{3,2,1,0:T(8,128)S(1)}, f32[2,20,8,256]{3,2,1,0:T(8,128)}, u32[]{:S(2)}) copy-start(f32[2,20,8,256]{3,2,1,0:T(8,128)} %get-tuple-element.23) | copy-start | bytes 983044
  85.5 22.2 %all-to-all-start.3 = ((f32[16,16,640]{2,1,0:T(8,128)}), f32[16,16,640]{2,1,0:T(8,128)S(1)}, u32[]{:S(2)}, u32[]{:S(2)}) async-start(f32[16,16,640]{2,1,0:T(8,128)} %bitcast.22), calls=%async_computation.3 | async-start | bytes 1310720 | tf_op jit(solution)/shard_map/all_to_all | solution.py:580
  89.3 10.0 %collective-permute-start.1 = (f32[2,20,8,256]{3,2,1,0:T(8,128)S(1)}, f32[2,20,8,256]{3,2,1,0:T(8,128)S(1)}, u32[]{:S(2)}, u32[]{:S(2)}) collective-permute-start(f32[2,20,8,256]{3,2,1,0:T(8,128)S(1)} %copy-done.9), channel_id=1, source_target_pairs={{0,16},{16,0},{1,17},{17,1},{2,18},{18,2},{3,19},{19,3},{4,20},{20... | collective-permute-start | bytes 983048 | tf_op jit(solution)/shard_map/ppermute | solution.py:539
  99.3 8.4 %copy-start = (f32[640,512]{1,0:T(8,128)S(1)}, f32[640,512]{1,0:T(8,128)}, u32[]{:S(2)}) copy-start(f32[640,512]{1,0:T(8,128)} %local_grad.1.local_ref) | copy-start | bytes 3932164

commit v4 on v3

--- a/solution.py
+++ b/solution.py
@@ -204,13 +204,13 @@
 
 def host_plane(owners, local_modes):
     mode = np.arange(owners * local_modes)
-    cell = np.arange(NZ * NT)
+    cell = np.arange(NZ * NT // 2)
     turns = np.outer(host_freq(mode // KT, KZ), cell // NT) / NZ
     turns = turns + np.outer(host_freq(mode % KT, KT), cell % NT) / NT
     angles = 2.0 * np.pi * turns
     table = np.stack([np.cos(angles), -np.sin(angles)]) / np.sqrt(NZ * NT)
-    table = table.reshape(2, owners, local_modes, NZ * NT)
-    return np.swapaxes(table, 0, 1).reshape(owners * 2 * local_modes, NZ * NT)
+    table = table.reshape(2, owners // 2, 2, local_modes, NZ * NT // 2)
+    return table.transpose(2, 1, 0, 3, 4).reshape(2, owners * local_modes, NZ * NT // 2)
 
 
 def host_cross(count_x, count_y, cells_x, cells_y):
@@ -275,6 +275,27 @@
     return copy
 
 
+def to_plane_modes(rows_ref, high_ref, low_ref, out_ref):
+    half = rows_ref.shape[1] // 2
+    block = out_ref.shape[0] // 16
+    for parity in range(2):
+        one, other = rows_ref[:, :half], rows_ref[:, half:]
+        values = one - other if parity else one + other
+        waves = product((high_ref[parity], low_ref[parity]), halves(values), 1, 1)
+        for k in range(8):
+            row = (2 * k + parity) * block
+            out_ref[row : row + block, :] = waves[k * block : (k + 1) * block]
+
+
+def from_plane_modes(got_ref, high_ref, low_ref):
+    block = got_ref.shape[0] // 16
+    waves = []
+    for parity in range(2):
+        parts = [got_ref[(2 * k + parity) * block : (2 * k + parity + 1) * block, :] for k in range(8)]
+        waves.append(product(halves(jnp.concatenate(parts, axis=0)), (high_ref[parity], low_ref[parity]), 0, 0))
+    return jnp.concatenate([waves[0] + waves[1], waves[0] - waves[1]], axis=1)
+
+
 def spans_of(channels, step):
     return [(first, min(first + step, channels)) for first in range(0, channels, step)]
 
@@ -296,7 +317,7 @@
                 rows_ref[row : row + cells_y, :] = field_ref[channel, place]
     for copy in tables:
         copy.wait()
-    out_ref[...] = product((high_ref[...], low_ref[...]), halves(rows_ref[...]), 1, 1)
+    to_plane_modes(rows_ref, high_ref, low_ref, out_ref)
 
 
 def blocks_even(shape):
@@ -476,14 +497,13 @@
         (start(local_hbm.at[span], local_ref.at[span], sems.at[0, k]), start(upstream_hbm.at[span], upstream_ref.at[span], sems.at[1, k]))
         for k, span in enumerate(spans)
     ]
-    table = (high_ref[...], low_ref[...])
-    grad_ref[...] = product(halves(got_ref[...]), table, 0, 0)
+    grad_ref[...] = from_plane_modes(got_ref, high_ref, low_ref)
     for k, span in enumerate(spans):
         rows = slice(span.start, span.start + span.size)
         for copy in copies[k]:
             copy.wait()
         grad_ref[rows, :] = upstream_ref[rows, :] * gelu_slope(grad_ref[rows, :] + local_ref[rows, :])
-    out_ref[...] = product(table, halves(grad_ref[...]), 1, 1)
+    to_plane_modes(grad_ref, high_ref, low_ref, out_ref)
 
 
 def grads_kernel(rows_ref, weight_ref, out_ref):
@@ -493,7 +513,7 @@
 def last_kernel(got_ref, local_ref, high_ref, low_ref, out_hbm, rows_ref, out_ref, sems):
     channels, cells_x, cells_y, _ = out_ref.shape
     cells = cells_x * cells_y
-    rows_ref[...] = product(halves(got_ref[...]), (high_ref[...], low_ref[...]), 0, 0)
+    rows_ref[...] = from_plane_modes(got_ref, high_ref, low_ref)
     leaving = []
     for first, last in spans_of(channels, 4):
         rows = slice(first * cells, last * cells)
@@ -685,8 +705,8 @@
     def on_any(*args):
         _, channels, cells_x, cells_y, _ = args[0].shape
         fits = args[2].shape[3] == 8 and args[2].shape[4] == 2 * LANES and KX * KY == 2 * LANES and cells_x * cells_y == LANES // 4
-        fits = fits and channels % 20 == 0 and lax.axis_size("dp") == 2
-        fits = fits and lax.axis_size("gx") % 2 == 0 and lax.axis_size("gy") == 4 and cells_y * 4 == KY
+        fits = fits and channels % 20 == 0 and args[2].shape[3] == KT and KZ * KT == 16 * 8 and lax.axis_size("dp") == 2
+        fits = fits and lax.axis_size("gx") == 4 and lax.axis_size("gy") == 4 and cells_y * 4 == KY
         return on_tiles(*args) if fits else on_device(*args)
 
     return jax.shard_map(

time: 110 us -> 110 us (level)
  no operation moved by 1% of the time
where the time goes in v4:
time: 110 us; the launch traced here: 109 us
  blocking collectives  47.4 us (43%)
  Pallas kernels  33.9 us (31%)
  waiting for transfers between devices  15.3 us (14%)
  starting transfers between devices  10.7 us (10%)
    all_to_all x2, blocking collectives, trade(): lax.all_to_all(values, ('gx', 'gy'), split_axis=0, concat_axis=0, tiled=T...  47.4 us
    all_to_all x2, waiting for transfers between devices, trade(): lax.all_to_all(values, ('gx', 'gy'), split_axis=0, concat_axis=0, tiled=T...  10.6 us
    pallas_call x2, Pallas kernels, across(): pl.pallas_call(body, out_shape=(held(sent), held(spectrum)), in_specs=[wh...  9.7 us
    all_to_all x2, starting transfers between devices, trade(): lax.all_to_all(values, ('gx', 'gy'), split_axis=0, concat_axis=0, tiled=T...  7.47 us
    pallas_call x1, Pallas kernels, on_tiles(): pl.pallas_call(local_kernel, out_shape=(held(cells), held(cells)), in_spe...  6.72 us
    pallas_call x1, Pallas kernels, on_tiles(): pl.pallas_call(grads_kernel, out_shape=held(cells), in_specs=[whole, scal...  5.43 us
    pallas_call x1, Pallas kernels, on_tiles(): pl.pallas_call(outer_kernel, out_shape=held(spectral_weight.shape), grid=...  5.32 us
    ppermute x2, waiting for transfers between devices, in_order(): other = lax.ppermute(own, 'dp', [(0, 1), (1, 0)])  4.64 us
  transfers between devices with their start and end apart: 4, of which 4 were waited for; matrix products, arithmetic and copies ran while one was open for 1% of the time, Pallas kernels for 16%

profile of v4, /device:TPU:0, one launch (start us, length us, event | category | flops | bytes accessed | tf_op | source)
XLA Modules:
  0.0 109.0 jit_solution(16982509948425008325)
XLA Ops:
  0.6 0.0 copy-start.4
  0.6 0.0 copy-start.5
  0.7 2.3 %front.1 = f32[256,640]{1,0:T(8,128)S(1)} custom-call(f32[20,8,4,512]{3,2,1,0:T(4,128)} %bitcast.17, bf16[2,128,256]{2,1,0:T(8,128)(2,1)} %constant.16.clone.high_hbm.high_ref, bf16[2,128,256]{2,1,0:T(8,128)(2,1)} %constant.17.clone.low_hbm.low_ref), custom_call_target="tpu_custom_call" | custom-call | tf_op jit(solution)/shard_map/front/pallas_call | solution.py:625
  2.9 25.7 %all_to_all.45 = f32[16,16,640]{2,1,0:T(8,128)S(1)} all-to-all(f32[16,16,640]{2,1,0:T(8,128)S(1)} %bitcast.13), channel_id=1, replica_groups=mesh['dp'=2,'gx'=4,'gy'=4] {'gx','gy'}, dimensions={0} | all-to-all | bytes 1310720 | tf_op jit(solution)/shard_map/all_to_all | solution.py:600
  28.6 4.9 %mix_modes.1 = (f32[256,640]{1,0:T(8,128)}, f32[2,20,8,256]{3,2,1,0:T(8,128)}) custom-call(f32[256,640]{1,0:T(8,128)S(1)} %bitcast.15, f32[2,20,20,8,256]{4,3,2,1,0:T(8,128)} %refs_1_.3, bf16[2,256,256]{2,1,0:T(8,128)(2,1)S(1)} %copy-done.5, bf16[2,256,256]{2,1,0:T(8,128)(2,1)S(1)} %copy-done.4), custom_call_target="tpu_custom_call" | custom-call | tf_op jit(solution)/shard_map/mix_modes/pallas_call | solution.py:606
  33.5 0.0 copy-start.8
  33.5 0.0 copy-start.6
  33.5 3.7 %all-to-all-start.1 = ((f32[16,16,640]{2,1,0:T(8,128)}), f32[16,16,640]{2,1,0:T(8,128)S(1)}, u32[]{:S(2)}, u32[]{:S(2)}) async-start(f32[16,16,640]{2,1,0:T(8,128)} %bitcast.21), calls=%async_computation.1 | async-start | bytes 1310720 | tf_op jit(solution)/shard_map/all_to_all | solution.py:600
  37.3 1.6 %collective-permute-start = (f32[2,20,8,256]{3,2,1,0:T(8,128)S(1)}, f32[2,20,8,256]{3,2,1,0:T(8,128)S(1)}, u32[]{:S(2)}, u32[]{:S(2)}) collective-permute-start(f32[2,20,8,256]{3,2,1,0:T(8,128)S(1)} %copy-done.8), channel_id=1, source_target_pairs={{0,16},{16,0},{1,17},{17,1},{2,18},{18,2},{3,19},{19,3},{4,20},{20... | collective-permute-start | bytes 983048 | tf_op jit(solution)/shard_map/ppermute | solution.py:559
  38.9 6.7 %local_pre.1 = (f32[640,512]{1,0:T(8,128)}, f32[640,512]{1,0:T(8,128)}) custom-call(f32[20,8,4,512]{3,2,1,0:T(4,128)} %bitcast.18, f32[20,8,4,512]{3,2,1,0:T(4,128)} %bitcast.20, f32[20,20]{1,0:T(8,128)S(1)} %copy-done.6, f32[20]{0:T(128)S(1)} %copy-done.7), custom_call_target="tpu_custom_call" | custom-call | tf_op jit(solution)/shard_map/local_pre/pallas_call | solution.py:642
  45.6 1.7 %collective-permute-done = f32[2,20,8,256]{3,2,1,0:T(8,128)S(1)} collective-permute-done((f32[2,20,8,256]{3,2,1,0:T(8,128)S(1)}, f32[2,20,8,256]{3,2,1,0:T(8,128)S(1)}, u32[]{:S(2)}, u32[]{:S(2)}) %collective-permute-start) | collective-permute-done | bytes 327712 | tf_op jit(solution)/shard_map/ppermute | solution.py:559
  47.3 0.9 broadcast_select_fusion.2
  48.2 7.5 %all-to-all-done.1 = f32[16,16,640]{2,1,0:T(8,128)S(1)} async-done(((f32[16,16,640]{2,1,0:T(8,128)}), f32[16,16,640]{2,1,0:T(8,128)S(1)}, u32[]{:S(2)}, u32[]{:S(2)}) %all-to-all-start.1) | async-done | bytes 655392 | tf_op jit(solution)/shard_map/all_to_all | solution.py:600
  55.7 2.8 %middle.1 = (f32[256,640]{1,0:T(8,128)S(1)}, f32[640,512]{1,0:T(8,128)S(1)}) custom-call(f32[256,640]{1,0:T(8,128)S(1)} %bitcast.11, f32[640,512]{1,0:T(8,128)} %get-tuple-element.16.local_hbm, f32[640,512]{1,0:T(8,128)} %get-tuple-element.17.upstream_hbm, bf16[2,128,256]{2,1,0:T(8,128)(2,1)S(1)} %copy-done.3, bf16[2,128,256]{2,1,0:T(8,128)(2,1)S(1)} %copy-done.2), custom_call_target="tpu_custom_call" | custom-call | tf_op jit(solution)/shard_map/middle/pallas_call | solution.py:654
  58.6 0.0 copy-start.1
  58.6 21.7 %all_to_all.46 = f32[16,16,640]{2,1,0:T(8,128)S(1)} all-to-all(f32[16,16,640]{2,1,0:T(8,128)S(1)} %bitcast.16), channel_id=1, replica_groups=mesh['dp'=2,'gx'=4,'gy'=4] {'gx','gy'}, dimensions={0} | all-to-all | bytes 1310720 | tf_op jit(solution)/shard_map/all_to_all | solution.py:600
  80.3 4.8 %unmix_modes.1 = (f32[256,640]{1,0:T(8,128)}, f32[2,20,8,256]{3,2,1,0:T(8,128)}) custom-call(f32[256,640]{1,0:T(8,128)S(1)} %bitcast.14, f32[2,20,20,8,256]{4,3,2,1,0:T(8,128)} %refs_1_.3, bf16[2,256,256]{2,1,0:T(8,128)(2,1)S(1)} %copy-done.5, bf16[2,256,256]{2,1,0:T(8,128)(2,1)S(1)} %copy-done.4), custom_call_target="tpu_custom_call" | custom-call | tf_op jit(solution)/shard_map/unmix_modes/pallas_call | solution.py:606
  85.1 3.7 %all-to-all-start.3 = ((f32[16,16,640]{2,1,0:T(8,128)}), f32[16,16,640]{2,1,0:T(8,128)S(1)}, u32[]{:S(2)}, u32[]{:S(2)}) async-start(f32[16,16,640]{2,1,0:T(8,128)} %bitcast.22), calls=%async_computation.3 | async-start | bytes 1310720 | tf_op jit(solution)/shard_map/all_to_all | solution.py:600
  88.9 1.6 %collective-permute-start.1 = (f32[2,20,8,256]{3,2,1,0:T(8,128)S(1)}, f32[2,20,8,256]{3,2,1,0:T(8,128)S(1)}, u32[]{:S(2)}, u32[]{:S(2)}) collective-permute-start(f32[2,20,8,256]{3,2,1,0:T(8,128)S(1)} %copy-done.9), channel_id=1, source_target_pairs={{0,16},{16,0},{1,17},{17,1},{2,18},{18,2},{3,19},{19,3},{4,20},{20... | collective-permute-start | bytes 983048 | tf_op jit(solution)/shard_map/ppermute | solution.py:559
  90.5 5.4 %local_grad.1.local_ref = f32[640,512]{1,0:T(8,128)} custom-call(f32[640,512]{1,0:T(8,128)} %copy-done.1, f32[20,20]{1,0:T(8,128)S(1)} %copy-done.6), custom_call_target="tpu_custom_call" | custom-call | tf_op jit(solution)/shard_map/local_grad/pallas_call | solution.py:667
  95.9 3.0 %collective-permute-done.1 = f32[2,20,8,256]{3,2,1,0:T(8,128)S(1)} collective-permute-done((f32[2,20,8,256]{3,2,1,0:T(8,128)S(1)}, f32[2,20,8,256]{3,2,1,0:T(8,128)S(1)}, u32[]{:S(2)}, u32[]{:S(2)}) %collective-permute-start.1) | collective-permute-done | bytes 327712 | tf_op jit(solution)/shard_map/ppermute | solution.py:559
  98.9 5.3 %outer.1 = f32[2,20,20,8,256]{4,3,2,1,0:T(8,128)} custom-call(f32[2,20,8,256]{3,2,1,0:T(8,128)} %get-tuple-element.21.first_spectra, f32[2,20,8,256]{3,2,1,0:T(8,128)} %get-tuple-element.22.second_spectra, f32[2,20,8,256]{3,2,1,0:T(8,128)S(1)} %get-tuple-element.25.first_grads, f32[2,20,8,256]{3,2,1,0:T(8,128)S(1)} %get-tuple-element.24.second_grads), custom_call_target="tpu_custom_call" | custom-call | tf_op jit(solution)/shard_map/outer/pallas_call | solution.py:675
  104.2 3.1 %all-to-all-done.3 = f32[16,16,640]{2,1,0:T(8,128)S(1)} async-done(((f32[16,16,640]{2,1,0:T(8,128)}), f32[16,16,640]{2,1,0:T(8,128)S(1)}, u32[]{:S(2)}, u32[]{:S(2)}) %all-to-all-start.3) | async-done | bytes 655392 | tf_op jit(solution)/shard_map/all_to_all | solution.py:600
  107.3 1.7 %last.1 = f32[20,8,4,512]{3,2,1,0:T(4,128)} custom-call(f32[256,640]{1,0:T(8,128)S(1)} %bitcast.12, f32[640,512]{1,0:T(8,128)S(1)} %copy-done, bf16[2,128,256]{2,1,0:T(8,128)(2,1)S(1)} %copy-done.3, bf16[2,128,256]{2,1,0:T(8,128)(2,1)S(1)} %copy-done.2), custom_call_target="tpu_custom_call" | custom-call | tf_op jit(solution)/shard_map/last/pallas_call | solution.py:684
  (16 shorter events, 0.1 us)
Async XLA Ops:
  0.6 28.0 %copy-start.4 = (bf16[2,256,256]{2,1,0:T(8,128)(2,1)S(1)}, bf16[2,256,256]{2,1,0:T(8,128)(2,1)}, u32[]{:S(2)}) copy-start(bf16[2,256,256]{2,1,0:T(8,128)(2,1)} %constant.19.clone.refs_3_) | copy-start | bytes 786436
  0.6 28.0 %copy-start.5 = (bf16[2,256,256]{2,1,0:T(8,128)(2,1)S(1)}, bf16[2,256,256]{2,1,0:T(8,128)(2,1)}, u32[]{:S(2)}) copy-start(bf16[2,256,256]{2,1,0:T(8,128)(2,1)} %constant.18.clone.refs_2_) | copy-start | bytes 786436
  33.5 3.8 %copy-start.8 = (f32[2,20,8,256]{3,2,1,0:T(8,128)S(1)}, f32[2,20,8,256]{3,2,1,0:T(8,128)}, u32[]{:S(2)}) copy-start(f32[2,20,8,256]{3,2,1,0:T(8,128)} %get-tuple-element.14) | copy-start | bytes 983044
  33.5 5.4 %copy-start.6 = (f32[20,20]{1,0:T(8,128)S(1)}, f32[20,20]{1,0:T(8,128)}, u32[]{:S(2)}) copy-start(f32[20,20]{1,0:T(8,128)} %weight_ref.3) | copy-start | bytes 4804
  33.5 5.4 %copy-start.7 = (f32[20]{0:T(128)S(1)}, f32[20]{0:T(128)}, u32[]{:S(2)}) copy-start(f32[20]{0:T(128)} %bias_ref.1) | copy-start | bytes 244
  33.5 22.2 %all-to-all-start.1 = ((f32[16,16,640]{2,1,0:T(8,128)}), f32[16,16,640]{2,1,0:T(8,128)S(1)}, u32[]{:S(2)}, u32[]{:S(2)}) async-start(f32[16,16,640]{2,1,0:T(8,128)} %bitcast.21), calls=%async_computation.1 | async-start | bytes 1310720 | tf_op jit(solution)/shard_map/all_to_all | solution.py:600
  37.3 10.0 %collective-permute-start = (f32[2,20,8,256]{3,2,1,0:T(8,128)S(1)}, f32[2,20,8,256]{3,2,1,0:T(8,128)S(1)}, u32[]{:S(2)}, u32[]{:S(2)}) collective-permute-start(f32[2,20,8,256]{3,2,1,0:T(8,128)S(1)} %copy-done.8), channel_id=1, source_target_pairs={{0,16},{16,0},{1,17},{17,1},{2,18},{18,2},{3,19},{19,3},{4,20},{20... | collective-permute-start | bytes 983048 | tf_op jit(solution)/shard_map/ppermute | solution.py:559
  45.6 10.1 %copy-start.2 = (bf16[2,128,256]{2,1,0:T(8,128)(2,1)S(1)}, bf16[2,128,256]{2,1,0:T(8,128)(2,1)}, u32[]{:S(2)}) copy-start(bf16[2,128,256]{2,1,0:T(8,128)(2,1)} %constant.17.clone.low_hbm.low_ref) | copy-start | bytes 393220
  45.6 10.1 %copy-start.3 = (bf16[2,128,256]{2,1,0:T(8,128)(2,1)S(1)}, bf16[2,128,256]{2,1,0:T(8,128)(2,1)}, u32[]{:S(2)}) copy-start(bf16[2,128,256]{2,1,0:T(8,128)(2,1)} %constant.16.clone.high_hbm.high_ref) | copy-start | bytes 393220
  58.6 26.5 %copy-start.1 = (f32[640,512]{1,0:T(8,128)}, f32[640,512]{1,0:T(8,128)S(1)}, u32[]{:S(2)}) copy-start(f32[640,512]{1,0:T(8,128)S(1)} %get-tuple-element.20.rows_ref) | copy-start | bytes 3932164
  85.1 3.8 %copy-start.9 = (f32[2,20,8,256]{3,2,1,0:T(8,128)S(1)}, f32[2,20,8,256]{3,2,1,0:T(8,128)}, u32[]{:S(2)}) copy-start(f32[2,20,8,256]{3,2,1,0:T(8,128)} %get-tuple-element.23) | copy-start | bytes 983044
  85.1 22.2 %all-to-all-start.3 = ((f32[16,16,640]{2,1,0:T(8,128)}), f32[16,16,640]{2,1,0:T(8,128)S(1)}, u32[]{:S(2)}, u32[]{:S(2)}) async-start(f32[16,16,640]{2,1,0:T(8,128)} %bitcast.22), calls=%async_computation.3 | async-start | bytes 1310720 | tf_op jit(solution)/shard_map/all_to_all | solution.py:600
  88.9 10.0 %collective-permute-start.1 = (f32[2,20,8,256]{3,2,1,0:T(8,128)S(1)}, f32[2,20,8,256]{3,2,1,0:T(8,128)S(1)}, u32[]{:S(2)}, u32[]{:S(2)}) collective-permute-start(f32[2,20,8,256]{3,2,1,0:T(8,128)S(1)} %copy-done.9), channel_id=1, source_target_pairs={{0,16},{16,0},{1,17},{17,1},{2,18},{18,2},{3,19},{19,3},{4,20},{20... | collective-permute-start | bytes 983048 | tf_op jit(solution)/shard_map/ppermute | solution.py:559
  98.9 8.4 %copy-start = (f32[640,512]{1,0:T(8,128)S(1)}, f32[640,512]{1,0:T(8,128)}, u32[]{:S(2)}) copy-start(f32[640,512]{1,0:T(8,128)} %local_grad.1.local_ref) | copy-start | bytes 3932164

commit v5 on v4

--- a/solution.py
+++ b/solution.py
@@ -283,7 +283,7 @@
         values = one - other if parity else one + other
         waves = product((high_ref[parity], low_ref[parity]), halves(values), 1, 1)
         for k in range(8):
-            row = (2 * k + parity) * block
+            row = slot(2 * k + parity) * block
             out_ref[row : row + block, :] = waves[k * block : (k + 1) * block]
 
 
@@ -291,9 +291,14 @@
     block = got_ref.shape[0] // 16
     waves = []
     for parity in range(2):
-        parts = [got_ref[(2 * k + parity) * block : (2 * k + parity + 1) * block, :] for k in range(8)]
+        rows = [slot(2 * k + parity) * block for k in range(8)]
+        parts = [got_ref[row : row + block, :] for row in rows]
         waves.append(product(halves(jnp.concatenate(parts, axis=0)), (high_ref[parity], low_ref[parity]), 0, 0))
     return jnp.concatenate([waves[0] + waves[1], waves[0] - waves[1]], axis=1)
+
+
+def slot(owner):
+    return owner % 4 * 4 + owner // 4
 
 
 def spans_of(channels, step):
@@ -368,7 +373,8 @@
     groups = channels // 4
 
     def owner_rows(quad, j):
-        return slice((4 * quad + j) * block, (4 * quad + j + 1) * block)
+        first = slot(4 * quad + j) * block
+        return slice(first, first + block)
 
     for pair in range(quads // 2):
         for group in range(groups):
@@ -453,8 +459,9 @@
                         for parity in range(2)
                     ]
                     for k in range(4):
-                        row = (4 * (2 * pair + k // 2) + k % 2) * block + side * local_modes
-                        other = row + 2 * block
+                        owner = 4 * (2 * pair + k // 2) + k % 2
+                        row = slot(owner) * block + side * local_modes
+                        other = slot(owner + 2) * block + side * local_modes
                         out_ref[row : row + local_modes, lanes] = sums[k] + gaps[k]
                         out_ref[other : other + local_modes, lanes] = sums[k] - gaps[k]
         place = (slice(None), pl.ds(first * LANES, (last - first) * LANES))
@@ -597,7 +604,7 @@
         return pltpu.HBM(shape, f32)
 
     def trade(values):
-        return lax.all_to_all(values, ("gx", "gy"), split_axis=0, concat_axis=0, tiled=True)
+        return lax.all_to_all(values, ("gy", "gx"), split_axis=0, concat_axis=0, tiled=True)
 
     def across(values, conjugate):
         def body(*refs):

time: 110 us -> 107 us (0.973)
  waiting for transfers between devices: 15.3 us -> 11.5 us
    all_to_all x2, waiting for transfers between devices: 10.6 us -> 6.88 us  [trade(): lax.all_to_all(values, ('gy', 'gx'), split_axis=0, concat_axis=0, tiled=T...]
where the time goes in v5:
time: 107 us; the launch traced here: 106 us
  blocking collectives  48.2 us (45%)
  Pallas kernels  33.9 us (32%)
  waiting for transfers between devices  11.5 us (11%)
  starting transfers between devices  10.6 us (10%)
    all_to_all x2, blocking collectives, trade(): lax.all_to_all(values, ('gy', 'gx'), split_axis=0, concat_axis=0, tiled=T...  48.2 us
    pallas_call x2, Pallas kernels, across(): pl.pallas_call(body, out_shape=(held(sent), held(spectrum)), in_specs=[wh...  9.7 us
    all_to_all x2, starting transfers between devices, trade(): lax.all_to_all(values, ('gy', 'gx'), split_axis=0, concat_axis=0, tiled=T...  7.47 us
    all_to_all x2, waiting for transfers between devices, trade(): lax.all_to_all(values, ('gy', 'gx'), split_axis=0, concat_axis=0, tiled=T...  6.88 us
    pallas_call x1, Pallas kernels, on_tiles(): pl.pallas_call(local_kernel, out_shape=(held(cells), held(cells)), in_spe...  6.72 us
    pallas_call x1, Pallas kernels, on_tiles(): pl.pallas_call(grads_kernel, out_shape=held(cells), in_specs=[whole, scal...  5.43 us
    pallas_call x1, Pallas kernels, on_tiles(): pl.pallas_call(outer_kernel, out_shape=held(spectral_weight.shape), grid=...  5.32 us
    ppermute x2, waiting for transfers between devices, in_order(): other = lax.ppermute(own, 'dp', [(0, 1), (1, 0)])  4.6 us
  transfers between devices with their start and end apart: 4, of which 4 were waited for; matrix products, arithmetic and copies ran while one was open for 1% of the time, Pallas kernels for 16%

profile of v5, /device:TPU:0, one launch (start us, length us, event | category | flops | bytes accessed | tf_op | source)
XLA Modules:
  0.0 106.0 jit_solution(11544166445167145147)
XLA Ops:
  0.6 0.0 copy-start.4
  0.6 0.0 copy-start.5
  0.7 2.3 %front.1 = f32[256,640]{1,0:T(8,128)S(1)} custom-call(f32[20,8,4,512]{3,2,1,0:T(4,128)} %bitcast.17, bf16[2,128,256]{2,1,0:T(8,128)(2,1)} %constant.16.clone.high_hbm.high_ref, bf16[2,128,256]{2,1,0:T(8,128)(2,1)} %constant.17.clone.low_hbm.low_ref), custom_call_target="tpu_custom_call" | custom-call | tf_op jit(solution)/shard_map/front/pallas_call | solution.py:632
  2.9 25.4 %all_to_all.45 = f32[16,16,640]{2,1,0:T(8,128)S(1)} all-to-all(f32[16,16,640]{2,1,0:T(8,128)S(1)} %bitcast.13), channel_id=1, replica_groups=mesh['dp'=2,'gx'=4,'gy'=4] {'gy','gx'}, dimensions={0} | all-to-all | bytes 1310720 | tf_op jit(solution)/shard_map/all_to_all | solution.py:607
  28.3 4.9 %mix_modes.1 = (f32[256,640]{1,0:T(8,128)}, f32[2,20,8,256]{3,2,1,0:T(8,128)}) custom-call(f32[256,640]{1,0:T(8,128)S(1)} %bitcast.15, f32[2,20,20,8,256]{4,3,2,1,0:T(8,128)} %refs_1_.3, bf16[2,256,256]{2,1,0:T(8,128)(2,1)S(1)} %copy-done.5, bf16[2,256,256]{2,1,0:T(8,128)(2,1)S(1)} %copy-done.4), custom_call_target="tpu_custom_call" | custom-call | tf_op jit(solution)/shard_map/mix_modes/pallas_call | solution.py:613
  33.2 0.0 copy-start.8
  33.2 0.0 copy-start.6
  33.2 0.0 copy-start.7
  33.2 3.7 %all-to-all-start.1 = ((f32[16,16,640]{2,1,0:T(8,128)}), f32[16,16,640]{2,1,0:T(8,128)S(1)}, u32[]{:S(2)}, u32[]{:S(2)}) async-start(f32[16,16,640]{2,1,0:T(8,128)} %bitcast.21), calls=%async_computation.1 | async-start | bytes 1310720 | tf_op jit(solution)/shard_map/all_to_all | solution.py:607
  37.0 1.6 %collective-permute-start = (f32[2,20,8,256]{3,2,1,0:T(8,128)S(1)}, f32[2,20,8,256]{3,2,1,0:T(8,128)S(1)}, u32[]{:S(2)}, u32[]{:S(2)}) collective-permute-start(f32[2,20,8,256]{3,2,1,0:T(8,128)S(1)} %copy-done.8), channel_id=1, source_target_pairs={{0,16},{16,0},{1,17},{17,1},{2,18},{18,2},{3,19},{19,3},{4,20},{20... | collective-permute-start | bytes 983048 | tf_op jit(solution)/shard_map/ppermute | solution.py:566
  38.6 6.7 %local_pre.1 = (f32[640,512]{1,0:T(8,128)}, f32[640,512]{1,0:T(8,128)}) custom-call(f32[20,8,4,512]{3,2,1,0:T(4,128)} %bitcast.18, f32[20,8,4,512]{3,2,1,0:T(4,128)} %bitcast.20, f32[20,20]{1,0:T(8,128)S(1)} %copy-done.6, f32[20]{0:T(128)S(1)} %copy-done.7), custom_call_target="tpu_custom_call" | custom-call | tf_op jit(solution)/shard_map/local_pre/pallas_call | solution.py:649
  45.3 1.7 %collective-permute-done = f32[2,20,8,256]{3,2,1,0:T(8,128)S(1)} collective-permute-done((f32[2,20,8,256]{3,2,1,0:T(8,128)S(1)}, f32[2,20,8,256]{3,2,1,0:T(8,128)S(1)}, u32[]{:S(2)}, u32[]{:S(2)}) %collective-permute-start) | collective-permute-done | bytes 327712 | tf_op jit(solution)/shard_map/ppermute | solution.py:566
  47.0 0.9 broadcast_select_fusion.2
  47.9 5.7 %all-to-all-done.1 = f32[16,16,640]{2,1,0:T(8,128)S(1)} async-done(((f32[16,16,640]{2,1,0:T(8,128)}), f32[16,16,640]{2,1,0:T(8,128)S(1)}, u32[]{:S(2)}, u32[]{:S(2)}) %all-to-all-start.1) | async-done | bytes 655392 | tf_op jit(solution)/shard_map/all_to_all | solution.py:607
  53.5 2.8 %middle.1 = (f32[256,640]{1,0:T(8,128)S(1)}, f32[640,512]{1,0:T(8,128)S(1)}) custom-call(f32[256,640]{1,0:T(8,128)S(1)} %bitcast.11, f32[640,512]{1,0:T(8,128)} %get-tuple-element.16.local_hbm, f32[640,512]{1,0:T(8,128)} %get-tuple-element.17.upstream_hbm, bf16[2,128,256]{2,1,0:T(8,128)(2,1)S(1)} %copy-done.3, bf16[2,128,256]{2,1,0:T(8,128)(2,1)S(1)} %copy-done.2), custom_call_target="tpu_custom_call" | custom-call | tf_op jit(solution)/shard_map/middle/pallas_call | solution.py:661
  56.4 22.8 %all_to_all.46 = f32[16,16,640]{2,1,0:T(8,128)S(1)} all-to-all(f32[16,16,640]{2,1,0:T(8,128)S(1)} %bitcast.16), channel_id=1, replica_groups=mesh['dp'=2,'gx'=4,'gy'=4] {'gy','gx'}, dimensions={0} | all-to-all | bytes 1310720 | tf_op jit(solution)/shard_map/all_to_all | solution.py:607
  79.1 4.8 %unmix_modes.1 = (f32[256,640]{1,0:T(8,128)}, f32[2,20,8,256]{3,2,1,0:T(8,128)}) custom-call(f32[256,640]{1,0:T(8,128)S(1)} %bitcast.14, f32[2,20,20,8,256]{4,3,2,1,0:T(8,128)} %refs_1_.3, bf16[2,256,256]{2,1,0:T(8,128)(2,1)S(1)} %copy-done.5, bf16[2,256,256]{2,1,0:T(8,128)(2,1)S(1)} %copy-done.4), custom_call_target="tpu_custom_call" | custom-call | tf_op jit(solution)/shard_map/unmix_modes/pallas_call | solution.py:613
  84.0 3.7 %all-to-all-start.3 = ((f32[16,16,640]{2,1,0:T(8,128)}), f32[16,16,640]{2,1,0:T(8,128)S(1)}, u32[]{:S(2)}, u32[]{:S(2)}) async-start(f32[16,16,640]{2,1,0:T(8,128)} %bitcast.22), calls=%async_computation.3 | async-start | bytes 1310720 | tf_op jit(solution)/shard_map/all_to_all | solution.py:607
  87.7 1.6 %collective-permute-start.1 = (f32[2,20,8,256]{3,2,1,0:T(8,128)S(1)}, f32[2,20,8,256]{3,2,1,0:T(8,128)S(1)}, u32[]{:S(2)}, u32[]{:S(2)}) collective-permute-start(f32[2,20,8,256]{3,2,1,0:T(8,128)S(1)} %copy-done.9), channel_id=1, source_target_pairs={{0,16},{16,0},{1,17},{17,1},{2,18},{18,2},{3,19},{19,3},{4,20},{20... | collective-permute-start | bytes 983048 | tf_op jit(solution)/shard_map/ppermute | solution.py:566
  89.3 5.4 %local_grad.1.local_ref = f32[640,512]{1,0:T(8,128)} custom-call(f32[640,512]{1,0:T(8,128)} %copy-done.1, f32[20,20]{1,0:T(8,128)S(1)} %copy-done.6), custom_call_target="tpu_custom_call" | custom-call | tf_op jit(solution)/shard_map/local_grad/pallas_call | solution.py:674
  94.8 2.9 %collective-permute-done.1 = f32[2,20,8,256]{3,2,1,0:T(8,128)S(1)} collective-permute-done((f32[2,20,8,256]{3,2,1,0:T(8,128)S(1)}, f32[2,20,8,256]{3,2,1,0:T(8,128)S(1)}, u32[]{:S(2)}, u32[]{:S(2)}) %collective-permute-start.1) | collective-permute-done | bytes 327712 | tf_op jit(solution)/shard_map/ppermute | solution.py:566
  97.8 5.3 %outer.1 = f32[2,20,20,8,256]{4,3,2,1,0:T(8,128)} custom-call(f32[2,20,8,256]{3,2,1,0:T(8,128)} %get-tuple-element.21.first_spectra, f32[2,20,8,256]{3,2,1,0:T(8,128)} %get-tuple-element.22.second_spectra, f32[2,20,8,256]{3,2,1,0:T(8,128)S(1)} %get-tuple-element.25.first_grads, f32[2,20,8,256]{3,2,1,0:T(8,128)S(1)} %get-tuple-element.24.second_grads), custom_call_target="tpu_custom_call" | custom-call | tf_op jit(solution)/shard_map/outer/pallas_call | solution.py:682
  103.1 1.2 %all-to-all-done.3 = f32[16,16,640]{2,1,0:T(8,128)S(1)} async-done(((f32[16,16,640]{2,1,0:T(8,128)}), f32[16,16,640]{2,1,0:T(8,128)S(1)}, u32[]{:S(2)}, u32[]{:S(2)}) %all-to-all-start.3) | async-done | bytes 655392 | tf_op jit(solution)/shard_map/all_to_all | solution.py:607
  104.3 1.7 %last.1 = f32[20,8,4,512]{3,2,1,0:T(4,128)} custom-call(f32[256,640]{1,0:T(8,128)S(1)} %bitcast.12, f32[640,512]{1,0:T(8,128)S(1)} %copy-done, bf16[2,128,256]{2,1,0:T(8,128)(2,1)S(1)} %copy-done.3, bf16[2,128,256]{2,1,0:T(8,128)(2,1)S(1)} %copy-done.2), custom_call_target="tpu_custom_call" | custom-call | tf_op jit(solution)/shard_map/last/pallas_call | solution.py:691
  (16 shorter events, 0.1 us)
Async XLA Ops:
  0.6 27.7 %copy-start.4 = (bf16[2,256,256]{2,1,0:T(8,128)(2,1)S(1)}, bf16[2,256,256]{2,1,0:T(8,128)(2,1)}, u32[]{:S(2)}) copy-start(bf16[2,256,256]{2,1,0:T(8,128)(2,1)} %constant.19.clone.refs_3_) | copy-start | bytes 786436
  0.6 27.7 %copy-start.5 = (bf16[2,256,256]{2,1,0:T(8,128)(2,1)S(1)}, bf16[2,256,256]{2,1,0:T(8,128)(2,1)}, u32[]{:S(2)}) copy-start(bf16[2,256,256]{2,1,0:T(8,128)(2,1)} %constant.18.clone.refs_2_) | copy-start | bytes 786436
  33.2 3.8 %copy-start.8 = (f32[2,20,8,256]{3,2,1,0:T(8,128)S(1)}, f32[2,20,8,256]{3,2,1,0:T(8,128)}, u32[]{:S(2)}) copy-start(f32[2,20,8,256]{3,2,1,0:T(8,128)} %get-tuple-element.14) | copy-start | bytes 983044
  33.2 5.4 %copy-start.6 = (f32[20,20]{1,0:T(8,128)S(1)}, f32[20,20]{1,0:T(8,128)}, u32[]{:S(2)}) copy-start(f32[20,20]{1,0:T(8,128)} %weight_ref.3) | copy-start | bytes 4804
  33.2 5.4 %copy-start.7 = (f32[20]{0:T(128)S(1)}, f32[20]{0:T(128)}, u32[]{:S(2)}) copy-start(f32[20]{0:T(128)} %bias_ref.1) | copy-start | bytes 244
  33.2 20.3 %all-to-all-start.1 = ((f32[16,16,640]{2,1,0:T(8,128)}), f32[16,16,640]{2,1,0:T(8,128)S(1)}, u32[]{:S(2)}, u32[]{:S(2)}) async-start(f32[16,16,640]{2,1,0:T(8,128)} %bitcast.21), calls=%async_computation.1 | async-start | bytes 1310720 | tf_op jit(solution)/shard_map/all_to_all | solution.py:607
  37.0 10.0 %collective-permute-start = (f32[2,20,8,256]{3,2,1,0:T(8,128)S(1)}, f32[2,20,8,256]{3,2,1,0:T(8,128)S(1)}, u32[]{:S(2)}, u32[]{:S(2)}) collective-permute-start(f32[2,20,8,256]{3,2,1,0:T(8,128)S(1)} %copy-done.8), channel_id=1, source_target_pairs={{0,16},{16,0},{1,17},{17,1},{2,18},{18,2},{3,19},{19,3},{4,20},{20... | collective-permute-start | bytes 983048 | tf_op jit(solution)/shard_map/ppermute | solution.py:566
  45.3 8.2 %copy-start.2 = (bf16[2,128,256]{2,1,0:T(8,128)(2,1)S(1)}, bf16[2,128,256]{2,1,0:T(8,128)(2,1)}, u32[]{:S(2)}) copy-start(bf16[2,128,256]{2,1,0:T(8,128)(2,1)} %constant.17.clone.low_hbm.low_ref) | copy-start | bytes 393220
  45.3 8.2 %copy-start.3 = (bf16[2,128,256]{2,1,0:T(8,128)(2,1)S(1)}, bf16[2,128,256]{2,1,0:T(8,128)(2,1)}, u32[]{:S(2)}) copy-start(bf16[2,128,256]{2,1,0:T(8,128)(2,1)} %constant.16.clone.high_hbm.high_ref) | copy-start | bytes 393220
  56.4 27.6 %copy-start.1 = (f32[640,512]{1,0:T(8,128)}, f32[640,512]{1,0:T(8,128)S(1)}, u32[]{:S(2)}) copy-start(f32[640,512]{1,0:T(8,128)S(1)} %get-tuple-element.20.rows_ref) | copy-start | bytes 3932164
  84.0 3.8 %copy-start.9 = (f32[2,20,8,256]{3,2,1,0:T(8,128)S(1)}, f32[2,20,8,256]{3,2,1,0:T(8,128)}, u32[]{:S(2)}) copy-start(f32[2,20,8,256]{3,2,1,0:T(8,128)} %get-tuple-element.23) | copy-start | bytes 983044
  84.0 20.3 %all-to-all-start.3 = ((f32[16,16,640]{2,1,0:T(8,128)}), f32[16,16,640]{2,1,0:T(8,128)S(1)}, u32[]{:S(2)}, u32[]{:S(2)}) async-start(f32[16,16,640]{2,1,0:T(8,128)} %bitcast.22), calls=%async_computation.3 | async-start | bytes 1310720 | tf_op jit(solution)/shard_map/all_to_all | solution.py:607
  87.7 10.0 %collective-permute-start.1 = (f32[2,20,8,256]{3,2,1,0:T(8,128)S(1)}, f32[2,20,8,256]{3,2,1,0:T(8,128)S(1)}, u32[]{:S(2)}, u32[]{:S(2)}) collective-permute-start(f32[2,20,8,256]{3,2,1,0:T(8,128)S(1)} %copy-done.9), channel_id=1, source_target_pairs={{0,16},{16,0},{1,17},{17,1},{2,18},{18,2},{3,19},{19,3},{4,20},{20... | collective-permute-start | bytes 983048 | tf_op jit(solution)/shard_map/ppermute | solution.py:566
  97.8 6.5 %copy-start = (f32[640,512]{1,0:T(8,128)S(1)}, f32[640,512]{1,0:T(8,128)}, u32[]{:S(2)}) copy-start(f32[640,512]{1,0:T(8,128)} %local_grad.1.local_ref) | copy-start | bytes 3932164

commit v6 on v5

--- a/solution.py
+++ b/solution.py
@@ -305,7 +305,9 @@
     return [(first, min(first + step, channels)) for first in range(0, channels, step)]
 
 
-def front_kernel(field_hbm, high_hbm, low_hbm, out_ref, field_ref, high_ref, low_ref, rows_ref, table_sems, field_sems):
+def front_kernel(
+    field_hbm, high_hbm, low_hbm, weight_hbm, out_ref, head_ref, field_ref, high_ref, low_ref, rows_ref, table_sems, field_sems, head_sem
+):
     channels, cells_x, cells_y, _ = field_ref.shape
     cells = cells_x * cells_y
     pieces = []
@@ -314,6 +316,7 @@
         pieces.append(start(field_hbm.at[span], field_ref.at[span], field_sems.at[len(pieces)]))
         if first == 0:
             tables = [start(high_hbm, high_ref, table_sems.at[0]), start(low_hbm, low_ref, table_sems.at[1])]
+    head = start(weight_hbm.at[:, :, pl.ds(0, head_ref.shape[2])], head_ref, head_sem)
     for piece, (first, last) in enumerate(spans_of(channels, 4)):
         pieces[piece].wait()
         for channel in range(first, last):
@@ -323,6 +326,7 @@
     for copy in tables:
         copy.wait()
     to_plane_modes(rows_ref, high_ref, low_ref, out_ref)
+    head.wait()
 
 
 def blocks_even(shape):
@@ -344,7 +348,7 @@
 
 
 def mode_kernel(
-    conjugate,
+    head_ref,
     got_ref,
     weight_hbm,
     high_ref,
@@ -361,9 +365,12 @@
     out_sems,
 ):
     _, channels, local_modes, modes = spectra_ref.shape
+    conjugate = head_ref is None
     chunk = channels // weight_sems.shape[0]
     weight_copies = []
     for k in range(weight_sems.shape[0]):
+        if k == 0 and not conjugate:
+            continue
         span = pl.ds(k * chunk, chunk)
         place = (slice(None), span) if conjugate else (slice(None), slice(None), span)
         weight_copies.append(start(weight_hbm.at[place], weight_ref.at[place], weight_sems.at[k]))
@@ -401,27 +408,28 @@
         for k, values in enumerate(in_ky_order(*pair)):
             spectra_ref[part, :, :, k * LANES : (k + 1) * LANES] = values.reshape(channels, local_modes, LANES)
     spectra_copy = start(spectra_ref, spectra_hbm, spectra_sem)
-    for part in range(len(weight_copies) * 2):
+    for part in range(weight_sems.shape[0] * 2):
         first_lane = part % 2 * LANES
         first_result = part // 2 * chunk
         span = slice(first_lane, first_lane + LANES)
         ins = [(spectra_ref[0, c, :, span], spectra_ref[1, c, :, span]) for c in range(channels)]
-        if first_lane == 0:
-            weight_copies[part // 2].wait()
-
-        def one(step, carry, span=span, ins=ins, first_result=first_result):
+        if first_lane == 0 and (conjugate or first_result > 0):
+            weight_copies[part // 2 - (not conjugate)].wait()
+        mixing_ref = weight_ref if conjugate or first_result > 0 else head_ref
+
+        def one(step, carry, span=span, ins=ins, first_result=first_result, mixing_ref=mixing_ref):
             result = first_result + step
             total_real = jnp.zeros((local_modes, LANES), jnp.float32)
             total_imag = jnp.zeros((local_modes, LANES), jnp.float32)
             for c, (in_real, in_imag) in enumerate(ins):
                 if conjugate:
-                    w_real = weight_ref[0, result, c, :, span]
-                    w_imag = weight_ref[1, result, c, :, span]
+                    w_real = mixing_ref[0, result, c, :, span]
+                    w_imag = mixing_ref[1, result, c, :, span]
                     total_real = total_real + (in_real * w_real + in_imag * w_imag)
                     total_imag = total_imag + (in_imag * w_real - in_real * w_imag)
                 else:
-                    w_real = weight_ref[0, c, result, :, span]
-                    w_imag = weight_ref[1, c, result, :, span]
+                    w_real = mixing_ref[0, c, result, :, span]
+                    w_imag = mixing_ref[1, c, result, :, span]
                     total_real = total_real + (in_real * w_real - in_imag * w_imag)
                     total_imag = total_imag + (in_imag * w_real + in_real * w_imag)
             row = pl.multiple_of(result * local_modes, local_modes)
@@ -606,14 +614,16 @@
     def trade(values):
         return lax.all_to_all(values, ("gy", "gx"), split_axis=0, concat_axis=0, tiled=True)
 
-    def across(values, conjugate):
+    def across(values, *head):
+        conjugate = not head
+
         def body(*refs):
-            mode_kernel(conjugate, *refs)
+            mode_kernel(*((None,) if conjugate else ()), *refs)
 
         return pl.pallas_call(
             body,
             out_shape=(held(sent), held(spectrum)),
-            in_specs=[whole, stays, whole, whole],
+            in_specs=[*[whole] * len(head), whole, stays, whole, whole],
             out_specs=(stays, stays),
             scratch_shapes=[
                 vmem(spectral_weight.shape, f32),
@@ -627,13 +637,13 @@
             ],
             compiler_params=params(),
             name="unmix_modes" if conjugate else "mix_modes",
-        )(*near(values), *far(spectral_weight), *near(*cross))
-
-    front = pl.pallas_call(
+        )(*near(*head, values), *far(spectral_weight), *near(*cross))
+
+    front, head = pl.pallas_call(
         front_kernel,
-        out_shape=vmem(sent, f32),
-        in_specs=[stays] * 3,
-        out_specs=whole,
+        out_shape=(vmem(sent, f32), vmem((2, channels, channels // 5, local_modes, modes), f32)),
+        in_specs=[stays] * 4,
+        out_specs=(whole, whole),
         scratch_shapes=[
             vmem(sample_cells.shape, f32),
             vmem(plane[0].shape, bf16),
@@ -641,10 +651,11 @@
             vmem(cells, f32),
             copies((2,)),
             copies((-(-channels // 4),)),
+            copies,
         ],
         compiler_params=params(),
         name="front",
-    )(*far(sample_cells, *plane))
+    )(*far(sample_cells, *plane, spectral_weight))
     got = trade(front)
     local, packed = pl.pallas_call(
         local_kernel,
@@ -655,7 +666,7 @@
         compiler_params=params(),
         name="local_pre",
     )(*far(sample_cells, upstream), channel_weight, channel_bias)
-    mixed, spectra = across(got, False)
+    mixed, spectra = across(got, head)
     both_spectra = in_order(spectra)
     got, both_spectra = lax.optimization_barrier((trade(mixed), both_spectra))
     front, grad_pre = pl.pallas_call(
@@ -668,7 +679,7 @@
         name="middle",
     )(*near(got), *far(local, packed), *near(*plane))
     got = trade(front)
-    back, grad_spectra = across(got, True)
+    back, grad_spectra = across(got)
     both_grads = in_order(grad_spectra)
     got = trade(back)
     local_grad = pl.pallas_call(

time: 107 us -> 106 us (level)
  transfers between devices with their start and end apart: 4 -> 4, of which waited for: 4 -> 4; matrix products, arithmetic and copies ran while one was open for 1% -> 1% of each run, Pallas kernels for 16% -> 17%
where the time goes in v6:
time: 106 us
  blocking collectives  48.3 us (46%)
  Pallas kernels  33.5 us (32%)
  waiting for transfers between devices  11.5 us (11%)
  starting transfers between devices  10.6 us (10%)
    all_to_all x2, blocking collectives, trade(): lax.all_to_all(values, ('gy', 'gx'), split_axis=0, concat_axis=0, tiled=T...  48.3 us
    pallas_call x2, Pallas kernels, across(): pl.pallas_call(body, out_shape=(held(sent), held(spectrum)), in_specs=[*[...  9.29 us
    all_to_all x2, starting transfers between devices, trade(): lax.all_to_all(values, ('gy', 'gx'), split_axis=0, concat_axis=0, tiled=T...  7.47 us
    all_to_all x2, waiting for transfers between devices, trade(): lax.all_to_all(values, ('gy', 'gx'), split_axis=0, concat_axis=0, tiled=T...  6.88 us
    pallas_call x1, Pallas kernels, on_tiles(): pl.pallas_call(local_kernel, out_shape=(held(cells), held(cells)), in_spe...  6.72 us
    pallas_call x1, Pallas kernels, on_tiles(): pl.pallas_call(grads_kernel, out_shape=held(cells), in_specs=[whole, scal...  5.42 us
    pallas_call x1, Pallas kernels, on_tiles(): pl.pallas_call(outer_kernel, out_shape=held(spectral_weight.shape), grid=...  5.32 us
    ppermute x2, waiting for transfers between devices, in_order(): other = lax.ppermute(own, 'dp', [(0, 1), (1, 0)])  4.62 us
  transfers between devices with their start and end apart: 4, of which 4 were waited for; matrix products, arithmetic and copies ran while one was open for 1% of the time, Pallas kernels for 17%

profile of v6, /device:TPU:0, one launch (start us, length us, event | category | flops | bytes accessed | tf_op | source)
XLA Modules:
  0.0 105.7 jit_solution(156946769315678759)
XLA Ops:
  0.6 2.2 %front.1 = (f32[256,640]{1,0:T(8,128)S(1)}, f32[2,20,4,8,256]{4,3,2,1,0:T(8,128)S(1)}) custom-call(f32[20,8,4,512]{3,2,1,0:T(4,128)} %bitcast.17, bf16[2,128,256]{2,1,0:T(8,128)(2,1)} %constant.16.clone.high_hbm.high_ref, bf16[2,128,256]{2,1,0:T(8,128)(2,1)} %constant.17.clone.low_hbm.low_ref, f32[2,20,20,8,256]{4,3,2,1,0:T(8,128)} %refs_1_.1), custom_call_target="tpu_custom_call" | custom-call | tf_op jit(solution)/shard_map/front/pallas_call | solution.py:642
  2.8 0.0 copy-start.4
  2.9 0.0 copy-start.5
  2.9 25.5 %all_to_all.45 = f32[16,16,640]{2,1,0:T(8,128)S(1)} all-to-all(f32[16,16,640]{2,1,0:T(8,128)S(1)} %bitcast.16), channel_id=1, replica_groups=mesh['dp'=2,'gx'=4,'gy'=4] {'gy','gx'}, dimensions={0} | all-to-all | bytes 1310720 | tf_op jit(solution)/shard_map/all_to_all | solution.py:615
  28.4 4.5 %mix_modes.1 = (f32[256,640]{1,0:T(8,128)}, f32[2,20,8,256]{3,2,1,0:T(8,128)}) custom-call(f32[2,20,4,8,256]{4,3,2,1,0:T(8,128)S(1)} %get-tuple-element.15.refs_0_, f32[256,640]{1,0:T(8,128)S(1)} %bitcast.11, f32[2,20,20,8,256]{4,3,2,1,0:T(8,128)} %refs_1_.1, bf16[2,256,256]{2,1,0:T(8,128)(2,1)S(1)} %copy-done.5, bf16[2,256,256]{2,1,0:T(8,128)(2,1)S(1)} %copy-done.4), custom_call_target="tpu_custom_call" | custom-call | tf_op jit(solution)/shard_map/mix_modes/pallas_call | solution.py:623
  32.9 0.0 copy-start.8
  32.9 0.0 copy-start.6
  32.9 0.0 copy-start.7
  32.9 3.7 %all-to-all-start.1 = ((f32[16,16,640]{2,1,0:T(8,128)}), f32[16,16,640]{2,1,0:T(8,128)S(1)}, u32[]{:S(2)}, u32[]{:S(2)}) async-start(f32[16,16,640]{2,1,0:T(8,128)} %bitcast.21), calls=%async_computation.1 | async-start | bytes 1310720 | tf_op jit(solution)/shard_map/all_to_all | solution.py:615
  36.7 1.6 %collective-permute-start = (f32[2,20,8,256]{3,2,1,0:T(8,128)S(1)}, f32[2,20,8,256]{3,2,1,0:T(8,128)S(1)}, u32[]{:S(2)}, u32[]{:S(2)}) collective-permute-start(f32[2,20,8,256]{3,2,1,0:T(8,128)S(1)} %copy-done.8), channel_id=1, source_target_pairs={{0,16},{16,0},{1,17},{17,1},{2,18},{18,2},{3,19},{19,3},{4,20},{20... | collective-permute-start | bytes 983048 | tf_op jit(solution)/shard_map/ppermute | solution.py:574
  38.3 6.7 %local_pre.1 = (f32[640,512]{1,0:T(8,128)}, f32[640,512]{1,0:T(8,128)}) custom-call(f32[20,8,4,512]{3,2,1,0:T(4,128)} %bitcast.18, f32[20,8,4,512]{3,2,1,0:T(4,128)} %bitcast.20, f32[20,20]{1,0:T(8,128)S(1)} %copy-done.6, f32[20]{0:T(128)S(1)} %copy-done.7), custom_call_target="tpu_custom_call" | custom-call | tf_op jit(solution)/shard_map/local_pre/pallas_call | solution.py:660
  45.0 1.7 %collective-permute-done = f32[2,20,8,256]{3,2,1,0:T(8,128)S(1)} collective-permute-done((f32[2,20,8,256]{3,2,1,0:T(8,128)S(1)}, f32[2,20,8,256]{3,2,1,0:T(8,128)S(1)}, u32[]{:S(2)}, u32[]{:S(2)}) %collective-permute-start) | collective-permute-done | bytes 327712 | tf_op jit(solution)/shard_map/ppermute | solution.py:574
  46.6 0.9 broadcast_select_fusion.2
  47.5 5.7 %all-to-all-done.1 = f32[16,16,640]{2,1,0:T(8,128)S(1)} async-done(((f32[16,16,640]{2,1,0:T(8,128)}), f32[16,16,640]{2,1,0:T(8,128)S(1)}, u32[]{:S(2)}, u32[]{:S(2)}) %all-to-all-start.1) | async-done | bytes 655392 | tf_op jit(solution)/shard_map/all_to_all | solution.py:615
  53.2 2.8 %middle.1 = (f32[256,640]{1,0:T(8,128)S(1)}, f32[640,512]{1,0:T(8,128)S(1)}) custom-call(f32[256,640]{1,0:T(8,128)S(1)} %bitcast.12, f32[640,512]{1,0:T(8,128)} %get-tuple-element.20.local_hbm, f32[640,512]{1,0:T(8,128)} %get-tuple-element.21.upstream_hbm, bf16[2,128,256]{2,1,0:T(8,128)(2,1)S(1)} %copy-done.3, bf16[2,128,256]{2,1,0:T(8,128)(2,1)S(1)} %copy-done.2), custom_call_target="tpu_custom_call" | custom-call | tf_op jit(solution)/shard_map/middle/pallas_call | solution.py:672
  56.1 22.8 %all_to_all.46 = f32[16,16,640]{2,1,0:T(8,128)S(1)} all-to-all(f32[16,16,640]{2,1,0:T(8,128)S(1)} %bitcast.15), channel_id=1, replica_groups=mesh['dp'=2,'gx'=4,'gy'=4] {'gy','gx'}, dimensions={0} | all-to-all | bytes 1310720 | tf_op jit(solution)/shard_map/all_to_all | solution.py:615
  78.8 4.8 %unmix_modes.1 = (f32[256,640]{1,0:T(8,128)}, f32[2,20,8,256]{3,2,1,0:T(8,128)}) custom-call(f32[256,640]{1,0:T(8,128)S(1)} %bitcast.14, f32[2,20,20,8,256]{4,3,2,1,0:T(8,128)} %refs_1_.1, bf16[2,256,256]{2,1,0:T(8,128)(2,1)S(1)} %copy-done.5, bf16[2,256,256]{2,1,0:T(8,128)(2,1)S(1)} %copy-done.4), custom_call_target="tpu_custom_call" | custom-call | tf_op jit(solution)/shard_map/unmix_modes/pallas_call | solution.py:623
  83.7 3.7 %all-to-all-start.3 = ((f32[16,16,640]{2,1,0:T(8,128)}), f32[16,16,640]{2,1,0:T(8,128)S(1)}, u32[]{:S(2)}, u32[]{:S(2)}) async-start(f32[16,16,640]{2,1,0:T(8,128)} %bitcast.22), calls=%async_computation.3 | async-start | bytes 1310720 | tf_op jit(solution)/shard_map/all_to_all | solution.py:615
  87.4 1.6 %collective-permute-start.1 = (f32[2,20,8,256]{3,2,1,0:T(8,128)S(1)}, f32[2,20,8,256]{3,2,1,0:T(8,128)S(1)}, u32[]{:S(2)}, u32[]{:S(2)}) collective-permute-start(f32[2,20,8,256]{3,2,1,0:T(8,128)S(1)} %copy-done.9), channel_id=1, source_target_pairs={{0,16},{16,0},{1,17},{17,1},{2,18},{18,2},{3,19},{19,3},{4,20},{20... | collective-permute-start | bytes 983048 | tf_op jit(solution)/shard_map/ppermute | solution.py:574
  89.0 5.4 %local_grad.1.local_ref = f32[640,512]{1,0:T(8,128)} custom-call(f32[640,512]{1,0:T(8,128)} %copy-done.1, f32[20,20]{1,0:T(8,128)S(1)} %copy-done.6), custom_call_target="tpu_custom_call" | custom-call | tf_op jit(solution)/shard_map/local_grad/pallas_call | solution.py:685
  94.4 3.0 %collective-permute-done.1 = f32[2,20,8,256]{3,2,1,0:T(8,128)S(1)} collective-permute-done((f32[2,20,8,256]{3,2,1,0:T(8,128)S(1)}, f32[2,20,8,256]{3,2,1,0:T(8,128)S(1)}, u32[]{:S(2)}, u32[]{:S(2)}) %collective-permute-start.1) | collective-permute-done | bytes 327712 | tf_op jit(solution)/shard_map/ppermute | solution.py:574
  97.4 5.3 %outer.1 = f32[2,20,20,8,256]{4,3,2,1,0:T(8,128)} custom-call(f32[2,20,8,256]{3,2,1,0:T(8,128)} %get-tuple-element.25.first_spectra, f32[2,20,8,256]{3,2,1,0:T(8,128)} %get-tuple-element.26.second_spectra, f32[2,20,8,256]{3,2,1,0:T(8,128)S(1)} %get-tuple-element.29.first_grads, f32[2,20,8,256]{3,2,1,0:T(8,128)S(1)} %get-tuple-element.28.second_grads), custom_call_target="tpu_custom_call" | custom-call | tf_op jit(solution)/shard_map/outer/pallas_call | solution.py:693
  102.8 1.2 %all-to-all-done.3 = f32[16,16,640]{2,1,0:T(8,128)S(1)} async-done(((f32[16,16,640]{2,1,0:T(8,128)}), f32[16,16,640]{2,1,0:T(8,128)S(1)}, u32[]{:S(2)}, u32[]{:S(2)}) %all-to-all-start.3) | async-done | bytes 655392 | tf_op jit(solution)/shard_map/all_to_all | solution.py:615
  104.0 1.7 %last.1 = f32[20,8,4,512]{3,2,1,0:T(4,128)} custom-call(f32[256,640]{1,0:T(8,128)S(1)} %bitcast.13, f32[640,512]{1,0:T(8,128)S(1)} %copy-done, bf16[2,128,256]{2,1,0:T(8,128)(2,1)S(1)} %copy-done.3, bf16[2,128,256]{2,1,0:T(8,128)(2,1)S(1)} %copy-done.2), custom_call_target="tpu_custom_call" | custom-call | tf_op jit(solution)/shard_map/last/pallas_call | solution.py:702
  (16 shorter events, 0.1 us)
Async XLA Ops:
  2.8 25.6 %copy-start.4 = (bf16[2,256,256]{2,1,0:T(8,128)(2,1)S(1)}, bf16[2,256,256]{2,1,0:T(8,128)(2,1)}, u32[]{:S(2)}) copy-start(bf16[2,256,256]{2,1,0:T(8,128)(2,1)} %constant.19.clone.refs_4_.refs_3_) | copy-start | bytes 786436
  2.9 25.5 %copy-start.5 = (bf16[2,256,256]{2,1,0:T(8,128)(2,1)S(1)}, bf16[2,256,256]{2,1,0:T(8,128)(2,1)}, u32[]{:S(2)}) copy-start(bf16[2,256,256]{2,1,0:T(8,128)(2,1)} %constant.18.clone.refs_3_.refs_2_) | copy-start | bytes 786436
  32.9 3.8 %copy-start.8 = (f32[2,20,8,256]{3,2,1,0:T(8,128)S(1)}, f32[2,20,8,256]{3,2,1,0:T(8,128)}, u32[]{:S(2)}) copy-start(f32[2,20,8,256]{3,2,1,0:T(8,128)} %get-tuple-element.18) | copy-start | bytes 983044
  32.9 5.4 %copy-start.6 = (f32[20,20]{1,0:T(8,128)S(1)}, f32[20,20]{1,0:T(8,128)}, u32[]{:S(2)}) copy-start(f32[20,20]{1,0:T(8,128)} %weight_ref.3) | copy-start | bytes 4804
  32.9 5.4 %copy-start.7 = (f32[20]{0:T(128)S(1)}, f32[20]{0:T(128)}, u32[]{:S(2)}) copy-start(f32[20]{0:T(128)} %bias_ref.1) | copy-start | bytes 244
  32.9 20.3 %all-to-all-start.1 = ((f32[16,16,640]{2,1,0:T(8,128)}), f32[16,16,640]{2,1,0:T(8,128)S(1)}, u32[]{:S(2)}, u32[]{:S(2)}) async-start(f32[16,16,640]{2,1,0:T(8,128)} %bitcast.21), calls=%async_computation.1 | async-start | bytes 1310720 | tf_op jit(solution)/shard_map/all_to_all | solution.py:615
  36.7 10.0 %collective-permute-start = (f32[2,20,8,256]{3,2,1,0:T(8,128)S(1)}, f32[2,20,8,256]{3,2,1,0:T(8,128)S(1)}, u32[]{:S(2)}, u32[]{:S(2)}) collective-permute-start(f32[2,20,8,256]{3,2,1,0:T(8,128)S(1)} %copy-done.8), channel_id=1, source_target_pairs={{0,16},{16,0},{1,17},{17,1},{2,18},{18,2},{3,19},{19,3},{4,20},{20... | collective-permute-start | bytes 983048 | tf_op jit(solution)/shard_map/ppermute | solution.py:574
  45.0 8.2 %copy-start.2 = (bf16[2,128,256]{2,1,0:T(8,128)(2,1)S(1)}, bf16[2,128,256]{2,1,0:T(8,128)(2,1)}, u32[]{:S(2)}) copy-start(bf16[2,128,256]{2,1,0:T(8,128)(2,1)} %constant.17.clone.low_hbm.low_ref) | copy-start | bytes 393220
  45.0 8.2 %copy-start.3 = (bf16[2,128,256]{2,1,0:T(8,128)(2,1)S(1)}, bf16[2,128,256]{2,1,0:T(8,128)(2,1)}, u32[]{:S(2)}) copy-start(bf16[2,128,256]{2,1,0:T(8,128)(2,1)} %constant.16.clone.high_hbm.high_ref) | copy-start | bytes 393220
  56.0 27.6 %copy-start.1 = (f32[640,512]{1,0:T(8,128)}, f32[640,512]{1,0:T(8,128)S(1)}, u32[]{:S(2)}) copy-start(f32[640,512]{1,0:T(8,128)S(1)} %get-tuple-element.24.rows_ref) | copy-start | bytes 3932164
  83.6 3.8 %copy-start.9 = (f32[2,20,8,256]{3,2,1,0:T(8,128)S(1)}, f32[2,20,8,256]{3,2,1,0:T(8,128)}, u32[]{:S(2)}) copy-start(f32[2,20,8,256]{3,2,1,0:T(8,128)} %get-tuple-element.27) | copy-start | bytes 983044
  83.7 20.3 %all-to-all-start.3 = ((f32[16,16,640]{2,1,0:T(8,128)}), f32[16,16,640]{2,1,0:T(8,128)S(1)}, u32[]{:S(2)}, u32[]{:S(2)}) async-start(f32[16,16,640]{2,1,0:T(8,128)} %bitcast.22), calls=%async_computation.3 | async-start | bytes 1310720 | tf_op jit(solution)/shard_map/all_to_all | solution.py:615
  87.4 10.0 %collective-permute-start.1 = (f32[2,20,8,256]{3,2,1,0:T(8,128)S(1)}, f32[2,20,8,256]{3,2,1,0:T(8,128)S(1)}, u32[]{:S(2)}, u32[]{:S(2)}) collective-permute-start(f32[2,20,8,256]{3,2,1,0:T(8,128)S(1)} %copy-done.9), channel_id=1, source_target_pairs={{0,16},{16,0},{1,17},{17,1},{2,18},{18,2},{3,19},{19,3},{4,20},{20... | collective-permute-start | bytes 983048 | tf_op jit(solution)/shard_map/ppermute | solution.py:574
  97.4 6.5 %copy-start = (f32[640,512]{1,0:T(8,128)S(1)}, f32[640,512]{1,0:T(8,128)}, u32[]{:S(2)}) copy-start(f32[640,512]{1,0:T(8,128)} %local_grad.1.local_ref) | copy-start | bytes 3932164

commit v7 on v6

--- a/solution.py
+++ b/solution.py
@@ -631,7 +631,7 @@
                 vmem(spectrum, f32),
                 vmem((2, 2 * channels * local_modes, owners * cells_x * cells_y // 2), f32),
                 vmem((2, channels * local_modes, modes), f32),
-                copies((5,)),
+                copies((5 if conjugate else 4,)),
                 copies,
                 copies((2,)),
             ],
@@ -641,7 +641,7 @@
 
     front, head = pl.pallas_call(
         front_kernel,
-        out_shape=(vmem(sent, f32), vmem((2, channels, channels // 5, local_modes, modes), f32)),
+        out_shape=(vmem(sent, f32), vmem((2, channels, channels // 4, local_modes, modes), f32)),
         in_specs=[stays] * 4,
         out_specs=(whole, whole),
         scratch_shapes=[

time: 106 us -> 106 us (level)
  no operation moved by 1% of the time
where the time goes in v7:
time: 106 us
  blocking collectives  48.3 us (46%)
  Pallas kernels  33.5 us (32%)
  waiting for transfers between devices  11.5 us (11%)
  starting transfers between devices  10.6 us (10%)
    all_to_all x2, blocking collectives, trade(): lax.all_to_all(values, ('gy', 'gx'), split_axis=0, concat_axis=0, tiled=T...  48.3 us
    pallas_call x2, Pallas kernels, across(): pl.pallas_call(body, out_shape=(held(sent), held(spectrum)), in_specs=[*[...  9.28 us
    all_to_all x2, starting transfers between devices, trade(): lax.all_to_all(values, ('gy', 'gx'), split_axis=0, concat_axis=0, tiled=T...  7.47 us
    all_to_all x2, waiting for transfers between devices, trade(): lax.all_to_all(values, ('gy', 'gx'), split_axis=0, concat_axis=0, tiled=T...  6.88 us
    pallas_call x1, Pallas kernels, on_tiles(): pl.pallas_call(local_kernel, out_shape=(held(cells), held(cells)), in_spe...  6.72 us
    pallas_call x1, Pallas kernels, on_tiles(): pl.pallas_call(grads_kernel, out_shape=held(cells), in_specs=[whole, scal...  5.42 us
    pallas_call x1, Pallas kernels, on_tiles(): pl.pallas_call(outer_kernel, out_shape=held(spectral_weight.shape), grid=...  5.32 us
    ppermute x2, waiting for transfers between devices, in_order(): other = lax.ppermute(own, 'dp', [(0, 1), (1, 0)])  4.61 us
  transfers between devices with their start and end apart: 4, of which 4 were waited for; matrix products, arithmetic and copies ran while one was open for 1% of the time, Pallas kernels for 17%

profile of v7, /device:TPU:0, one launch (start us, length us, event | category | flops | bytes accessed | tf_op | source)
XLA Modules:
  0.0 105.7 jit_solution(7349366934910778436)
XLA Ops:
  0.6 2.2 %front.1 = (f32[256,640]{1,0:T(8,128)S(1)}, f32[2,20,5,8,256]{4,3,2,1,0:T(8,128)S(1)}) custom-call(f32[20,8,4,512]{3,2,1,0:T(4,128)} %bitcast.17, bf16[2,128,256]{2,1,0:T(8,128)(2,1)} %constant.16.clone.high_hbm.high_ref, bf16[2,128,256]{2,1,0:T(8,128)(2,1)} %constant.17.clone.low_hbm.low_ref, f32[2,20,20,8,256]{4,3,2,1,0:T(8,128)} %refs_1_.1), custom_call_target="tpu_custom_call" | custom-call | tf_op jit(solution)/shard_map/front/pallas_call | solution.py:642
  2.8 0.0 copy-start.4
  2.9 0.0 copy-start.5
  2.9 25.5 %all_to_all.45 = f32[16,16,640]{2,1,0:T(8,128)S(1)} all-to-all(f32[16,16,640]{2,1,0:T(8,128)S(1)} %bitcast.16), channel_id=1, replica_groups=mesh['dp'=2,'gx'=4,'gy'=4] {'gy','gx'}, dimensions={0} | all-to-all | bytes 1310720 | tf_op jit(solution)/shard_map/all_to_all | solution.py:615
  28.4 4.5 %mix_modes.1 = (f32[256,640]{1,0:T(8,128)}, f32[2,20,8,256]{3,2,1,0:T(8,128)}) custom-call(f32[2,20,5,8,256]{4,3,2,1,0:T(8,128)S(1)} %get-tuple-element.15.refs_0_, f32[256,640]{1,0:T(8,128)S(1)} %bitcast.11, f32[2,20,20,8,256]{4,3,2,1,0:T(8,128)} %refs_1_.1, bf16[2,256,256]{2,1,0:T(8,128)(2,1)S(1)} %copy-done.5, bf16[2,256,256]{2,1,0:T(8,128)(2,1)S(1)} %copy-done.4), custom_call_target="tpu_custom_call" | custom-call | tf_op jit(solution)/shard_map/mix_modes/pallas_call | solution.py:623
  32.9 0.0 copy-start.8
  32.9 0.0 copy-start.6
  32.9 0.0 copy-start.7
  32.9 3.7 %all-to-all-start.1 = ((f32[16,16,640]{2,1,0:T(8,128)}), f32[16,16,640]{2,1,0:T(8,128)S(1)}, u32[]{:S(2)}, u32[]{:S(2)}) async-start(f32[16,16,640]{2,1,0:T(8,128)} %bitcast.21), calls=%async_computation.1 | async-start | bytes 1310720 | tf_op jit(solution)/shard_map/all_to_all | solution.py:615
  36.7 1.6 %collective-permute-start = (f32[2,20,8,256]{3,2,1,0:T(8,128)S(1)}, f32[2,20,8,256]{3,2,1,0:T(8,128)S(1)}, u32[]{:S(2)}, u32[]{:S(2)}) collective-permute-start(f32[2,20,8,256]{3,2,1,0:T(8,128)S(1)} %copy-done.8), channel_id=1, source_target_pairs={{0,16},{16,0},{1,17},{17,1},{2,18},{18,2},{3,19},{19,3},{4,20},{20... | collective-permute-start | bytes 983048 | tf_op jit(solution)/shard_map/ppermute | solution.py:574
  38.3 6.7 %local_pre.1 = (f32[640,512]{1,0:T(8,128)}, f32[640,512]{1,0:T(8,128)}) custom-call(f32[20,8,4,512]{3,2,1,0:T(4,128)} %bitcast.18, f32[20,8,4,512]{3,2,1,0:T(4,128)} %bitcast.20, f32[20,20]{1,0:T(8,128)S(1)} %copy-done.6, f32[20]{0:T(128)S(1)} %copy-done.7), custom_call_target="tpu_custom_call" | custom-call | tf_op jit(solution)/shard_map/local_pre/pallas_call | solution.py:660
  45.0 1.7 %collective-permute-done = f32[2,20,8,256]{3,2,1,0:T(8,128)S(1)} collective-permute-done((f32[2,20,8,256]{3,2,1,0:T(8,128)S(1)}, f32[2,20,8,256]{3,2,1,0:T(8,128)S(1)}, u32[]{:S(2)}, u32[]{:S(2)}) %collective-permute-start) | collective-permute-done | bytes 327712 | tf_op jit(solution)/shard_map/ppermute | solution.py:574
  46.6 0.9 broadcast_select_fusion.2
  47.5 5.7 %all-to-all-done.1 = f32[16,16,640]{2,1,0:T(8,128)S(1)} async-done(((f32[16,16,640]{2,1,0:T(8,128)}), f32[16,16,640]{2,1,0:T(8,128)S(1)}, u32[]{:S(2)}, u32[]{:S(2)}) %all-to-all-start.1) | async-done | bytes 655392 | tf_op jit(solution)/shard_map/all_to_all | solution.py:615
  53.2 2.8 %middle.1 = (f32[256,640]{1,0:T(8,128)S(1)}, f32[640,512]{1,0:T(8,128)S(1)}) custom-call(f32[256,640]{1,0:T(8,128)S(1)} %bitcast.12, f32[640,512]{1,0:T(8,128)} %get-tuple-element.20.local_hbm, f32[640,512]{1,0:T(8,128)} %get-tuple-element.21.upstream_hbm, bf16[2,128,256]{2,1,0:T(8,128)(2,1)S(1)} %copy-done.3, bf16[2,128,256]{2,1,0:T(8,128)(2,1)S(1)} %copy-done.2), custom_call_target="tpu_custom_call" | custom-call | tf_op jit(solution)/shard_map/middle/pallas_call | solution.py:672
  56.1 22.8 %all_to_all.46 = f32[16,16,640]{2,1,0:T(8,128)S(1)} all-to-all(f32[16,16,640]{2,1,0:T(8,128)S(1)} %bitcast.15), channel_id=1, replica_groups=mesh['dp'=2,'gx'=4,'gy'=4] {'gy','gx'}, dimensions={0} | all-to-all | bytes 1310720 | tf_op jit(solution)/shard_map/all_to_all | solution.py:615
  78.8 4.8 %unmix_modes.1 = (f32[256,640]{1,0:T(8,128)}, f32[2,20,8,256]{3,2,1,0:T(8,128)}) custom-call(f32[256,640]{1,0:T(8,128)S(1)} %bitcast.14, f32[2,20,20,8,256]{4,3,2,1,0:T(8,128)} %refs_1_.1, bf16[2,256,256]{2,1,0:T(8,128)(2,1)S(1)} %copy-done.5, bf16[2,256,256]{2,1,0:T(8,128)(2,1)S(1)} %copy-done.4), custom_call_target="tpu_custom_call" | custom-call | tf_op jit(solution)/shard_map/unmix_modes/pallas_call | solution.py:623
  83.7 3.7 %all-to-all-start.3 = ((f32[16,16,640]{2,1,0:T(8,128)}), f32[16,16,640]{2,1,0:T(8,128)S(1)}, u32[]{:S(2)}, u32[]{:S(2)}) async-start(f32[16,16,640]{2,1,0:T(8,128)} %bitcast.22), calls=%async_computation.3 | async-start | bytes 1310720 | tf_op jit(solution)/shard_map/all_to_all | solution.py:615
  87.4 1.6 %collective-permute-start.1 = (f32[2,20,8,256]{3,2,1,0:T(8,128)S(1)}, f32[2,20,8,256]{3,2,1,0:T(8,128)S(1)}, u32[]{:S(2)}, u32[]{:S(2)}) collective-permute-start(f32[2,20,8,256]{3,2,1,0:T(8,128)S(1)} %copy-done.9), channel_id=1, source_target_pairs={{0,16},{16,0},{1,17},{17,1},{2,18},{18,2},{3,19},{19,3},{4,20},{20... | collective-permute-start | bytes 983048 | tf_op jit(solution)/shard_map/ppermute | solution.py:574
  89.0 5.4 %local_grad.1.local_ref = f32[640,512]{1,0:T(8,128)} custom-call(f32[640,512]{1,0:T(8,128)} %copy-done.1, f32[20,20]{1,0:T(8,128)S(1)} %copy-done.6), custom_call_target="tpu_custom_call" | custom-call | tf_op jit(solution)/shard_map/local_grad/pallas_call | solution.py:685
  94.4 3.0 %collective-permute-done.1 = f32[2,20,8,256]{3,2,1,0:T(8,128)S(1)} collective-permute-done((f32[2,20,8,256]{3,2,1,0:T(8,128)S(1)}, f32[2,20,8,256]{3,2,1,0:T(8,128)S(1)}, u32[]{:S(2)}, u32[]{:S(2)}) %collective-permute-start.1) | collective-permute-done | bytes 327712 | tf_op jit(solution)/shard_map/ppermute | solution.py:574
  97.4 5.3 %outer.1 = f32[2,20,20,8,256]{4,3,2,1,0:T(8,128)} custom-call(f32[2,20,8,256]{3,2,1,0:T(8,128)} %get-tuple-element.25.first_spectra, f32[2,20,8,256]{3,2,1,0:T(8,128)} %get-tuple-element.26.second_spectra, f32[2,20,8,256]{3,2,1,0:T(8,128)S(1)} %get-tuple-element.29.first_grads, f32[2,20,8,256]{3,2,1,0:T(8,128)S(1)} %get-tuple-element.28.second_grads), custom_call_target="tpu_custom_call" | custom-call | tf_op jit(solution)/shard_map/outer/pallas_call | solution.py:693
  102.8 1.2 %all-to-all-done.3 = f32[16,16,640]{2,1,0:T(8,128)S(1)} async-done(((f32[16,16,640]{2,1,0:T(8,128)}), f32[16,16,640]{2,1,0:T(8,128)S(1)}, u32[]{:S(2)}, u32[]{:S(2)}) %all-to-all-start.3) | async-done | bytes 655392 | tf_op jit(solution)/shard_map/all_to_all | solution.py:615
  104.0 1.7 %last.1 = f32[20,8,4,512]{3,2,1,0:T(4,128)} custom-call(f32[256,640]{1,0:T(8,128)S(1)} %bitcast.13, f32[640,512]{1,0:T(8,128)S(1)} %copy-done, bf16[2,128,256]{2,1,0:T(8,128)(2,1)S(1)} %copy-done.3, bf16[2,128,256]{2,1,0:T(8,128)(2,1)S(1)} %copy-done.2), custom_call_target="tpu_custom_call" | custom-call | tf_op jit(solution)/shard_map/last/pallas_call | solution.py:702
  (16 shorter events, 0.1 us)
Async XLA Ops:
  2.8 25.6 %copy-start.4 = (bf16[2,256,256]{2,1,0:T(8,128)(2,1)S(1)}, bf16[2,256,256]{2,1,0:T(8,128)(2,1)}, u32[]{:S(2)}) copy-start(bf16[2,256,256]{2,1,0:T(8,128)(2,1)} %constant.19.clone.refs_4_.refs_3_) | copy-start | bytes 786436
  2.9 25.5 %copy-start.5 = (bf16[2,256,256]{2,1,0:T(8,128)(2,1)S(1)}, bf16[2,256,256]{2,1,0:T(8,128)(2,1)}, u32[]{:S(2)}) copy-start(bf16[2,256,256]{2,1,0:T(8,128)(2,1)} %constant.18.clone.refs_3_.refs_2_) | copy-start | bytes 786436
  32.9 3.8 %copy-start.8 = (f32[2,20,8,256]{3,2,1,0:T(8,128)S(1)}, f32[2,20,8,256]{3,2,1,0:T(8,128)}, u32[]{:S(2)}) copy-start(f32[2,20,8,256]{3,2,1,0:T(8,128)} %get-tuple-element.18) | copy-start | bytes 983044
  32.9 5.4 %copy-start.6 = (f32[20,20]{1,0:T(8,128)S(1)}, f32[20,20]{1,0:T(8,128)}, u32[]{:S(2)}) copy-start(f32[20,20]{1,0:T(8,128)} %weight_ref.3) | copy-start | bytes 4804
  32.9 5.4 %copy-start.7 = (f32[20]{0:T(128)S(1)}, f32[20]{0:T(128)}, u32[]{:S(2)}) copy-start(f32[20]{0:T(128)} %bias_ref.1) | copy-start | bytes 244
  32.9 20.3 %all-to-all-start.1 = ((f32[16,16,640]{2,1,0:T(8,128)}), f32[16,16,640]{2,1,0:T(8,128)S(1)}, u32[]{:S(2)}, u32[]{:S(2)}) async-start(f32[16,16,640]{2,1,0:T(8,128)} %bitcast.21), calls=%async_computation.1 | async-start | bytes 1310720 | tf_op jit(solution)/shard_map/all_to_all | solution.py:615
  36.7 10.0 %collective-permute-start = (f32[2,20,8,256]{3,2,1,0:T(8,128)S(1)}, f32[2,20,8,256]{3,2,1,0:T(8,128)S(1)}, u32[]{:S(2)}, u32[]{:S(2)}) collective-permute-start(f32[2,20,8,256]{3,2,1,0:T(8,128)S(1)} %copy-done.8), channel_id=1, source_target_pairs={{0,16},{16,0},{1,17},{17,1},{2,18},{18,2},{3,19},{19,3},{4,20},{20... | collective-permute-start | bytes 983048 | tf_op jit(solution)/shard_map/ppermute | solution.py:574
  45.0 8.2 %copy-start.2 = (bf16[2,128,256]{2,1,0:T(8,128)(2,1)S(1)}, bf16[2,128,256]{2,1,0:T(8,128)(2,1)}, u32[]{:S(2)}) copy-start(bf16[2,128,256]{2,1,0:T(8,128)(2,1)} %constant.17.clone.low_hbm.low_ref) | copy-start | bytes 393220
  45.0 8.2 %copy-start.3 = (bf16[2,128,256]{2,1,0:T(8,128)(2,1)S(1)}, bf16[2,128,256]{2,1,0:T(8,128)(2,1)}, u32[]{:S(2)}) copy-start(bf16[2,128,256]{2,1,0:T(8,128)(2,1)} %constant.16.clone.high_hbm.high_ref) | copy-start | bytes 393220
  56.0 27.6 %copy-start.1 = (f32[640,512]{1,0:T(8,128)}, f32[640,512]{1,0:T(8,128)S(1)}, u32[]{:S(2)}) copy-start(f32[640,512]{1,0:T(8,128)S(1)} %get-tuple-element.24.rows_ref) | copy-start | bytes 3932164
  83.6 3.8 %copy-start.9 = (f32[2,20,8,256]{3,2,1,0:T(8,128)S(1)}, f32[2,20,8,256]{3,2,1,0:T(8,128)}, u32[]{:S(2)}) copy-start(f32[2,20,8,256]{3,2,1,0:T(8,128)} %get-tuple-element.27) | copy-start | bytes 983044
  83.7 20.3 %all-to-all-start.3 = ((f32[16,16,640]{2,1,0:T(8,128)}), f32[16,16,640]{2,1,0:T(8,128)S(1)}, u32[]{:S(2)}, u32[]{:S(2)}) async-start(f32[16,16,640]{2,1,0:T(8,128)} %bitcast.22), calls=%async_computation.3 | async-start | bytes 1310720 | tf_op jit(solution)/shard_map/all_to_all | solution.py:615
  87.4 10.0 %collective-permute-start.1 = (f32[2,20,8,256]{3,2,1,0:T(8,128)S(1)}, f32[2,20,8,256]{3,2,1,0:T(8,128)S(1)}, u32[]{:S(2)}, u32[]{:S(2)}) collective-permute-start(f32[2,20,8,256]{3,2,1,0:T(8,128)S(1)} %copy-done.9), channel_id=1, source_target_pairs={{0,16},{16,0},{1,17},{17,1},{2,18},{18,2},{3,19},{19,3},{4,20},{20... | collective-permute-start | bytes 983048 | tf_op jit(solution)/shard_map/ppermute | solution.py:574
  97.4 6.5 %copy-start = (f32[640,512]{1,0:T(8,128)S(1)}, f32[640,512]{1,0:T(8,128)}, u32[]{:S(2)}) copy-start(f32[640,512]{1,0:T(8,128)} %local_grad.1.local_ref) | copy-start | bytes 3932164
